TPU v7x, 256 devices: a whole 4x4x8 slice. The times are simulated.
256 devices in a mesh: mpo: 8 (over y, core), blk: 32 (over x, z).
Axes of the slice: x: 4, y: 4, z: 8, core: 2. Of those that a mesh axis runs over, the one named last changes fastest.
Arguments:
- two_site: bfloat16 [256, 16, 128, 128], P('blk'), may hold values from -6 to 6
- left_env: bfloat16 [34, 256, 128, 128], P(None, 'blk'), may hold values from -0.5 to 0.5
- right_env: bfloat16 [34, 256, 128, 128], P(None, 'blk'), may hold values from -0.5 to 0.5
- mpo_terms: bfloat16 [64, 16, 16], P('mpo'), may hold values from -0.1875 to 0.1875
- term_left: int32 [64], P('mpo'), may hold values from 0 to 33
- term_right: int32 [64], P('mpo'), may hold values from 0 to 33
- shifts: int32 [16], replicated, may hold values from -1 to 1, as said below
- block_sizes: int32 [256], replicated, may hold values from 64 to 128, as said below
Outputs:
- applied: bfloat16 [256, 16, 128, 128], P('blk', 'mpo')
Inputs may be any that keep to these rules, and one draw needn't show every extreme that they name: `shifts`: both -1 and 1 occur among the offsets. `block_sizes`: both 128 // 2 and 128 occur among the live dimensions.
All inputs are finite; a program needn't handle non-finite values.
Results may differ from a plain program's by a relative error of at most 0.0057.
Values may be sent and summed in bfloat16 or wider, within the bound.
A program may use at most 128 MiB of HBM per device.

v0:
```python
import jax
import jax.numpy as jnp
from jax import lax
from jax.sharding import PartitionSpec as P

SH = 1


def with_halo(cells, sides, width):
    for axis, dim in sides:
        count = lax.axis_size(axis)
        ends = count - 1
        head = lax.slice_in_dim(cells, 0, width, axis=dim)
        tail = lax.slice_in_dim(cells, cells.shape[dim] - width, cells.shape[dim], axis=dim)
        cells = jnp.concatenate(
            [
                lax.ppermute(tail, axis, [(i, (i + 1) % count) for i in range(ends)]),
                cells,
                lax.ppermute(head, axis, [((i + 1) % count, i) for i in range(ends)]),
            ],
            axis=dim,
        )
    return cells


def sector_mask(block_sizes, shifts, first, blocks, total, depth):
    rows_left = first + jnp.arange(blocks, dtype=jnp.int32)
    right_index = rows_left[:, None] + shifts[None, :]
    inside = (right_index >= 0) & (right_index < total)
    table = jnp.arange(total, dtype=jnp.int32)
    size_left = jnp.sum(
        jnp.where(rows_left[:, None] == table[None, :], block_sizes[None, :], 0), axis=1
    )
    size_right = jnp.sum(
        jnp.where(right_index[:, :, None] == table[None, None, :], block_sizes[None, None, :], 0),
        axis=2,
    )
    lines = jnp.arange(depth, dtype=jnp.int32)
    keep_rows = lines[None, None, :, None] < size_left[:, None, None, None]
    keep_cols = lines[None, None, None, :] < size_right[:, :, None, None]
    return keep_rows & keep_cols & inside[:, :, None, None]


def body(two_site, left_env, right_env, mpo_terms, term_left, term_right, shifts, block_sizes):
    blocks = two_site.shape[0]
    depth = two_site.shape[2]
    total = blocks * lax.axis_size("blk")
    first = lax.axis_index("blk") * blocks
    mask = sector_mask(block_sizes, shifts, first, blocks, total, depth)
    clean = jnp.where(mask, two_site, jnp.zeros_like(two_site))
    padded = with_halo(right_env, (("blk", 1),), SH)
    starts = shifts + SH

    def one_term(summed, item):
        left_index, right_index, matrix = item
        left_block = lax.dynamic_index_in_dim(left_env, left_index, 0, keepdims=False)
        applied_left = jnp.einsum(
            "bxy,bqyz->bqxz", left_block, clean, preferred_element_type=jnp.float32
        ).astype(jnp.bfloat16)
        mixed = jnp.einsum(
            "pq,bqxz->bpxz", matrix, applied_left, preferred_element_type=jnp.float32
        )
        mixed_half = mixed.astype(jnp.bfloat16)
        right_rows = lax.dynamic_index_in_dim(padded, right_index, 0, keepdims=False)
        gathered = jax.vmap(lambda begin: lax.dynamic_slice_in_dim(right_rows, begin, blocks, 0))(
            starts
        )
        product = jnp.einsum(
            "bpxz,pbzy->bpxy", mixed_half, gathered, preferred_element_type=jnp.float32
        )
        return (summed + product, None)

    summed, unused = lax.scan(
        one_term, jnp.zeros(two_site.shape, jnp.float32), (term_left, term_right, mpo_terms)
    )
    masked = jnp.where(mask, summed, jnp.float32(0.0))
    return lax.psum_scatter(masked, "mpo", scatter_dimension=1, tiled=True).astype(jnp.bfloat16)


def solution(mesh):
    return jax.shard_map(
        body,
        mesh=mesh,
        in_specs=(
            P("blk", None, None, None),
            P(None, "blk", None, None),
            P(None, "blk", None, None),
            P("mpo", None, None),
            P("mpo"),
            P("mpo"),
            P(),
            P(),
        ),
        out_specs=P("blk", "mpo", None, None),
        check_vma=False,
    )
```

profile of v0, /device:TPU:7, one launch (start us, length us, event | category | flops | bytes accessed | tf_op | source)
XLA Modules:
  0.0 375.0 jit_solution(1623430495436177643)
XLA Ops:
  0.0 1.8 fusion.22
  1.8 3.5 collective-permute-start
  5.3 6.1 %collective-permute-start.1 = (bf16[34,1,128,128]{3,2,1,0:T(8,128)(2,1)S(1)}, bf16[34,1,128,128]{3,2,1,0:T(8,128)(2,1)}, u32[]{:S(2)}, u32[]{:S(2)}) collective-permute-start(bf16[34,1,128,128]{3,2,1,0:T(8,128)(2,1)S(1)} %get-tuple-element.102), channel_id=1, source_target_pairs={{1,0},{2,1},{3,2},{4,3},{5,4},{6,5},{7,6},{8,7},{9,8},{10,9},{11,1... | collective-permute-start | bytes 3342344 | tf_op jit(solution)/shard_map/ppermute | solution.py:19
  13.6 5.1 %fusion.21 = bf16[8,16,128,128]{3,2,1,0:T(8,128)(2,1)} fusion(bf16[8,16,128,128]{3,2,1,0:T(8,128)(2,1)} %param.10, pred[8,16]{1,0:T(8,128)(4,1)S(1)} %compare_and_fusion, pred[8,16,128]{2,1,0:T(8,128)(4,1)S(1)} %iota_compare_fusion.1, pred[8,128]{1,0:T(8,128)(4,1)S(1)} %iota_compare_fusion.3), kind=kLoop, calls=%fused_computation.23 | loop fusion | flops 6291456 | bytes 8406144 | tf_op jit(solution)/shard_map/jit(_where)/select_n | solution.py:50
  18.7 15.1 %collective-permute-done = bf16[34,1,128,128]{3,2,1,0:T(8,128)(2,1)S(1)} collective-permute-done((bf16[34,1,128,128]{3,2,1,0:T(8,128)(2,1)S(1)}, bf16[34,1,128,128]{3,2,1,0:T(8,128)(2,1)S(1)}, u32[]{:S(2)}, u32[]{:S(2)}) %collective-permute-start) | collective-permute-done | bytes 1114144 | tf_op jit(solution)/shard_map/ppermute | solution.py:17
  34.7 10.1 %pad_maximum_fusion = bf16[34,10,128,128]{3,2,1,0:T(8,128)(2,1)} fusion(bf16[34,1,128,128]{3,2,1,0:T(8,128)(2,1)} %collective-permute-done.1, bf16[34,8,128,128]{3,2,1,0:T(8,128)(2,1)} %param.12, bf16[34,1,128,128]{3,2,1,0:T(8,128)(2,1)S(1)} %collective-permute-done), kind=kLoop, calls=%fused_computation.20 | loop fusion | flops 11141120 | bytes 22282240 | tf_op jit(solution)/shard_map/concatenate | solution.py:15
  44.8 229.9 %while.11 = (s32[]{:T(128)}, f32[8,16,128,128]{3,2,1,0:T(8,128)}, s32[8]{0:T(128)S(1)}, bf16[34,8,128,128]{3,2,1,0:T(8,128)(2,1)}, bf16[8,16,128,128]{3,2,1,0:T(...) while((s32[]{:T(128)}, f32[8,16,128,128]{3,2,1,0:T(8,128)}, ...), condition=%wide.region_3.4_spmd.clone, body=%wide.region_2.3_spmd.clone.sunk | while | flops 1149239296 | bytes 51254304 | solution.py:73
  47.3 3.5 convert_bitcast_fusion.4
  50.8 5.5 %convert_bitcast_fusion.5 = bf16[8,16,128,128]{3,1,2,0:T(8,128)(2,1)} fusion(bf16[8,16,128,128]{3,2,1,0:T(8,128)(2,1)S(1)} %convert_bitcast_fusion.4, bf16[8,16,16]{2,1,0:T(8,128)(2,1)} %get-tuple-element.187, s32[]{:T(128)} %get-tuple-element.170), kind=kOutput, calls=%fused_computation.7.clone.1 | convolution fusion | flops 69206016 | bytes 8393216 | tf_op jit(solution)/shard_map/while/body/eval_jaxpr/pq,bqxz->bpxz/dot_general | solution.py:60
  58.8 1.0 dynamic-slice_bitcast_fusion.2
  59.9 3.2 gather_fusion
  63.0 8.4 %select_add_fusion.2 = f32[8,16,128,128]{3,2,1,0:T(8,128)} fusion(f32[8,16,128,128]{3,2,1,0:T(8,128)} %get-tuple-element.171, pred[]{:T(512)S(6)} %compare.4, bf16[16,8,128,128]{3,2,1,0:T(8,128)(2,1)} %gather_fusion, bf16[8,16,128,128]{3,1,2,0:T(8,128)(2,1)} %convert_bitcast_fusion.5), kind=kOutput, calls=%fused_computation.1.clone.1 | convolution fusion | flops 541065216 | bytes 25165824 | tf_op jit(solution)/shard_map/while/body/eval_jaxpr/bpxz,pbzy->bpxy/dot_general | solution.py:68
  74.0 3.5 convert_bitcast_fusion.4
  77.5 5.5 %convert_bitcast_fusion.5 = bf16[8,16,128,128]{3,1,2,0:T(8,128)(2,1)} fusion(bf16[8,16,128,128]{3,2,1,0:T(8,128)(2,1)S(1)} %convert_bitcast_fusion.4, bf16[8,16,16]{2,1,0:T(8,128)(2,1)} %get-tuple-element.187, s32[]{:T(128)} %get-tuple-element.170), kind=kOutput, calls=%fused_computation.7.clone.1 | convolution fusion | flops 69206016 | bytes 8393216 | tf_op jit(solution)/shard_map/while/body/eval_jaxpr/pq,bqxz->bpxz/dot_general | solution.py:60
  85.5 1.0 dynamic-slice_bitcast_fusion.2
  86.5 3.2 gather_fusion
  89.7 10.8 %select_add_fusion.2 = f32[8,16,128,128]{3,2,1,0:T(8,128)} fusion(f32[8,16,128,128]{3,2,1,0:T(8,128)} %get-tuple-element.171, pred[]{:T(512)S(6)} %compare.4, bf16[16,8,128,128]{3,2,1,0:T(8,128)(2,1)} %gather_fusion, bf16[8,16,128,128]{3,1,2,0:T(8,128)(2,1)} %convert_bitcast_fusion.5), kind=kOutput, calls=%fused_computation.1.clone.1 | convolution fusion | flops 541065216 | bytes 25165824 | tf_op jit(solution)/shard_map/while/body/eval_jaxpr/bpxz,pbzy->bpxy/dot_general | solution.py:68
  103.0 3.5 convert_bitcast_fusion.4
  106.5 5.5 %convert_bitcast_fusion.5 = bf16[8,16,128,128]{3,1,2,0:T(8,128)(2,1)} fusion(bf16[8,16,128,128]{3,2,1,0:T(8,128)(2,1)S(1)} %convert_bitcast_fusion.4, bf16[8,16,16]{2,1,0:T(8,128)(2,1)} %get-tuple-element.187, s32[]{:T(128)} %get-tuple-element.170), kind=kOutput, calls=%fused_computation.7.clone.1 | convolution fusion | flops 69206016 | bytes 8393216 | tf_op jit(solution)/shard_map/while/body/eval_jaxpr/pq,bqxz->bpxz/dot_general | solution.py:60
  114.5 1.0 dynamic-slice_bitcast_fusion.2
  115.5 3.2 gather_fusion
  118.7 10.8 %select_add_fusion.2 = f32[8,16,128,128]{3,2,1,0:T(8,128)} fusion(f32[8,16,128,128]{3,2,1,0:T(8,128)} %get-tuple-element.171, pred[]{:T(512)S(6)} %compare.4, bf16[16,8,128,128]{3,2,1,0:T(8,128)(2,1)} %gather_fusion, bf16[8,16,128,128]{3,1,2,0:T(8,128)(2,1)} %convert_bitcast_fusion.5), kind=kOutput, calls=%fused_computation.1.clone.1 | convolution fusion | flops 541065216 | bytes 25165824 | tf_op jit(solution)/shard_map/while/body/eval_jaxpr/bpxz,pbzy->bpxy/dot_general | solution.py:68
  132.0 3.5 convert_bitcast_fusion.4
  135.6 5.5 %convert_bitcast_fusion.5 = bf16[8,16,128,128]{3,1,2,0:T(8,128)(2,1)} fusion(bf16[8,16,128,128]{3,2,1,0:T(8,128)(2,1)S(1)} %convert_bitcast_fusion.4, bf16[8,16,16]{2,1,0:T(8,128)(2,1)} %get-tuple-element.187, s32[]{:T(128)} %get-tuple-element.170), kind=kOutput, calls=%fused_computation.7.clone.1 | convolution fusion | flops 69206016 | bytes 8393216 | tf_op jit(solution)/shard_map/while/body/eval_jaxpr/pq,bqxz->bpxz/dot_general | solution.py:60
  143.6 1.0 dynamic-slice_bitcast_fusion.2
  144.6 3.2 gather_fusion
  147.7 10.8 %select_add_fusion.2 = f32[8,16,128,128]{3,2,1,0:T(8,128)} fusion(f32[8,16,128,128]{3,2,1,0:T(8,128)} %get-tuple-element.171, pred[]{:T(512)S(6)} %compare.4, bf16[16,8,128,128]{3,2,1,0:T(8,128)(2,1)} %gather_fusion, bf16[8,16,128,128]{3,1,2,0:T(8,128)(2,1)} %convert_bitcast_fusion.5), kind=kOutput, calls=%fused_computation.1.clone.1 | convolution fusion | flops 541065216 | bytes 25165824 | tf_op jit(solution)/shard_map/while/body/eval_jaxpr/bpxz,pbzy->bpxy/dot_general | solution.py:68
  161.1 3.5 convert_bitcast_fusion.4
  164.6 5.5 %convert_bitcast_fusion.5 = bf16[8,16,128,128]{3,1,2,0:T(8,128)(2,1)} fusion(bf16[8,16,128,128]{3,2,1,0:T(8,128)(2,1)S(1)} %convert_bitcast_fusion.4, bf16[8,16,16]{2,1,0:T(8,128)(2,1)} %get-tuple-element.187, s32[]{:T(128)} %get-tuple-element.170), kind=kOutput, calls=%fused_computation.7.clone.1 | convolution fusion | flops 69206016 | bytes 8393216 | tf_op jit(solution)/shard_map/while/body/eval_jaxpr/pq,bqxz->bpxz/dot_general | solution.py:60
  173.6 3.2 gather_fusion
  176.8 10.8 %select_add_fusion.2 = f32[8,16,128,128]{3,2,1,0:T(8,128)} fusion(f32[8,16,128,128]{3,2,1,0:T(8,128)} %get-tuple-element.171, pred[]{:T(512)S(6)} %compare.4, bf16[16,8,128,128]{3,2,1,0:T(8,128)(2,1)} %gather_fusion, bf16[8,16,128,128]{3,1,2,0:T(8,128)(2,1)} %convert_bitcast_fusion.5), kind=kOutput, calls=%fused_computation.1.clone.1 | convolution fusion | flops 541065216 | bytes 25165824 | tf_op jit(solution)/shard_map/while/body/eval_jaxpr/bpxz,pbzy->bpxy/dot_general | solution.py:68
  190.1 3.5 convert_bitcast_fusion.4
  193.6 5.5 %convert_bitcast_fusion.5 = bf16[8,16,128,128]{3,1,2,0:T(8,128)(2,1)} fusion(bf16[8,16,128,128]{3,2,1,0:T(8,128)(2,1)S(1)} %convert_bitcast_fusion.4, bf16[8,16,16]{2,1,0:T(8,128)(2,1)} %get-tuple-element.187, s32[]{:T(128)} %get-tuple-element.170), kind=kOutput, calls=%fused_computation.7.clone.1 | convolution fusion | flops 69206016 | bytes 8393216 | tf_op jit(solution)/shard_map/while/body/eval_jaxpr/pq,bqxz->bpxz/dot_general | solution.py:60
  201.6 1.0 dynamic-slice_bitcast_fusion.2
  202.6 3.2 gather_fusion
  205.8 10.8 %select_add_fusion.2 = f32[8,16,128,128]{3,2,1,0:T(8,128)} fusion(f32[8,16,128,128]{3,2,1,0:T(8,128)} %get-tuple-element.171, pred[]{:T(512)S(6)} %compare.4, bf16[16,8,128,128]{3,2,1,0:T(8,128)(2,1)} %gather_fusion, bf16[8,16,128,128]{3,1,2,0:T(8,128)(2,1)} %convert_bitcast_fusion.5), kind=kOutput, calls=%fused_computation.1.clone.1 | convolution fusion | flops 541065216 | bytes 25165824 | tf_op jit(solution)/shard_map/while/body/eval_jaxpr/bpxz,pbzy->bpxy/dot_general | solution.py:68
  219.1 3.5 convert_bitcast_fusion.4
  222.7 5.5 %convert_bitcast_fusion.5 = bf16[8,16,128,128]{3,1,2,0:T(8,128)(2,1)} fusion(bf16[8,16,128,128]{3,2,1,0:T(8,128)(2,1)S(1)} %convert_bitcast_fusion.4, bf16[8,16,16]{2,1,0:T(8,128)(2,1)} %get-tuple-element.187, s32[]{:T(128)} %get-tuple-element.170), kind=kOutput, calls=%fused_computation.7.clone.1 | convolution fusion | flops 69206016 | bytes 8393216 | tf_op jit(solution)/shard_map/while/body/eval_jaxpr/pq,bqxz->bpxz/dot_general | solution.py:60
  231.7 3.2 gather_fusion
  234.8 10.8 %select_add_fusion.2 = f32[8,16,128,128]{3,2,1,0:T(8,128)} fusion(f32[8,16,128,128]{3,2,1,0:T(8,128)} %get-tuple-element.171, pred[]{:T(512)S(6)} %compare.4, bf16[16,8,128,128]{3,2,1,0:T(8,128)(2,1)} %gather_fusion, bf16[8,16,128,128]{3,1,2,0:T(8,128)(2,1)} %convert_bitcast_fusion.5), kind=kOutput, calls=%fused_computation.1.clone.1 | convolution fusion | flops 541065216 | bytes 25165824 | tf_op jit(solution)/shard_map/while/body/eval_jaxpr/bpxz,pbzy->bpxy/dot_general | solution.py:68
  248.2 3.5 convert_bitcast_fusion.4
  251.7 5.5 %convert_bitcast_fusion.5 = bf16[8,16,128,128]{3,1,2,0:T(8,128)(2,1)} fusion(bf16[8,16,128,128]{3,2,1,0:T(8,128)(2,1)S(1)} %convert_bitcast_fusion.4, bf16[8,16,16]{2,1,0:T(8,128)(2,1)} %get-tuple-element.187, s32[]{:T(128)} %get-tuple-element.170), kind=kOutput, calls=%fused_computation.7.clone.1 | convolution fusion | flops 69206016 | bytes 8393216 | tf_op jit(solution)/shard_map/while/body/eval_jaxpr/pq,bqxz->bpxz/dot_general | solution.py:60
  259.7 1.0 dynamic-slice_bitcast_fusion.2
  260.7 3.2 gather_fusion
  263.9 10.8 %select_add_fusion.2 = f32[8,16,128,128]{3,2,1,0:T(8,128)} fusion(f32[8,16,128,128]{3,2,1,0:T(8,128)} %get-tuple-element.171, pred[]{:T(512)S(6)} %compare.4, bf16[16,8,128,128]{3,2,1,0:T(8,128)(2,1)} %gather_fusion, bf16[8,16,128,128]{3,1,2,0:T(8,128)(2,1)} %convert_bitcast_fusion.5), kind=kOutput, calls=%fused_computation.1.clone.1 | convolution fusion | flops 541065216 | bytes 25165824 | tf_op jit(solution)/shard_map/while/body/eval_jaxpr/bpxz,pbzy->bpxy/dot_general | solution.py:68
  274.7 6.5 %fusion.20 = f32[8,16,128,128]{3,2,1,0:T(8,128)} fusion(f32[8,16,128,128]{3,2,1,0:T(8,128)} %get-tuple-element.52, pred[8,16]{1,0:T(8,128)(4,1)S(1)} %compare_and_fusion, pred[8,16,128]{2,1,0:T(8,128)(4,1)S(1)} %iota_compare_fusion.1, pred[8,128]{1,0:T(8,128)(4,1)S(1)} %iota_compare_fusion.3), kind=kLoop, calls=%fused_computation.22 | loop fusion | flops 6291456 | bytes 16794752 | tf_op jit(solution)/shard_map/jit(_where)/select_n | solution.py:76
  281.2 92.0 %all-reduce.3 = bf16[8,16,128,128]{3,2,1,0:T(8,128)(2,1)} all-reduce(f32[8,16,128,128]{3,2,1,0:T(8,128)} %fusion.20), channel_id=2, replica_groups=mesh['mpo'=8,'blk'=32] {'mpo'}, use_global_device_ids=true, to_apply=%region_4.5.clone | all-reduce | flops 2097152 | bytes 12582912
  373.1 1.9 dynamic-slice_convert_fusion
  (47 shorter events, 14.1 us)
Async XLA Ops:
  0.0 11.8 %copy-start.4 = (u32[256]{0:T(256)S(1)}, u32[256]{0:T(256)}, u32[]{:S(2)}) copy-start(u32[256]{0:T(256)} %constant.75) | copy-start | bytes 3076
  0.0 11.5 %copy-start.1 = (s32[16]{0:T(128)S(1)}, s32[16]{0:T(128)}, u32[]{:S(2)}) copy-start(s32[16]{0:T(128)} %param.16) | copy-start | bytes 196
  0.0 11.6 %copy-start = (s32[256]{0:T(256)S(1)}, s32[256]{0:T(256)}, u32[]{:S(2)}) copy-start(s32[256]{0:T(256)} %param.17) | copy-start | bytes 3076
  1.8 32.0 %collective-permute-start = (bf16[34,1,128,128]{3,2,1,0:T(8,128)(2,1)S(1)}, bf16[34,1,128,128]{3,2,1,0:T(8,128)(2,1)S(1)}, u32[]{:S(2)}, u32[]{:S(2)}) collective-permute-start(bf16[34,1,128,128]{3,2,1,0:T(8,128)(2,1)S(1)} %get-tuple-element.101), channel_id=1, source_target_pairs={{0,1},{1,2},{2,3},{3,4},{4,5},{5,6},{6,7},{7,8},{8,9},{9,10},{10,1... | collective-permute-start | bytes 3342344 | tf_op jit(solution)/shard_map/ppermute | solution.py:17
  5.3 29.3 %collective-permute-start.1 = (bf16[34,1,128,128]{3,2,1,0:T(8,128)(2,1)S(1)}, bf16[34,1,128,128]{3,2,1,0:T(8,128)(2,1)}, u32[]{:S(2)}, u32[]{:S(2)}) collective-permute-start(bf16[34,1,128,128]{3,2,1,0:T(8,128)(2,1)S(1)} %get-tuple-element.102), channel_id=1, source_target_pairs={{1,0},{2,1},{3,2},{4,3},{5,4},{6,5},{7,6},{8,7},{9,8},{10,9},{11,1... | collective-permute-start | bytes 3342344 | tf_op jit(solution)/shard_map/ppermute | solution.py:19
  18.7 26.1 %copy-start.2 = (s32[8]{0:T(128)S(1)}, s32[8]{0:T(128)}, u32[]{:S(2)}) copy-start(s32[8]{0:T(128)} %param.14) | copy-start | bytes 100
  18.7 26.1 %copy-start.3 = (s32[8]{0:T(128)S(1)}, s32[8]{0:T(128)}, u32[]{:S(2)}) copy-start(s32[8]{0:T(128)} %param.15) | copy-start | bytes 100
where the time goes:
time: 377 us; the launch traced here: 375 us
  matrix products  157 us (42%)
  blocking collectives  92 us (24%)
  local copies, waits for them, and re-layouts  47.4 us (13%)
  loops' own time  30.1 us (8%)
  other arithmetic  22.5 us (6%)
  waiting for transfers between devices  16 us (4%)
  starting transfers between devices  9.67 us (3%)
    unnamed x1, blocking collectives  92 us
    dot_general x8, matrix products, one_term(): jnp.einsum('bpxz,pbzy->bpxy', mixed_half, gathered, preferred_element_typ...  84.3 us
    dot_general x8, matrix products, one_term(): jnp.einsum('pq,bqxz->bpxz', matrix, applied_left, preferred_element_type=...  44.3 us
    another operation x1, loops' own time, body(): lax.scan(one_term, jnp.zeros(two_site.shape, jnp.float32), (term_left, te...  30.1 us
    dot_general x8, matrix products, one_term(): jnp.einsum('bxy,bqyz->bqxz', left_block, clean, preferred_element_type=jn...  28.2 us
    gather x8, local copies, waits for them, and re-layouts, one_term(): lax.dynamic_slice_in_dim(right_rows, begin, blocks, 0)  25.3 us
    ppermute x1, waiting for transfers between devices, with_halo(): lax.ppermute(tail, axis, [(i, (i + 1) % count) for i in range(ends)])  15.1 us
    concatenate x1, other arithmetic, with_halo(): jnp.concatenate([lax.ppermute(tail, axis, [(i, (i + 1) % count) for i in...  10.1 us
  transfers between devices with their start and end apart: 2, of which 2 were waited for; matrix products, arithmetic and copies ran while one was open for 2% of the time, Pallas kernels for 0%

commit v1 on v0

v1 whole, which is shorter than its diff:
```python
import functools

import jax
import jax.numpy as jnp
from jax import lax
from jax.experimental import pallas as pl
from jax.experimental.pallas import tpu as pltpu
from jax.sharding import PartitionSpec as P

SH = 1
YT = 16


def sector_limits(block_sizes, shifts, first, blocks, total):
    rows_left = first + jnp.arange(blocks, dtype=jnp.int32)
    right_index = rows_left[:, None] + shifts[None, :]
    inside = (right_index >= 0) & (right_index < total)
    size_left = block_sizes[rows_left]
    size_right = jnp.where(inside, block_sizes[jnp.clip(right_index, 0, total - 1)], 0)
    return size_left.astype(jnp.int32), size_right.astype(jnp.int32)


def kernel(npl, nt, tl_ref, tr_ref, rowlim_ref, collim_ref, outlim_ref, sloc_ref,
           ts_ref, left_ref, kron_ref, rloc0_ref, rloc1_ref, lo_ref, hi_ref,
           out_ref, c_scr, x_scr, y_scr):
    i = pl.program_id(0)
    nb = pl.num_programs(0)
    depth = ts_ref.shape[-1]
    nq = ts_ref.shape[1]
    rows = lax.broadcasted_iota(jnp.int32, (depth, depth), 0)
    cols = lax.broadcasted_iota(jnp.int32, (depth, depth), 1)
    row_ok = rows < rowlim_ref[i]
    for q in range(nq):
        keep = row_ok & (cols < collim_ref[i * nq + q])
        c_scr[q] = jnp.where(keep, ts_ref[0, q], jnp.zeros_like(ts_ref[0, q]))

    nr = npl * nt
    rchunk = 32
    for yb in range(depth // YT):
        cy = c_scr[:, yb * YT:(yb + 1) * YT, :].reshape(nq * YT, depth)
        for rc in range(nr // rchunk):
            k = kron_ref[rc * rchunk * YT:(rc + 1) * rchunk * YT, :]
            xy = jnp.dot(k, cy, preferred_element_type=jnp.float32)
            x_scr[rc * rchunk:(rc + 1) * rchunk, yb * YT:(yb + 1) * YT, :] = (
                xy.reshape(rchunk, YT, depth).astype(x_scr.dtype))

    def left_step(t, carry):
        lt = left_ref[tl_ref[t], 0]
        xs = jnp.concatenate([x_scr[t * npl + p] for p in range(npl)], axis=1)
        yt = jnp.dot(lt, xs, preferred_element_type=jnp.float32).astype(y_scr.dtype)
        for p in range(npl):
            y_scr[p, t] = yt[:, p * depth:(p + 1) * depth]
        return carry

    lax.fori_loop(0, nt, left_step, 0)

    def right_sum(p, src):
        def step(t, acc):
            return acc + jnp.dot(y_scr[p, t], src[tr_ref[t], 0],
                                 preferred_element_type=jnp.float32)
        acc = lax.fori_loop(0, nt, step, jnp.zeros((depth, depth), jnp.float32))
        keep = row_ok & (cols < outlim_ref[i * npl + p])
        out_ref[0, p] = jnp.where(keep, acc, 0.0).astype(out_ref.dtype)

    for p, rloc in enumerate((rloc0_ref, rloc1_ref)):
        j = i + sloc_ref[p]

        @pl.when(j < 0)
        def _():
            right_sum(p, lo_ref)

        @pl.when((j >= 0) & (j < nb))
        def _():
            right_sum(p, rloc)

        @pl.when(j >= nb)
        def _():
            right_sum(p, hi_ref)


def halos(cells, axis, dim, width):
    count = lax.axis_size(axis)
    ends = count - 1
    head = lax.slice_in_dim(cells, 0, width, axis=dim)
    tail = lax.slice_in_dim(cells, cells.shape[dim] - width, cells.shape[dim], axis=dim)
    lo = lax.ppermute(tail, axis, [(i, i + 1) for i in range(ends)])
    hi = lax.ppermute(head, axis, [(i + 1, i) for i in range(ends)])
    return lo, hi


def body(two_site, left_env, right_env, mpo_terms, term_left, term_right, shifts, block_sizes):
    blocks, nq, depth, _ = two_site.shape
    width = left_env.shape[0]
    nmpo = lax.axis_size("mpo")
    npl = nq // nmpo
    total = blocks * lax.axis_size("blk")
    first = lax.axis_index("blk") * blocks
    p_first = lax.axis_index("mpo") * npl

    terms = lax.all_gather(mpo_terms, "mpo", axis=0, tiled=True)
    tl = lax.all_gather(term_left, "mpo", axis=0, tiled=True)
    tr = lax.all_gather(term_right, "mpo", axis=0, tiled=True)
    nt = terms.shape[0]

    rowlim, collim = sector_limits(block_sizes, shifts, first, blocks, total)
    outlim = lax.dynamic_slice_in_dim(collim, p_first, npl, axis=1)
    sloc = lax.dynamic_slice_in_dim(shifts, p_first, npl)

    mine = lax.dynamic_slice_in_dim(terms, p_first, npl, axis=1).reshape(nt * npl, nq)
    eye = jnp.eye(YT, dtype=mine.dtype)
    kron = (mine[:, None, :, None] * eye[None, :, None, :]).reshape(nt * npl * YT, nq * YT)

    lo, hi = halos(right_env, "blk", 1, SH)

    rblock = (width, 1, depth, depth)

    def rloc_map(p):
        def index(b, tl_r, tr_r, rl, cl, ol, sl):
            return (0, jnp.clip(b + sl[p], 0, blocks - 1), 0, 0)
        return index

    const4 = lambda b, *refs: (0, 0, 0, 0)
    grid_spec = pltpu.PrefetchScalarGridSpec(
        num_scalar_prefetch=6,
        grid=(blocks,),
        in_specs=[
            pl.BlockSpec((1, nq, depth, depth), lambda b, *refs: (b, 0, 0, 0)),
            pl.BlockSpec(rblock, lambda b, *refs: (0, b, 0, 0)),
            pl.BlockSpec(kron.shape, lambda b, *refs: (0, 0)),
            pl.BlockSpec(rblock, rloc_map(0)),
            pl.BlockSpec(rblock, rloc_map(1)),
            pl.BlockSpec(rblock, const4),
            pl.BlockSpec(rblock, const4),
        ],
        out_specs=pl.BlockSpec((1, npl, depth, depth), lambda b, *refs: (b, 0, 0, 0)),
        scratch_shapes=[
            pltpu.VMEM((nq, depth, depth), jnp.bfloat16),
            pltpu.VMEM((nt * npl, depth, depth), jnp.bfloat16),
            pltpu.VMEM((npl, nt, depth, depth), jnp.bfloat16),
        ],
    )
    flops = 2 * blocks * (nt * npl * YT * nq * YT * depth + 2 * nt * npl * depth ** 3)
    return pl.pallas_call(
        functools.partial(kernel, npl, nt),
        out_shape=jax.ShapeDtypeStruct((blocks, npl, depth, depth), jnp.bfloat16),
        grid_spec=grid_spec,
        compiler_params=pltpu.CompilerParams(
            dimension_semantics=("arbitrary",), vmem_limit_bytes=60 * 1024 * 1024),
        cost_estimate=pl.CostEstimate(
            flops=flops, transcendentals=0,
            bytes_accessed=2 * (two_site.size + left_env.size + 3 * right_env.size)),
    )(tl, tr, rowlim, collim.reshape(-1), outlim.reshape(-1), sloc,
      two_site, left_env, kron, right_env, right_env, lo, hi)


def solution(mesh):
    return jax.shard_map(
        body,
        mesh=mesh,
        in_specs=(
            P("blk", None, None, None),
            P(None, "blk", None, None),
            P(None, "blk", None, None),
            P("mpo", None, None),
            P("mpo"),
            P("mpo"),
            P(),
            P(),
        ),
        out_specs=P("blk", "mpo", None, None),
        check_vma=False,
    )
```

time: 377 us -> 304 us (0.81)
  Pallas kernels: 0 us -> 246 us
  matrix products: 157 us -> 0 us
  blocking collectives: 92 us -> 21.9 us
  loops' own time: 30.1 us -> 0 us
  local copies, waits for them, and re-layouts: 47.4 us -> 19.4 us
  other arithmetic: 22.5 us -> 4.68 us
  waiting for transfers between devices: 16 us -> 0.01 us
    pallas_call x0 -> x1, Pallas kernels: none -> 246 us  [body(): pl.pallas_call(functools.partial(kernel, npl, nt), out_shape=jax.ShapeDty...]
    dot_general x24 -> x0, matrix products: 157 us -> none  [the longest x8 84.3 us: one_term(): jnp.einsum('bpxz,pbzy->bpxy', mixed_half, gathered, preferred_element_typ...]
    unnamed x1, blocking collectives: 92 us -> 7.8 us
    another operation x1 -> x0, loops' own time: 30.1 us -> none  [body(): lax.scan(one_term, jnp.zeros(two_site.shape, jnp.float32), (term_left, te...]
    gather x8 -> x3, local copies, waits for them, and re-layouts: 25.3 us -> 2.52 us  [the longest x2 1.34 us: sector_limits(): block_sizes[jnp.clip(right_index, 0, total - 1)]]
    ppermute x2, waiting for transfers between devices: 16 us -> 0.01 us  [the longest x1 0.01 us: halos(): lo = lax.ppermute(tail, axis, [(i, i + 1) for i in range(ends)])]
    all_gather x0 -> x1, blocking collectives: none -> 14.1 us  [body(): terms = lax.all_gather(mpo_terms, 'mpo', axis=0, tiled=True)]
    mul x0 -> x1, local copies, waits for them, and re-layouts: none -> 11 us  [body(): mine[:, None, :, None] * eye[None, :, None, :]]
  transfers between devices with their start and end apart: 2 -> 2, of which waited for: 2 -> 0; matrix products, arithmetic and copies ran while one was open for 2% -> 7% of each run, Pallas kernels for 0% -> 0%
where the time goes in v1:
time: 304 us; the launch traced here: 303 us
  Pallas kernels  246 us (81%)
  blocking collectives  21.9 us (7%)
  local copies, waits for them, and re-layouts  19.4 us (6%)
  starting transfers between devices  9.67 us (3%)
  other arithmetic  4.68 us (2%)
    pallas_call x1, Pallas kernels, body(): pl.pallas_call(functools.partial(kernel, npl, nt), out_shape=jax.ShapeDty...  246 us
    all_gather x1, blocking collectives, body(): terms = lax.all_gather(mpo_terms, 'mpo', axis=0, tiled=True)  14.1 us
    mul x1, local copies, waits for them, and re-layouts, body(): mine[:, None, :, None] * eye[None, :, None, :]  11 us
    unnamed x1, blocking collectives  7.8 us
    ppermute x1, starting transfers between devices, halos(): hi = lax.ppermute(head, axis, [(i + 1, i) for i in range(ends)])  6.13 us
  transfers between devices with their start and end apart: 2, of which 0 were waited for; matrix products, arithmetic and copies ran while one was open for 7% of the time, Pallas kernels for 0%

profile of v1, /device:TPU:7, one launch (start us, length us, event | category | flops | bytes accessed | tf_op | source)
XLA Modules:
  0.0 302.8 jit_solution(8348204172777959744)
XLA Ops:
  0.0 0.0 copy-start
  0.0 0.0 copy-start.2
  0.0 0.0 copy-start.1
  0.0 1.8 fusion.4
  1.8 3.5 %collective-permute-start = (bf16[34,1,128,128]{3,2,1,0:T(8,128)(2,1)S(1)}, bf16[34,1,128,128]{3,2,1,0:T(8,128)(2,1)S(1)}, u32[]{:S(2)}, u32[]{:S(2)}) collective-permute-start(bf16[34,1,128,128]{3,2,1,0:T(8,128)(2,1)S(1)} %get-tuple-element.8), channel_id=1, source_target_pairs={{0,1},{1,2},{2,3},{3,4},{4,5},{5,6},{6,7},{7,8},{8,9},{9,10},{10,1... | collective-permute-start | bytes 3342344 | tf_op jit(solution)/shard_map/ppermute | solution.py:86
  5.3 6.1 %collective-permute-start.1 = (bf16[34,1,128,128]{3,2,1,0:T(8,128)(2,1)S(1)}, bf16[34,1,128,128]{3,2,1,0:T(8,128)(2,1)}, u32[]{:S(2)}, u32[]{:S(2)}) collective-permute-start(bf16[34,1,128,128]{3,2,1,0:T(8,128)(2,1)S(1)} %get-tuple-element.7), channel_id=1, source_target_pairs={{1,0},{2,1},{3,2},{4,3},{5,4},{6,5},{7,6},{8,7},{9,8},{10,9},{11,1... | collective-permute-start | bytes 3342344 | tf_op jit(solution)/shard_map/ppermute | solution.py:87
  11.5 0.7 compare_select_fusion
  12.3 0.1 reshape.110
  12.4 0.0 copy-done
  12.4 1.2 gather_fusion
  13.5 1.3 gather_fusion.1
  14.8 0.1 reshape.109
  14.9 0.0 copy-done.2
  14.9 0.1 fusion.2
  15.0 0.6 select_n.36.collim_ref
  15.6 0.6 dynamic_slice.10.sloc_ref
  16.2 0.1 constant_dynamic-slice_fusion.1
  16.2 0.6 reshape.99.outlim_ref
  16.9 0.0 copy-done.1
  16.9 14.1 %all_gather.11 = bf16[64,16,16]{2,1,0:T(8,128)(2,1)S(1)} all-gather(bf16[8,16,16]{2,1,0:T(8,128)(2,1)S(1)} %copy-done.1), channel_id=1, replica_groups=mesh['mpo'=8,'blk'=32] {'mpo'}, dimensions={0}, use_global_device_ids=true | all-gather | bytes 36864 | tf_op jit(solution)/shard_map/all_gather | solution.py:100
  31.0 0.0 copy-start.6
  31.1 0.0 copy-start.4
  31.1 0.0 copy-start.5
  31.1 3.8 %broadcast_multiply_fusion = bf16[128,16,16,16]{3,2,1,0:T(8,128)(2,1)} fusion(bf16[16,16]{1,0:T(8,128)(2,1)S(1)} %fusion, bf16[128,16]{1,0:T(8,128)(2,1)S(1)} %bitcast.8), kind=kLoop, calls=%fused_computation.2 | loop fusion | flops 524288 | bytes 1053184 | tf_op jit(solution)/shard_map/mul | solution.py:111
  34.9 11.0 %mul.31.kron_ref = bf16[2048,256]{1,0:T(8,128)(2,1)} reshape(bf16[128,16,16,16]{3,2,1,0:T(8,128)(2,1)} %broadcast_multiply_fusion) | data formatting | bytes 2097152 | tf_op jit(solution)/shard_map/mul | solution.py:111
  45.9 0.0 copy-done.6
  45.9 0.6 dynamic-slice
  47.2 0.0 copy-done.4
  47.2 0.2 dynamic-update-slice
  47.4 0.0 copy-done.5
  47.4 0.2 dynamic-update-slice.1
  47.7 7.8 %all-reduce.2 = (s32[64]{0:T(128)}, s32[64]{0:T(128)}) all-reduce(s32[64]{0:T(128)S(1)} %dynamic-update-slice, s32[64]{0:T(128)S(1)} %dynamic-update-slice.1), channel_id=1, replica_groups=mesh['mpo'=8,'blk'=32] {'mpo'}, use_global_device_ids=true, to_apply=%add | all-reduce | flops 128 | bytes 1024
  55.5 0.0 collective-permute-done.lo_ref
  55.5 0.0 copy-start.3
  55.5 0.0 collective-permute-done.1.hi_ref
  55.5 1.0 copy-done.3
  56.5 246.3 %shard_map.82 = bf16[8,2,128,128]{3,2,1,0:T(8,128)(2,1)} custom-call(s32[64]{0:T(128)} %get-tuple-element.5.tl_ref, s32[64]{0:T(128)} %get-tuple-element.6.tr_ref, s32[8]{0:T(128)} %gather_fusion, s32[128]{0:T(128)} %select_n.36.collim_ref, s32[16]{0:T(128)} %reshape.99.outlim_ref, s32[2]{0:T(128)} %dynamic_slice.10.sloc_ref, ...), custom_call_target="tpu_custom_call" | custom-call | flops 9663676416 | bytes 39845888 | tf_op jit(solution)/shard_map/pallas_call | solution.py:143
  (8 shorter events, 0.1 us)
Async XLA Ops:
  0.0 12.4 %copy-start = (s32[256]{0:T(256)S(1)}, s32[256]{0:T(256)}, u32[]{:S(2)}) copy-start(s32[256]{0:T(256)} %param.15) | copy-start | bytes 3076
  0.0 14.9 %copy-start.2 = (s32[16]{0:T(128)S(1)}, s32[16]{0:T(128)}, u32[]{:S(2)}) copy-start(s32[16]{0:T(128)} %param.14) | copy-start | bytes 196
  0.0 16.9 %copy-start.1 = (bf16[8,16,16]{2,1,0:T(8,128)(2,1)S(1)}, bf16[8,16,16]{2,1,0:T(8,128)(2,1)}, u32[]{:S(2)}) copy-start(bf16[8,16,16]{2,1,0:T(8,128)(2,1)} %param.11) | copy-start | bytes 12292
  1.8 53.7 %collective-permute-start = (bf16[34,1,128,128]{3,2,1,0:T(8,128)(2,1)S(1)}, bf16[34,1,128,128]{3,2,1,0:T(8,128)(2,1)S(1)}, u32[]{:S(2)}, u32[]{:S(2)}) collective-permute-start(bf16[34,1,128,128]{3,2,1,0:T(8,128)(2,1)S(1)} %get-tuple-element.8), channel_id=1, source_target_pairs={{0,1},{1,2},{2,3},{3,4},{4,5},{5,6},{6,7},{7,8},{8,9},{9,10},{10,1... | collective-permute-start | bytes 3342344 | tf_op jit(solution)/shard_map/ppermute | solution.py:86
  5.3 50.1 %collective-permute-start.1 = (bf16[34,1,128,128]{3,2,1,0:T(8,128)(2,1)S(1)}, bf16[34,1,128,128]{3,2,1,0:T(8,128)(2,1)}, u32[]{:S(2)}, u32[]{:S(2)}) collective-permute-start(bf16[34,1,128,128]{3,2,1,0:T(8,128)(2,1)S(1)} %get-tuple-element.7), channel_id=1, source_target_pairs={{1,0},{2,1},{3,2},{4,3},{5,4},{6,5},{7,6},{8,7},{9,8},{10,9},{11,1... | collective-permute-start | bytes 3342344 | tf_op jit(solution)/shard_map/ppermute | solution.py:87
  31.0 14.9 %copy-start.6 = (u32[256]{0:T(256)S(1)}, u32[256]{0:T(256)}, u32[]{:S(2)}) copy-start(u32[256]{0:T(256)} %constant.29) | copy-start | bytes 3076
  31.1 16.1 %copy-start.4 = (s32[8]{0:T(128)S(1)}, s32[8]{0:T(128)}, u32[]{:S(2)}) copy-start(s32[8]{0:T(128)} %param.12) | copy-start | bytes 100
  31.1 16.4 %copy-start.5 = (s32[8]{0:T(128)S(1)}, s32[8]{0:T(128)}, u32[]{:S(2)}) copy-start(s32[8]{0:T(128)} %param.13) | copy-start | bytes 100
  55.5 1.0 copy-start.3

commit v2 on v1

--- a/solution.py
+++ b/solution.py
@@ -9,6 +9,8 @@
 
 SH = 1
 YT = 16
+UNROLL = 8
+VARIANT = ""
 
 
 def sector_limits(block_sizes, shifts, first, blocks, total):
@@ -21,8 +23,8 @@
 
 
 def kernel(npl, nt, tl_ref, tr_ref, rowlim_ref, collim_ref, outlim_ref, sloc_ref,
-           ts_ref, left_ref, kron_ref, rloc0_ref, rloc1_ref, lo_ref, hi_ref,
-           out_ref, c_scr, x_scr, y_scr):
+           ts_ref, left_ref, mq_ref, rloc0_ref, rloc1_ref, lo_ref, hi_ref,
+           out_ref, c_scr, x_scr, y_scr, kron_scr):
     i = pl.program_id(0)
     nb = pl.num_programs(0)
     depth = ts_ref.shape[-1]
@@ -36,13 +38,29 @@
 
     nr = npl * nt
     rchunk = 32
-    for yb in range(depth // YT):
-        cy = c_scr[:, yb * YT:(yb + 1) * YT, :].reshape(nq * YT, depth)
+
+    @pl.when(i == 0)
+    def _():
+        a = lax.broadcasted_iota(jnp.int32, (nr * YT, nr), 0)
+        r = lax.broadcasted_iota(jnp.int32, (nr * YT, nr), 1)
+        pick = jnp.where(a // YT == r, 1.0, 0.0).astype(mq_ref.dtype)
+        rep = jnp.dot(pick, mq_ref[...], preferred_element_type=jnp.float32)
+        ra = lax.broadcasted_iota(jnp.int32, rep.shape, 0)
+        cb = lax.broadcasted_iota(jnp.int32, rep.shape, 1)
+        kron_scr[...] = jnp.where(ra % YT == cb % YT, rep, 0.0).astype(kron_scr.dtype)
+
+    for yb in range(0 if "nomix" in VARIANT else depth // (2 * YT)):
+        ya, yc = 2 * yb * YT, (2 * yb + 1) * YT
+        cy = jnp.concatenate(
+            [c_scr[:, ya:ya + YT, :].reshape(nq * YT, depth),
+             c_scr[:, yc:yc + YT, :].reshape(nq * YT, depth)], axis=1)
         for rc in range(nr // rchunk):
-            k = kron_ref[rc * rchunk * YT:(rc + 1) * rchunk * YT, :]
+            k = kron_scr[rc * rchunk * YT:(rc + 1) * rchunk * YT, :]
             xy = jnp.dot(k, cy, preferred_element_type=jnp.float32)
-            x_scr[rc * rchunk:(rc + 1) * rchunk, yb * YT:(yb + 1) * YT, :] = (
-                xy.reshape(rchunk, YT, depth).astype(x_scr.dtype))
+            for half, y0 in enumerate((ya, yc)):
+                x_scr[rc * rchunk:(rc + 1) * rchunk, y0:y0 + YT, :] = (
+                    xy[:, half * depth:(half + 1) * depth]
+                    .reshape(rchunk, YT, depth).astype(x_scr.dtype))
 
     def left_step(t, carry):
         lt = left_ref[tl_ref[t], 0]
@@ -52,17 +70,21 @@
             y_scr[p, t] = yt[:, p * depth:(p + 1) * depth]
         return carry
 
-    lax.fori_loop(0, nt, left_step, 0)
+    if "noleft" not in VARIANT:
+        lax.fori_loop(0, nt, left_step, 0, unroll=UNROLL)
 
     def right_sum(p, src):
-        def step(t, acc):
-            return acc + jnp.dot(y_scr[p, t], src[tr_ref[t], 0],
-                                 preferred_element_type=jnp.float32)
-        acc = lax.fori_loop(0, nt, step, jnp.zeros((depth, depth), jnp.float32))
+        def step(u, acc):
+            ta, tb = 2 * u, 2 * u + 1
+            lhs = jnp.concatenate([y_scr[p, ta], y_scr[p, tb]], axis=1)
+            rhs = jnp.concatenate([src[tr_ref[ta], 0], src[tr_ref[tb], 0]], axis=0)
+            return acc + jnp.dot(lhs, rhs, preferred_element_type=jnp.float32)
+        acc = lax.fori_loop(0, nt // 2, step, jnp.zeros((depth, depth), jnp.float32),
+                            unroll=UNROLL)
         keep = row_ok & (cols < outlim_ref[i * npl + p])
         out_ref[0, p] = jnp.where(keep, acc, 0.0).astype(out_ref.dtype)
 
-    for p, rloc in enumerate((rloc0_ref, rloc1_ref)):
+    for p, rloc in enumerate(() if "noright" in VARIANT else (rloc0_ref, rloc1_ref)):
         j = i + sloc_ref[p]
 
         @pl.when(j < 0)
@@ -97,21 +119,35 @@
     first = lax.axis_index("blk") * blocks
     p_first = lax.axis_index("mpo") * npl
 
-    terms = lax.all_gather(mpo_terms, "mpo", axis=0, tiled=True)
-    tl = lax.all_gather(term_left, "mpo", axis=0, tiled=True)
-    tr = lax.all_gather(term_right, "mpo", axis=0, tiled=True)
-    nt = terms.shape[0]
+    local_terms = mpo_terms.shape[0]
+    packed = jnp.concatenate(
+        [mpo_terms.reshape(local_terms, nq * nq),
+         term_left[:, None].astype(mpo_terms.dtype),
+         term_right[:, None].astype(mpo_terms.dtype)], axis=1)
+    packed = lax.all_gather(packed, "mpo", axis=0, tiled=True)
+    nt = packed.shape[0]
+    terms = packed[:, :nq * nq].reshape(nt, nq, nq)
+    tl = packed[:, nq * nq].astype(jnp.int32)
+    tr = packed[:, nq * nq + 1].astype(jnp.int32)
 
     rowlim, collim = sector_limits(block_sizes, shifts, first, blocks, total)
     outlim = lax.dynamic_slice_in_dim(collim, p_first, npl, axis=1)
     sloc = lax.dynamic_slice_in_dim(shifts, p_first, npl)
 
     mine = lax.dynamic_slice_in_dim(terms, p_first, npl, axis=1).reshape(nt * npl, nq)
-    eye = jnp.eye(YT, dtype=mine.dtype)
-    kron = (mine[:, None, :, None] * eye[None, :, None, :]).reshape(nt * npl * YT, nq * YT)
+    mq = jnp.repeat(mine, YT, axis=1)
 
     lo, hi = halos(right_env, "blk", 1, SH)
 
+    return block_call(tl, tr, rowlim, collim.reshape(-1), outlim.reshape(-1), sloc,
+                      two_site, left_env, mq, right_env, lo, hi)
+
+
+def block_call(tl, tr, rowlim, collim, outlim, sloc, two_site, left_env, mq, right_env, lo, hi):
+    blocks, nq, depth, _ = two_site.shape
+    width = left_env.shape[0]
+    npl = sloc.shape[0]
+    nt = tl.shape[0]
     rblock = (width, 1, depth, depth)
 
     def rloc_map(p):
@@ -126,7 +162,7 @@
         in_specs=[
             pl.BlockSpec((1, nq, depth, depth), lambda b, *refs: (b, 0, 0, 0)),
             pl.BlockSpec(rblock, lambda b, *refs: (0, b, 0, 0)),
-            pl.BlockSpec(kron.shape, lambda b, *refs: (0, 0)),
+            pl.BlockSpec(mq.shape, lambda b, *refs: (0, 0)),
             pl.BlockSpec(rblock, rloc_map(0)),
             pl.BlockSpec(rblock, rloc_map(1)),
             pl.BlockSpec(rblock, const4),
@@ -137,6 +173,7 @@
             pltpu.VMEM((nq, depth, depth), jnp.bfloat16),
             pltpu.VMEM((nt * npl, depth, depth), jnp.bfloat16),
             pltpu.VMEM((npl, nt, depth, depth), jnp.bfloat16),
+            pltpu.VMEM((nt * npl * YT, nq * YT), jnp.bfloat16),
         ],
     )
     flops = 2 * blocks * (nt * npl * YT * nq * YT * depth + 2 * nt * npl * depth ** 3)
@@ -149,8 +186,8 @@
         cost_estimate=pl.CostEstimate(
             flops=flops, transcendentals=0,
             bytes_accessed=2 * (two_site.size + left_env.size + 3 * right_env.size)),
-    )(tl, tr, rowlim, collim.reshape(-1), outlim.reshape(-1), sloc,
-      two_site, left_env, kron, right_env, right_env, lo, hi)
+    )(tl, tr, rowlim, collim, outlim, sloc,
+      two_site, left_env, mq, right_env, right_env, lo, hi)
 
 
 def solution(mesh):

time: 304 us -> 95.2 us (0.31)
  Pallas kernels: 246 us -> 55 us
  local copies, waits for them, and re-layouts: 19.4 us -> 7.71 us
  blocking collectives: 21.9 us -> 14.1 us
  waiting for transfers between devices: 0.01 us -> 6.17 us
  other arithmetic: 4.68 us -> 1.03 us
    pallas_call x1, Pallas kernels: 246 us -> 55 us  [block_call(): pl.pallas_call(functools.partial(kernel, npl, nt), out_shape=jax.ShapeDty...]
    mul x1 -> x0, local copies, waits for them, and re-layouts: 11 us -> none  [body(): mine[:, None, :, None] * eye[None, :, None, :]]
    unnamed x1 -> x0, blocking collectives: 7.8 us -> none
    ppermute x1, waiting for transfers between devices: 0.01 us -> 6.01 us  [halos(): lo = lax.ppermute(tail, axis, [(i, i + 1) for i in range(ends)])]
    mul x1 -> x0, other arithmetic: 3.85 us -> none  [body(): mine[:, None, :, None] * eye[None, :, None, :]]
  transfers between devices with their start and end apart: 2 -> 2, of which waited for: 0 -> 2; matrix products, arithmetic and copies ran while one was open for 7% -> 7% of each run, Pallas kernels for 0% -> 0%
where the time goes in v2:
time: 95.2 us; the launch traced here: 93.8 us
  Pallas kernels  55 us (58%)
  blocking collectives  14.1 us (15%)
  starting transfers between devices  9.67 us (10%)
  local copies, waits for them, and re-layouts  7.71 us (8%)
  waiting for transfers between devices  6.17 us (6%)
  other arithmetic  1.03 us (1%)
    pallas_call x1, Pallas kernels, block_call(): pl.pallas_call(functools.partial(kernel, npl, nt), out_shape=jax.ShapeDty...  55 us
    all_gather x1, blocking collectives, body(): packed = lax.all_gather(packed, 'mpo', axis=0, tiled=True)  14.1 us
    ppermute x1, starting transfers between devices, halos(): hi = lax.ppermute(head, axis, [(i + 1, i) for i in range(ends)])  7.75 us
    ppermute x1, waiting for transfers between devices, halos(): lo = lax.ppermute(tail, axis, [(i, i + 1) for i in range(ends)])  6.01 us
    ppermute x1, starting transfers between devices, halos(): lo = lax.ppermute(tail, axis, [(i, i + 1) for i in range(ends)])  1.92 us
  transfers between devices with their start and end apart: 2, of which 2 were waited for; matrix products, arithmetic and copies ran while one was open for 7% of the time, Pallas kernels for 0%

profile of v2, /device:TPU:7, one launch (start us, length us, event | category | flops | bytes accessed | tf_op | source)
XLA Modules:
  0.0 93.8 jit_solution(8840195986917928786)
XLA Ops:
  0.0 0.0 copy-start
  0.0 0.0 copy-start.4
  0.0 0.0 copy-start.2
  0.0 0.0 copy-start.5
  0.0 1.8 %fusion.3 = (bf16[34,1,128,128]{3,2,1,0:T(8,128)(2,1)S(1)}, bf16[34,1,128,128]{3,2,1,0:T(8,128)(2,1)S(1)}) fusion(bf16[34,8,128,128]{3,2,1,0:T(8,128)(2,1)} %rloc1_ref.1), kind=kLoop, calls=%fused_computation.19 | loop fusion | bytes 4456448 | tf_op jit(solution)/shard_map/slice | solution.py:106
  1.8 7.8 %collective-permute-start.1 = (bf16[34,1,128,128]{3,2,1,0:T(8,128)(2,1)S(1)}, bf16[34,1,128,128]{3,2,1,0:T(8,128)(2,1)S(1)}, u32[]{:S(2)}, u32[]{:S(2)}) collective-permute-start(bf16[34,1,128,128]{3,2,1,0:T(8,128)(2,1)S(1)} %get-tuple-element.7), channel_id=1, source_target_pairs={{1,0},{2,1},{3,2},{4,3},{5,4},{6,5},{7,6},{8,7},{9,8},{10,9},{11,1... | collective-permute-start | bytes 3342344 | tf_op jit(solution)/shard_map/ppermute | solution.py:109
  9.6 1.9 %collective-permute-start = (bf16[34,1,128,128]{3,2,1,0:T(8,128)(2,1)S(1)}, bf16[34,1,128,128]{3,2,1,0:T(8,128)(2,1)}, u32[]{:S(2)}, u32[]{:S(2)}) collective-permute-start(bf16[34,1,128,128]{3,2,1,0:T(8,128)(2,1)S(1)} %get-tuple-element.8), channel_id=1, source_target_pairs={{0,1},{1,2},{2,3},{3,4},{4,5},{5,6},{6,7},{7,8},{8,9},{9,10},{10,1... | collective-permute-start | bytes 3342344 | tf_op jit(solution)/shard_map/ppermute | solution.py:108
  11.5 0.0 copy-done.4
  11.5 0.0 copy-done.2
  11.5 0.1 compare_select_fusion
  11.6 0.0 copy-done.5
  11.6 0.7 dynamic_slice.10.sloc_ref
  12.3 0.1 copy.25
  12.4 0.1 copy.24
  12.5 0.1 reshape.121
  12.6 0.0 copy-done
  12.6 1.1 %gather_fusion = s32[8]{0:T(128)} fusion(s32[256]{0:T(256)S(1)} %copy-done, s32[1024]{0:T(1024)S(1)} %pad_clamp_fusion.1), kind=kCustom, calls=%fused_computation | custom fusion | bytes 96 | tf_op jit(solution)/shard_map/gather | solution.py:20
  13.7 0.0 copy-start.1
  13.7 1.3 %gather_fusion.1 = s32[128]{0:T(128)S(1)} fusion(s32[256]{0:T(256)S(1)} %copy-done, s32[1024]{0:T(1024)S(1)} %pad_clamp_fusion), kind=kCustom, calls=%fused_computation.1 | custom fusion | bytes 1536 | tf_op jit(solution)/shard_map/gather | solution.py:21
  15.0 0.1 reshape.120
  15.1 0.1 fusion.1
  15.2 0.7 select_n.36.collim_ref
  15.8 0.1 constant_dynamic-slice_fusion.1
  15.9 0.6 reshape.105.outlim_ref
  16.5 0.0 copy-done.1
  16.5 0.1 reshape.104
  16.6 0.1 pad_maximum_fusion
  16.7 14.1 %all_gather.3 = bf16[64,258]{1,0:T(8,128)(2,1)S(1)} all-gather(bf16[8,258]{1,0:T(8,128)(2,1)S(1)} %pad_maximum_fusion), channel_id=1, replica_groups=mesh['mpo'=8,'blk'=32] {'mpo'}, dimensions={0}, use_global_device_ids=true | all-gather | bytes 37152 | tf_op jit(solution)/shard_map/all_gather | solution.py:127
  30.8 0.1 copy.30
  30.9 0.1 copy.27
  31.0 0.1 copy.28
  31.1 0.7 copy.29.mq_ref
  31.8 0.8 convert_reduce_fusion
  32.6 0.2 collective-permute-done.1.hi_ref
  32.8 0.0 copy-start.3
  32.8 6.0 %collective-permute-done.lo_ref = bf16[34,1,128,128]{3,2,1,0:T(8,128)(2,1)} collective-permute-done((bf16[34,1,128,128]{3,2,1,0:T(8,128)(2,1)S(1)}, bf16[34,1,128,128]{3,2,1,0:T(8,128)(2,1)}, u32[]{:S(2)}, u32[]{:S(2)}) %collective-permute-start) | collective-permute-done | bytes 1114144 | tf_op jit(solution)/shard_map/ppermute | solution.py:108
  38.8 0.0 copy-done.3
  38.8 55.0 %shard_map.82 = bf16[8,2,128,128]{3,2,1,0:T(8,128)(2,1)} custom-call(s32[64]{0:T(128)} %get-tuple-element.6.tl_ref, s32[64]{0:T(128)} %get-tuple-element.5.tr_ref, s32[8]{0:T(128)} %gather_fusion, s32[128]{0:T(128)} %select_n.36.collim_ref, s32[16]{0:T(128)} %reshape.105.outlim_ref, s32[2]{0:T(128)} %dynamic_slice.10.sloc_ref, ...), custom_call_target="tpu_custom_call" | custom-call | flops 9663676416 | bytes 39845888 | tf_op jit(solution)/shard_map/pallas_call | solution.py:180
  (9 shorter events, 0.1 us)
Async XLA Ops:
  0.0 12.6 %copy-start = (s32[256]{0:T(256)S(1)}, s32[256]{0:T(256)}, u32[]{:S(2)}) copy-start(s32[256]{0:T(256)} %param.15) | copy-start | bytes 3076
  0.0 11.5 %copy-start.4 = (s32[8]{0:T(128)S(1)}, s32[8]{0:T(128)}, u32[]{:S(2)}) copy-start(s32[8]{0:T(128)} %param.12) | copy-start | bytes 100
  0.0 11.5 %copy-start.2 = (s32[16]{0:T(128)S(1)}, s32[16]{0:T(128)}, u32[]{:S(2)}) copy-start(s32[16]{0:T(128)} %param.14) | copy-start | bytes 196
  0.0 11.6 %copy-start.5 = (s32[8]{0:T(128)S(1)}, s32[8]{0:T(128)}, u32[]{:S(2)}) copy-start(s32[8]{0:T(128)} %param.13) | copy-start | bytes 100
  1.8 31.0 %collective-permute-start.1 = (bf16[34,1,128,128]{3,2,1,0:T(8,128)(2,1)S(1)}, bf16[34,1,128,128]{3,2,1,0:T(8,128)(2,1)S(1)}, u32[]{:S(2)}, u32[]{:S(2)}) collective-permute-start(bf16[34,1,128,128]{3,2,1,0:T(8,128)(2,1)S(1)} %get-tuple-element.7), channel_id=1, source_target_pairs={{1,0},{2,1},{3,2},{4,3},{5,4},{6,5},{7,6},{8,7},{9,8},{10,9},{11,1... | collective-permute-start | bytes 3342344 | tf_op jit(solution)/shard_map/ppermute | solution.py:109
  9.6 29.2 %collective-permute-start = (bf16[34,1,128,128]{3,2,1,0:T(8,128)(2,1)S(1)}, bf16[34,1,128,128]{3,2,1,0:T(8,128)(2,1)}, u32[]{:S(2)}, u32[]{:S(2)}) collective-permute-start(bf16[34,1,128,128]{3,2,1,0:T(8,128)(2,1)S(1)} %get-tuple-element.8), channel_id=1, source_target_pairs={{0,1},{1,2},{2,3},{3,4},{4,5},{5,6},{6,7},{7,8},{8,9},{9,10},{10,1... | collective-permute-start | bytes 3342344 | tf_op jit(solution)/shard_map/ppermute | solution.py:108
  13.7 2.8 %copy-start.1 = (bf16[8,16,16]{2,1,0:T(8,128)(2,1)S(1)}, bf16[8,16,16]{2,1,0:T(8,128)(2,1)}, u32[]{:S(2)}) copy-start(bf16[8,16,16]{2,1,0:T(8,128)(2,1)} %param.11) | copy-start | bytes 12292
  32.8 6.0 %copy-start.3 = (bf16[34,1,128,128]{3,2,1,0:T(8,128)(2,1)}, bf16[34,1,128,128]{3,2,1,0:T(8,128)(2,1)S(1)}, u32[]{:S(2)}) copy-start(bf16[34,1,128,128]{3,2,1,0:T(8,128)(2,1)S(1)} %collective-permute-done.1.hi_ref) | copy-start | bytes 3342340

commit v3 on v2

--- a/solution.py
+++ b/solution.py
@@ -100,6 +100,42 @@
             right_sum(p, hi_ref)
 
 
+def gather_kernel(nm, x_ref, out_ref, send_sem, recv_sem):
+    me = lax.axis_index("mpo")
+    barrier = pltpu.get_barrier_semaphore()
+    for d in range(1, nm):
+        pl.semaphore_signal(barrier, inc=1, device_id={"mpo": lax.rem(me + d, nm)},
+                            device_id_type=pl.DeviceIdType.MESH)
+    pl.semaphore_wait(barrier, nm - 1)
+    copies = []
+    for d in range(1, nm):
+        copy = pltpu.make_async_remote_copy(
+            src_ref=x_ref,
+            dst_ref=out_ref.at[me],
+            send_sem=send_sem.at[d],
+            recv_sem=recv_sem.at[d],
+            device_id={"mpo": lax.rem(me + d, nm)},
+            device_id_type=pl.DeviceIdType.MESH,
+        )
+        copy.start()
+        copies.append(copy)
+    out_ref[me] = x_ref[...]
+    for copy in copies:
+        copy.wait()
+
+
+def gather_terms(packed):
+    nm = lax.axis_size("mpo")
+    return pl.pallas_call(
+        functools.partial(gather_kernel, nm),
+        out_shape=jax.ShapeDtypeStruct((nm,) + packed.shape, packed.dtype),
+        in_specs=[pl.BlockSpec(memory_space=pltpu.VMEM)],
+        out_specs=pl.BlockSpec(memory_space=pltpu.VMEM),
+        scratch_shapes=[pltpu.SemaphoreType.DMA((nm,)), pltpu.SemaphoreType.DMA((nm,))],
+        compiler_params=pltpu.CompilerParams(collective_id=0, has_side_effects=True),
+    )(packed).reshape(nm * packed.shape[0], packed.shape[1])
+
+
 def halos(cells, axis, dim, width):
     count = lax.axis_size(axis)
     ends = count - 1
@@ -123,10 +159,10 @@
     packed = jnp.concatenate(
         [mpo_terms.reshape(local_terms, nq * nq),
          term_left[:, None].astype(mpo_terms.dtype),
-         term_right[:, None].astype(mpo_terms.dtype)], axis=1)
-    packed = lax.all_gather(packed, "mpo", axis=0, tiled=True)
+         term_right[:, None].astype(mpo_terms.dtype)], axis=1).astype(jnp.float32)
+    packed = gather_terms(packed)
     nt = packed.shape[0]
-    terms = packed[:, :nq * nq].reshape(nt, nq, nq)
+    terms = packed[:, :nq * nq].reshape(nt, nq, nq).astype(mpo_terms.dtype)
     tl = packed[:, nq * nq].astype(jnp.int32)
     tr = packed[:, nq * nq + 1].astype(jnp.int32)
 

time: 95.2 us -> 95.3 us (level)
  blocking collectives: 14.1 us -> 0 us
  Pallas kernels: 55 us -> 63.7 us
  waiting for transfers between devices: 6.17 us -> 9.23 us
  other arithmetic: 1.03 us -> 2.46 us
    all_gather x1 -> x0, blocking collectives: 14.1 us -> none  [body(): packed = lax.all_gather(packed, 'mpo', axis=0, tiled=True)]
    pallas_call x0 -> x1, Pallas kernels: none -> 8.7 us  [gather_terms(): pl.pallas_call(functools.partial(gather_kernel, nm), out_shape=jax.ShapeD...]
    ppermute x1, waiting for transfers between devices: 0.15 us -> 3.22 us  [halos(): hi = lax.ppermute(head, axis, [(i + 1, i) for i in range(ends)])]
    slice x1 -> x2, local copies, waits for them, and re-layouts: 0.01 us -> 0.96 us  [body(): terms = packed[:, :nq * nq].reshape(nt, nq, nq).astype(mpo_terms.dtype)]
  transfers between devices with their start and end apart: 2 -> 2, of which waited for: 2 -> 2; matrix products, arithmetic and copies ran while one was open for 7% -> 10% of each run, Pallas kernels for 0% -> 9%
where the time goes in v3:
time: 95.3 us; the launch traced here: 93.8 us
  Pallas kernels  63.7 us (67%)
  starting transfers between devices  9.67 us (10%)
  waiting for transfers between devices  9.23 us (10%)
  local copies, waits for them, and re-layouts  8.59 us (9%)
  other arithmetic  2.46 us (3%)
    pallas_call x1, Pallas kernels, block_call(): pl.pallas_call(functools.partial(kernel, npl, nt), out_shape=jax.ShapeDty...  55 us
    pallas_call x1, Pallas kernels, gather_terms(): pl.pallas_call(functools.partial(gather_kernel, nm), out_shape=jax.ShapeD...  8.7 us
    ppermute x1, starting transfers between devices, halos(): hi = lax.ppermute(head, axis, [(i + 1, i) for i in range(ends)])  7.75 us
    ppermute x1, waiting for transfers between devices, halos(): lo = lax.ppermute(tail, axis, [(i, i + 1) for i in range(ends)])  6.01 us
    ppermute x1, waiting for transfers between devices, halos(): hi = lax.ppermute(head, axis, [(i + 1, i) for i in range(ends)])  3.22 us
    ppermute x1, starting transfers between devices, halos(): lo = lax.ppermute(tail, axis, [(i, i + 1) for i in range(ends)])  1.92 us
  transfers between devices with their start and end apart: 2, of which 2 were waited for; matrix products, arithmetic and copies ran while one was open for 10% of the time, Pallas kernels for 9%

profile of v3, /device:TPU:7, one launch (start us, length us, event | category | flops | bytes accessed | tf_op | source)
XLA Modules:
  0.0 93.8 jit_solution(8018660628129332505)
XLA Ops:
  0.0 0.0 copy-start
  0.0 0.0 copy-start.4
  0.0 0.0 copy-start.2
  0.0 0.0 copy-start.5
  0.0 1.8 %fusion.5 = (bf16[34,1,128,128]{3,2,1,0:T(8,128)(2,1)S(1)}, bf16[34,1,128,128]{3,2,1,0:T(8,128)(2,1)S(1)}) fusion(bf16[34,8,128,128]{3,2,1,0:T(8,128)(2,1)} %rloc1_ref.1), kind=kLoop, calls=%fused_computation.22 | loop fusion | bytes 4456448 | tf_op jit(solution)/shard_map/slice | solution.py:142
  1.8 7.8 %collective-permute-start.1 = (bf16[34,1,128,128]{3,2,1,0:T(8,128)(2,1)S(1)}, bf16[34,1,128,128]{3,2,1,0:T(8,128)(2,1)S(1)}, u32[]{:S(2)}, u32[]{:S(2)}) collective-permute-start(bf16[34,1,128,128]{3,2,1,0:T(8,128)(2,1)S(1)} %get-tuple-element.7), channel_id=1, source_target_pairs={{1,0},{2,1},{3,2},{4,3},{5,4},{6,5},{7,6},{8,7},{9,8},{10,9},{11,1... | collective-permute-start | bytes 3342344 | tf_op jit(solution)/shard_map/ppermute | solution.py:145
  9.6 1.9 %collective-permute-start = (bf16[34,1,128,128]{3,2,1,0:T(8,128)(2,1)S(1)}, bf16[34,1,128,128]{3,2,1,0:T(8,128)(2,1)}, u32[]{:S(2)}, u32[]{:S(2)}) collective-permute-start(bf16[34,1,128,128]{3,2,1,0:T(8,128)(2,1)S(1)} %get-tuple-element.8), channel_id=1, source_target_pairs={{0,1},{1,2},{2,3},{3,4},{4,5},{5,6},{6,7},{7,8},{8,9},{9,10},{10,1... | collective-permute-start | bytes 3342344 | tf_op jit(solution)/shard_map/ppermute | solution.py:144
  11.5 0.0 copy-done.4
  11.5 0.0 copy-done.2
  11.5 0.1 compare_select_fusion
  11.6 0.0 copy-done.5
  11.6 0.7 dynamic_slice.10.sloc_ref
  12.3 0.1 copy.34
  12.4 0.1 copy.33
  12.5 0.1 reshape.119
  12.6 0.0 copy-done
  12.6 1.2 %gather_fusion = s32[8]{0:T(128)} fusion(s32[256]{0:T(256)S(1)} %copy-done, s32[1024]{0:T(1024)S(1)} %pad_clamp_fusion.1), kind=kCustom, calls=%fused_computation | custom fusion | bytes 96 | tf_op jit(solution)/shard_map/gather | solution.py:20
  13.8 0.0 copy-start.1
  13.8 1.3 %gather_fusion.1 = s32[128]{0:T(128)S(1)} fusion(s32[256]{0:T(256)S(1)} %copy-done, s32[1024]{0:T(1024)S(1)} %pad_clamp_fusion), kind=kCustom, calls=%fused_computation.1 | custom fusion | bytes 1536 | tf_op jit(solution)/shard_map/gather | solution.py:21
  15.0 0.1 reshape.118
  15.1 0.1 fusion.3
  15.2 0.7 select_n.36.collim_ref
  15.9 0.1 constant_dynamic-slice_fusion.1
  15.9 0.6 reshape.106.outlim_ref
  16.5 0.0 copy-done.1
  16.5 0.1 reshape.104
  16.6 0.7 maximum_convert_fusion.x_ref
  17.3 8.7 %shard_map.82 = f32[8,8,258]{2,1,0:T(8,128)} custom-call(f32[8,258]{1,0:T(8,128)} %maximum_convert_fusion.x_ref), custom_call_target="tpu_custom_call" | custom-call | tf_op jit(solution)/shard_map/pallas_call | solution.py:129
  26.0 0.8 slice.35
  26.9 0.1 copy.35
  27.0 0.1 copy.36
  27.1 0.1 copy.37
  27.2 0.7 copy.38.mq_ref
  27.9 1.6 %fusion = (s32[64]{0:T(128)}, s32[64]{0:T(128)}) fusion(f32[64,258]{1,0:T(8,128)} %bitcast.13), kind=kLoop, calls=%fused_computation.4 | loop fusion | flops 128 | bytes 1024 | tf_op jit(solution)/shard_map/convert_element_type | solution.py:167
  29.6 3.2 %collective-permute-done.1.hi_ref = bf16[34,1,128,128]{3,2,1,0:T(8,128)(2,1)S(1)} collective-permute-done((bf16[34,1,128,128]{3,2,1,0:T(8,128)(2,1)S(1)}, bf16[34,1,128,128]{3,2,1,0:T(8,128)(2,1)S(1)}, u32[]{:S(2)}, u32[]{:S(2)}) %collective-permute-start.1) | collective-permute-done | bytes 1114144 | tf_op jit(solution)/shard_map/ppermute | solution.py:145
  32.8 0.0 copy-start.3
  32.8 6.0 %collective-permute-done.lo_ref = bf16[34,1,128,128]{3,2,1,0:T(8,128)(2,1)} collective-permute-done((bf16[34,1,128,128]{3,2,1,0:T(8,128)(2,1)S(1)}, bf16[34,1,128,128]{3,2,1,0:T(8,128)(2,1)}, u32[]{:S(2)}, u32[]{:S(2)}) %collective-permute-start) | collective-permute-done | bytes 1114144 | tf_op jit(solution)/shard_map/ppermute | solution.py:144
  38.8 0.0 copy-done.3
  38.8 55.0 %shard_map.83 = bf16[8,2,128,128]{3,2,1,0:T(8,128)(2,1)} custom-call(s32[64]{0:T(128)} %get-tuple-element.6.tl_ref, s32[64]{0:T(128)} %get-tuple-element.5.tr_ref, s32[8]{0:T(128)} %gather_fusion, s32[128]{0:T(128)} %select_n.36.collim_ref, s32[16]{0:T(128)} %reshape.106.outlim_ref, s32[2]{0:T(128)} %dynamic_slice.10.sloc_ref, ...), custom_call_target="tpu_custom_call" | custom-call | flops 9663676416 | bytes 39845888 | tf_op jit(solution)/shard_map/pallas_call | solution.py:216
  (8 shorter events, 0.1 us)
Async XLA Ops:
  0.0 12.6 %copy-start = (s32[256]{0:T(256)S(1)}, s32[256]{0:T(256)}, u32[]{:S(2)}) copy-start(s32[256]{0:T(256)} %param.15) | copy-start | bytes 3076
  0.0 11.5 %copy-start.4 = (s32[8]{0:T(128)S(1)}, s32[8]{0:T(128)}, u32[]{:S(2)}) copy-start(s32[8]{0:T(128)} %param.12) | copy-start | bytes 100
  0.0 11.5 %copy-start.2 = (s32[16]{0:T(128)S(1)}, s32[16]{0:T(128)}, u32[]{:S(2)}) copy-start(s32[16]{0:T(128)} %param.14) | copy-start | bytes 196
  0.0 11.6 %copy-start.5 = (s32[8]{0:T(128)S(1)}, s32[8]{0:T(128)}, u32[]{:S(2)}) copy-start(s32[8]{0:T(128)} %param.13) | copy-start | bytes 100
  1.8 31.0 %collective-permute-start.1 = (bf16[34,1,128,128]{3,2,1,0:T(8,128)(2,1)S(1)}, bf16[34,1,128,128]{3,2,1,0:T(8,128)(2,1)S(1)}, u32[]{:S(2)}, u32[]{:S(2)}) collective-permute-start(bf16[34,1,128,128]{3,2,1,0:T(8,128)(2,1)S(1)} %get-tuple-element.7), channel_id=1, source_target_pairs={{1,0},{2,1},{3,2},{4,3},{5,4},{6,5},{7,6},{8,7},{9,8},{10,9},{11,1... | collective-permute-start | bytes 3342344 | tf_op jit(solution)/shard_map/ppermute | solution.py:145
  9.6 29.2 %collective-permute-start = (bf16[34,1,128,128]{3,2,1,0:T(8,128)(2,1)S(1)}, bf16[34,1,128,128]{3,2,1,0:T(8,128)(2,1)}, u32[]{:S(2)}, u32[]{:S(2)}) collective-permute-start(bf16[34,1,128,128]{3,2,1,0:T(8,128)(2,1)S(1)} %get-tuple-element.8), channel_id=1, source_target_pairs={{0,1},{1,2},{2,3},{3,4},{4,5},{5,6},{6,7},{7,8},{8,9},{9,10},{10,1... | collective-permute-start | bytes 3342344 | tf_op jit(solution)/shard_map/ppermute | solution.py:144
  13.8 2.8 %copy-start.1 = (bf16[8,16,16]{2,1,0:T(8,128)(2,1)S(1)}, bf16[8,16,16]{2,1,0:T(8,128)(2,1)}, u32[]{:S(2)}) copy-start(bf16[8,16,16]{2,1,0:T(8,128)(2,1)} %param.11) | copy-start | bytes 12292
  32.8 6.0 %copy-start.3 = (bf16[34,1,128,128]{3,2,1,0:T(8,128)(2,1)}, bf16[34,1,128,128]{3,2,1,0:T(8,128)(2,1)S(1)}, u32[]{:S(2)}) copy-start(bf16[34,1,128,128]{3,2,1,0:T(8,128)(2,1)S(1)} %collective-permute-done.1.hi_ref) | copy-start | bytes 3342340

commit v4 on v3

--- a/solution.py
+++ b/solution.py
@@ -9,8 +9,10 @@
 
 SH = 1
 YT = 16
-UNROLL = 8
+UNROLL = 32
 VARIANT = ""
+RG = 4
+RCHUNK = 64
 
 
 def sector_limits(block_sizes, shifts, first, blocks, total):
@@ -37,7 +39,7 @@
         c_scr[q] = jnp.where(keep, ts_ref[0, q], jnp.zeros_like(ts_ref[0, q]))
 
     nr = npl * nt
-    rchunk = 32
+    rchunk = RCHUNK
 
     @pl.when(i == 0)
     def _():
@@ -75,12 +77,12 @@
 
     def right_sum(p, src):
         def step(u, acc):
-            ta, tb = 2 * u, 2 * u + 1
-            lhs = jnp.concatenate([y_scr[p, ta], y_scr[p, tb]], axis=1)
-            rhs = jnp.concatenate([src[tr_ref[ta], 0], src[tr_ref[tb], 0]], axis=0)
+            ts_ = [RG * u + g for g in range(RG)]
+            lhs = jnp.concatenate([y_scr[p, t] for t in ts_], axis=1)
+            rhs = jnp.concatenate([src[tr_ref[t], 0] for t in ts_], axis=0)
             return acc + jnp.dot(lhs, rhs, preferred_element_type=jnp.float32)
-        acc = lax.fori_loop(0, nt // 2, step, jnp.zeros((depth, depth), jnp.float32),
-                            unroll=UNROLL)
+        acc = lax.fori_loop(0, nt // RG, step, jnp.zeros((depth, depth), jnp.float32),
+                            unroll=max(1, UNROLL * 2 // RG))
         keep = row_ok & (cols < outlim_ref[i * npl + p])
         out_ref[0, p] = jnp.where(keep, acc, 0.0).astype(out_ref.dtype)
 

time: 95.3 us -> 80.4 us (0.84)
  Pallas kernels: 63.7 us -> 48.8 us
    pallas_call x1, Pallas kernels: 55 us -> 40.1 us  [block_call(): pl.pallas_call(functools.partial(kernel, npl, nt), out_shape=jax.ShapeDty...]
  transfers between devices with their start and end apart: 2 -> 2, of which waited for: 2 -> 2; matrix products, arithmetic and copies ran while one was open for 10% -> 12% of each run, Pallas kernels for 9% -> 11%
where the time goes in v4:
time: 80.4 us; the launch traced here: 78.8 us
  Pallas kernels  48.8 us (61%)
  starting transfers between devices  9.67 us (12%)
  waiting for transfers between devices  9.23 us (11%)
  local copies, waits for them, and re-layouts  8.59 us (11%)
  other arithmetic  2.46 us (3%)
    pallas_call x1, Pallas kernels, block_call(): pl.pallas_call(functools.partial(kernel, npl, nt), out_shape=jax.ShapeDty...  40.1 us
    pallas_call x1, Pallas kernels, gather_terms(): pl.pallas_call(functools.partial(gather_kernel, nm), out_shape=jax.ShapeD...  8.7 us
    ppermute x1, starting transfers between devices, halos(): hi = lax.ppermute(head, axis, [(i + 1, i) for i in range(ends)])  7.75 us
    ppermute x1, waiting for transfers between devices, halos(): lo = lax.ppermute(tail, axis, [(i, i + 1) for i in range(ends)])  6.01 us
    ppermute x1, waiting for transfers between devices, halos(): hi = lax.ppermute(head, axis, [(i + 1, i) for i in range(ends)])  3.22 us
    ppermute x1, starting transfers between devices, halos(): lo = lax.ppermute(tail, axis, [(i, i + 1) for i in range(ends)])  1.92 us
    slice x1, local copies, waits for them, and re-layouts, halos(): head = lax.slice_in_dim(cells, 0, width, axis=dim)  1.78 us
  transfers between devices with their start and end apart: 2, of which 2 were waited for; matrix products, arithmetic and copies ran while one was open for 12% of the time, Pallas kernels for 11%

profile of v4, /device:TPU:7, one launch (start us, length us, event | category | flops | bytes accessed | tf_op | source)
XLA Modules:
  0.0 78.8 jit_solution(10948527777560749333)
XLA Ops:
  0.0 0.0 copy-start
  0.0 0.0 copy-start.4
  0.0 0.0 copy-start.2
  0.0 0.0 copy-start.5
  0.0 1.8 %fusion.5 = (bf16[34,1,128,128]{3,2,1,0:T(8,128)(2,1)S(1)}, bf16[34,1,128,128]{3,2,1,0:T(8,128)(2,1)S(1)}) fusion(bf16[34,8,128,128]{3,2,1,0:T(8,128)(2,1)} %rloc1_ref.1), kind=kLoop, calls=%fused_computation.22 | loop fusion | bytes 4456448 | tf_op jit(solution)/shard_map/slice | solution.py:144
  1.8 7.8 %collective-permute-start.1 = (bf16[34,1,128,128]{3,2,1,0:T(8,128)(2,1)S(1)}, bf16[34,1,128,128]{3,2,1,0:T(8,128)(2,1)S(1)}, u32[]{:S(2)}, u32[]{:S(2)}) collective-permute-start(bf16[34,1,128,128]{3,2,1,0:T(8,128)(2,1)S(1)} %get-tuple-element.7), channel_id=1, source_target_pairs={{1,0},{2,1},{3,2},{4,3},{5,4},{6,5},{7,6},{8,7},{9,8},{10,9},{11,1... | collective-permute-start | bytes 3342344 | tf_op jit(solution)/shard_map/ppermute | solution.py:147
  9.6 1.9 %collective-permute-start = (bf16[34,1,128,128]{3,2,1,0:T(8,128)(2,1)S(1)}, bf16[34,1,128,128]{3,2,1,0:T(8,128)(2,1)}, u32[]{:S(2)}, u32[]{:S(2)}) collective-permute-start(bf16[34,1,128,128]{3,2,1,0:T(8,128)(2,1)S(1)} %get-tuple-element.8), channel_id=1, source_target_pairs={{0,1},{1,2},{2,3},{3,4},{4,5},{5,6},{6,7},{7,8},{8,9},{9,10},{10,1... | collective-permute-start | bytes 3342344 | tf_op jit(solution)/shard_map/ppermute | solution.py:146
  11.5 0.0 copy-done.4
  11.5 0.0 copy-done.2
  11.5 0.1 compare_select_fusion
  11.6 0.0 copy-done.5
  11.6 0.7 dynamic_slice.10.sloc_ref
  12.3 0.1 copy.34
  12.4 0.1 copy.33
  12.5 0.1 reshape.119
  12.6 0.0 copy-done
  12.6 1.2 %gather_fusion = s32[8]{0:T(128)} fusion(s32[256]{0:T(256)S(1)} %copy-done, s32[1024]{0:T(1024)S(1)} %pad_clamp_fusion.1), kind=kCustom, calls=%fused_computation | custom fusion | bytes 96 | tf_op jit(solution)/shard_map/gather | solution.py:22
  13.8 0.0 copy-start.1
  13.8 1.3 %gather_fusion.1 = s32[128]{0:T(128)S(1)} fusion(s32[256]{0:T(256)S(1)} %copy-done, s32[1024]{0:T(1024)S(1)} %pad_clamp_fusion), kind=kCustom, calls=%fused_computation.1 | custom fusion | bytes 1536 | tf_op jit(solution)/shard_map/gather | solution.py:23
  15.0 0.1 reshape.118
  15.1 0.1 fusion.3
  15.2 0.7 select_n.36.collim_ref
  15.9 0.1 constant_dynamic-slice_fusion.1
  15.9 0.6 reshape.106.outlim_ref
  16.5 0.0 copy-done.1
  16.5 0.1 reshape.104
  16.6 0.7 maximum_convert_fusion.x_ref
  17.3 8.7 %shard_map.82 = f32[8,8,258]{2,1,0:T(8,128)} custom-call(f32[8,258]{1,0:T(8,128)} %maximum_convert_fusion.x_ref), custom_call_target="tpu_custom_call" | custom-call | tf_op jit(solution)/shard_map/pallas_call | solution.py:131
  26.0 0.8 %slice.35 = bf16[64,256]{1,0:T(8,128)(2,1)S(1)} slice(f32[64,258]{1,0:T(8,128)} %bitcast.12), slice={[0:64], [0:256]} | slice | bytes 65536 | tf_op jit(solution)/shard_map/slice | solution.py:167
  26.9 0.1 copy.35
  27.0 0.1 copy.36
  27.1 0.1 copy.37
  27.2 0.7 copy.38.mq_ref
  27.9 1.6 %fusion = (s32[64]{0:T(128)}, s32[64]{0:T(128)}) fusion(f32[64,258]{1,0:T(8,128)} %bitcast.13), kind=kLoop, calls=%fused_computation.4 | loop fusion | flops 128 | bytes 1024 | tf_op jit(solution)/shard_map/convert_element_type | solution.py:169
  29.6 3.2 %collective-permute-done.1.hi_ref = bf16[34,1,128,128]{3,2,1,0:T(8,128)(2,1)S(1)} collective-permute-done((bf16[34,1,128,128]{3,2,1,0:T(8,128)(2,1)S(1)}, bf16[34,1,128,128]{3,2,1,0:T(8,128)(2,1)S(1)}, u32[]{:S(2)}, u32[]{:S(2)}) %collective-permute-start.1) | collective-permute-done | bytes 1114144 | tf_op jit(solution)/shard_map/ppermute | solution.py:147
  32.8 0.0 copy-start.3
  32.8 6.0 %collective-permute-done.lo_ref = bf16[34,1,128,128]{3,2,1,0:T(8,128)(2,1)} collective-permute-done((bf16[34,1,128,128]{3,2,1,0:T(8,128)(2,1)S(1)}, bf16[34,1,128,128]{3,2,1,0:T(8,128)(2,1)}, u32[]{:S(2)}, u32[]{:S(2)}) %collective-permute-start) | collective-permute-done | bytes 1114144 | tf_op jit(solution)/shard_map/ppermute | solution.py:146
  38.8 0.0 copy-done.3
  38.8 40.1 %shard_map.83 = bf16[8,2,128,128]{3,2,1,0:T(8,128)(2,1)} custom-call(s32[64]{0:T(128)} %get-tuple-element.6.tl_ref, s32[64]{0:T(128)} %get-tuple-element.5.tr_ref, s32[8]{0:T(128)} %gather_fusion, s32[128]{0:T(128)} %select_n.36.collim_ref, s32[16]{0:T(128)} %reshape.106.outlim_ref, s32[2]{0:T(128)} %dynamic_slice.10.sloc_ref, ...), custom_call_target="tpu_custom_call" | custom-call | flops 9663676416 | bytes 39845888 | tf_op jit(solution)/shard_map/pallas_call | solution.py:218
  (8 shorter events, 0.1 us)
Async XLA Ops:
  0.0 12.6 %copy-start = (s32[256]{0:T(256)S(1)}, s32[256]{0:T(256)}, u32[]{:S(2)}) copy-start(s32[256]{0:T(256)} %param.15) | copy-start | bytes 3076
  0.0 11.5 %copy-start.4 = (s32[8]{0:T(128)S(1)}, s32[8]{0:T(128)}, u32[]{:S(2)}) copy-start(s32[8]{0:T(128)} %param.12) | copy-start | bytes 100
  0.0 11.5 %copy-start.2 = (s32[16]{0:T(128)S(1)}, s32[16]{0:T(128)}, u32[]{:S(2)}) copy-start(s32[16]{0:T(128)} %param.14) | copy-start | bytes 196
  0.0 11.6 %copy-start.5 = (s32[8]{0:T(128)S(1)}, s32[8]{0:T(128)}, u32[]{:S(2)}) copy-start(s32[8]{0:T(128)} %param.13) | copy-start | bytes 100
  1.8 31.0 %collective-permute-start.1 = (bf16[34,1,128,128]{3,2,1,0:T(8,128)(2,1)S(1)}, bf16[34,1,128,128]{3,2,1,0:T(8,128)(2,1)S(1)}, u32[]{:S(2)}, u32[]{:S(2)}) collective-permute-start(bf16[34,1,128,128]{3,2,1,0:T(8,128)(2,1)S(1)} %get-tuple-element.7), channel_id=1, source_target_pairs={{1,0},{2,1},{3,2},{4,3},{5,4},{6,5},{7,6},{8,7},{9,8},{10,9},{11,1... | collective-permute-start | bytes 3342344 | tf_op jit(solution)/shard_map/ppermute | solution.py:147
  9.6 29.2 %collective-permute-start = (bf16[34,1,128,128]{3,2,1,0:T(8,128)(2,1)S(1)}, bf16[34,1,128,128]{3,2,1,0:T(8,128)(2,1)}, u32[]{:S(2)}, u32[]{:S(2)}) collective-permute-start(bf16[34,1,128,128]{3,2,1,0:T(8,128)(2,1)S(1)} %get-tuple-element.8), channel_id=1, source_target_pairs={{0,1},{1,2},{2,3},{3,4},{4,5},{5,6},{6,7},{7,8},{8,9},{9,10},{10,1... | collective-permute-start | bytes 3342344 | tf_op jit(solution)/shard_map/ppermute | solution.py:146
  13.8 2.8 %copy-start.1 = (bf16[8,16,16]{2,1,0:T(8,128)(2,1)S(1)}, bf16[8,16,16]{2,1,0:T(8,128)(2,1)}, u32[]{:S(2)}) copy-start(bf16[8,16,16]{2,1,0:T(8,128)(2,1)} %param.11) | copy-start | bytes 12292
  32.8 6.0 %copy-start.3 = (bf16[34,1,128,128]{3,2,1,0:T(8,128)(2,1)}, bf16[34,1,128,128]{3,2,1,0:T(8,128)(2,1)S(1)}, u32[]{:S(2)}) copy-start(bf16[34,1,128,128]{3,2,1,0:T(8,128)(2,1)S(1)} %collective-permute-done.1.hi_ref) | copy-start | bytes 3342340

commit v5 on v4

--- a/solution.py
+++ b/solution.py
@@ -10,6 +10,7 @@
 SH = 1
 YT = 16
 UNROLL = 32
+RUNROLL = 16
 VARIANT = ""
 RG = 4
 RCHUNK = 64
@@ -24,11 +25,17 @@
     return size_left.astype(jnp.int32), size_right.astype(jnp.int32)
 
 
-def kernel(npl, nt, tl_ref, tr_ref, rowlim_ref, collim_ref, outlim_ref, sloc_ref,
-           ts_ref, left_ref, mq_ref, rloc0_ref, rloc1_ref, lo_ref, hi_ref,
-           out_ref, c_scr, x_scr, y_scr, kron_scr):
-    i = pl.program_id(0)
-    nb = pl.num_programs(0)
+def kernel(npl, nt, base, stride, nb, halo, *refs):
+    (tl_ref, tr_ref, rowlim_ref, collim_ref, outlim_ref, sloc_ref,
+     ts_ref, left_ref, mq_ref, rloc0_ref, rloc1_ref) = refs[:11]
+    if halo:
+        lo_ref, hi_ref = refs[11:13]
+        refs = refs[14:]
+    else:
+        refs = refs[11:]
+    out_ref, c_scr, x_scr, y_scr, kron_scr = refs
+    first_step = pl.program_id(0) == 0
+    i = base + pl.program_id(0) * stride
     depth = ts_ref.shape[-1]
     nq = ts_ref.shape[1]
     rows = lax.broadcasted_iota(jnp.int32, (depth, depth), 0)
@@ -41,7 +48,7 @@
     nr = npl * nt
     rchunk = RCHUNK
 
-    @pl.when(i == 0)
+    @pl.when(first_step)
     def _():
         a = lax.broadcasted_iota(jnp.int32, (nr * YT, nr), 0)
         r = lax.broadcasted_iota(jnp.int32, (nr * YT, nr), 1)
@@ -82,11 +89,14 @@
             rhs = jnp.concatenate([src[tr_ref[t], 0] for t in ts_], axis=0)
             return acc + jnp.dot(lhs, rhs, preferred_element_type=jnp.float32)
         acc = lax.fori_loop(0, nt // RG, step, jnp.zeros((depth, depth), jnp.float32),
-                            unroll=max(1, UNROLL * 2 // RG))
+                            unroll=RUNROLL)
         keep = row_ok & (cols < outlim_ref[i * npl + p])
         out_ref[0, p] = jnp.where(keep, acc, 0.0).astype(out_ref.dtype)
 
     for p, rloc in enumerate(() if "noright" in VARIANT else (rloc0_ref, rloc1_ref)):
+        if not halo:
+            right_sum(p, rloc)
+            continue
         j = i + sloc_ref[p]
 
         @pl.when(j < 0)
@@ -177,12 +187,19 @@
 
     lo, hi = halos(right_env, "blk", 1, SH)
 
-    return block_call(tl, tr, rowlim, collim.reshape(-1), outlim.reshape(-1), sloc,
-                      two_site, left_env, mq, right_env, lo, hi)
-
-
-def block_call(tl, tr, rowlim, collim, outlim, sloc, two_site, left_env, mq, right_env, lo, hi):
+    scalars = (tl, tr, rowlim, collim.reshape(-1), outlim.reshape(-1), sloc)
+    inner = block_call(*scalars, two_site, left_env, mq, right_env, None, None, None)
+    return block_call(*scalars, two_site, left_env, mq, right_env, lo, hi, inner)
+
+
+def block_call(tl, tr, rowlim, collim, outlim, sloc, two_site, left_env, mq, right_env,
+               lo, hi, prev):
     blocks, nq, depth, _ = two_site.shape
+    halo = prev is not None
+    if halo:
+        base, stride, steps = 0, blocks - 1, 2
+    else:
+        base, stride, steps = 1, 1, blocks - 2
     width = left_env.shape[0]
     npl = sloc.shape[0]
     nt = tl.shape[0]
@@ -190,23 +207,30 @@
 
     def rloc_map(p):
         def index(b, tl_r, tr_r, rl, cl, ol, sl):
-            return (0, jnp.clip(b + sl[p], 0, blocks - 1), 0, 0)
+            return (0, jnp.clip(base + b * stride + sl[p], 0, blocks - 1), 0, 0)
         return index
 
     const4 = lambda b, *refs: (0, 0, 0, 0)
+    in_specs = [
+        pl.BlockSpec((1, nq, depth, depth), lambda b, *refs: (base + b * stride, 0, 0, 0)),
+        pl.BlockSpec(rblock, lambda b, *refs: (0, base + b * stride, 0, 0)),
+        pl.BlockSpec(mq.shape, lambda b, *refs: (0, 0)),
+        pl.BlockSpec(rblock, rloc_map(0)),
+        pl.BlockSpec(rblock, rloc_map(1)),
+    ]
+    operands = [two_site, left_env, mq, right_env, right_env]
+    aliases = {}
+    if halo:
+        in_specs += [pl.BlockSpec(rblock, const4), pl.BlockSpec(rblock, const4),
+                     pl.BlockSpec(memory_space=pl.ANY)]
+        operands += [lo, hi, prev]
+        aliases = {6 + len(operands) - 1: 0}
     grid_spec = pltpu.PrefetchScalarGridSpec(
         num_scalar_prefetch=6,
-        grid=(blocks,),
-        in_specs=[
-            pl.BlockSpec((1, nq, depth, depth), lambda b, *refs: (b, 0, 0, 0)),
-            pl.BlockSpec(rblock, lambda b, *refs: (0, b, 0, 0)),
-            pl.BlockSpec(mq.shape, lambda b, *refs: (0, 0)),
-            pl.BlockSpec(rblock, rloc_map(0)),
-            pl.BlockSpec(rblock, rloc_map(1)),
-            pl.BlockSpec(rblock, const4),
-            pl.BlockSpec(rblock, const4),
-        ],
-        out_specs=pl.BlockSpec((1, npl, depth, depth), lambda b, *refs: (b, 0, 0, 0)),
+        grid=(steps,),
+        in_specs=in_specs,
+        out_specs=pl.BlockSpec((1, npl, depth, depth),
+                               lambda b, *refs: (base + b * stride, 0, 0, 0)),
         scratch_shapes=[
             pltpu.VMEM((nq, depth, depth), jnp.bfloat16),
             pltpu.VMEM((nt * npl, depth, depth), jnp.bfloat16),
@@ -214,18 +238,19 @@
             pltpu.VMEM((nt * npl * YT, nq * YT), jnp.bfloat16),
         ],
     )
-    flops = 2 * blocks * (nt * npl * YT * nq * YT * depth + 2 * nt * npl * depth ** 3)
+    flops = 2 * steps * (nt * npl * YT * nq * YT * depth + 2 * nt * npl * depth ** 3)
     return pl.pallas_call(
-        functools.partial(kernel, npl, nt),
+        functools.partial(kernel, npl, nt, base, stride, blocks, halo),
         out_shape=jax.ShapeDtypeStruct((blocks, npl, depth, depth), jnp.bfloat16),
         grid_spec=grid_spec,
         compiler_params=pltpu.CompilerParams(
             dimension_semantics=("arbitrary",), vmem_limit_bytes=60 * 1024 * 1024),
         cost_estimate=pl.CostEstimate(
             flops=flops, transcendentals=0,
-            bytes_accessed=2 * (two_site.size + left_env.size + 3 * right_env.size)),
-    )(tl, tr, rowlim, collim, outlim, sloc,
-      two_site, left_env, mq, right_env, right_env, lo, hi)
+            bytes_accessed=2 * steps * (two_site.size + left_env.size + 3 * right_env.size)
+            // blocks),
+        input_output_aliases=aliases,
+    )(tl, tr, rowlim, collim, outlim, sloc, *operands)
 
 
 def solution(mesh):

time: 80.4 us -> 73.7 us (0.917); the launches traced: 78.8 us -> 73.5 us
  waiting for transfers between devices: 9.23 us -> 0.01 us
  Pallas kernels: 48.8 us -> 51.2 us
  local copies, waits for them, and re-layouts: 8.59 us -> 10.8 us
  other arithmetic: 2.46 us -> 1.61 us
    ppermute x1, waiting for transfers between devices: 6.01 us -> 0.01 us  [halos(): lo = lax.ppermute(tail, axis, [(i, i + 1) for i in range(ends)])]
    ppermute x1, waiting for transfers between devices: 3.22 us -> 0.01 us  [halos(): hi = lax.ppermute(head, axis, [(i + 1, i) for i in range(ends)])]
    pallas_call x1 -> x2, Pallas kernels: 40.1 us -> 42.6 us  [block_call(): pl.pallas_call(functools.partial(kernel, npl, nt, base, stride, blocks, h...]
    unnamed x12 -> x16, local copies, waits for them, and re-layouts: 0.02 us -> 2.05 us
    ppermute x1, starting transfers between devices: 7.75 us -> 6.12 us  [halos(): hi = lax.ppermute(head, axis, [(i + 1, i) for i in range(ends)])]
    ppermute x1, starting transfers between devices: 1.92 us -> 3.53 us  [halos(): lo = lax.ppermute(tail, axis, [(i, i + 1) for i in range(ends)])]
    slice x1, local copies, waits for them, and re-layouts: 1.78 us -> 2.84 us  [halos(): head = lax.slice_in_dim(cells, 0, width, axis=dim)]
    convert_element_type x1, other arithmetic: 1.6 us -> 0.75 us  [body(): tr = packed[:, nq * nq + 1].astype(jnp.int32)]
  transfers between devices with their start and end apart: 2 -> 2, of which waited for: 2 -> 0; matrix products, arithmetic and copies ran while one was open for 12% -> 10% of each run, Pallas kernels for 11% -> 52%
where the time goes in v5:
time: 73.7 us; the launch traced here: 73.5 us
  Pallas kernels  51.2 us (69%)
  local copies, waits for them, and re-layouts  10.8 us (15%)
  starting transfers between devices  9.66 us (13%)
  other arithmetic  1.61 us (2%)
    pallas_call x2, Pallas kernels, block_call(): pl.pallas_call(functools.partial(kernel, npl, nt, base, stride, blocks, h...  42.6 us
    pallas_call x1, Pallas kernels, gather_terms(): pl.pallas_call(functools.partial(gather_kernel, nm), out_shape=jax.ShapeD...  8.61 us
    ppermute x1, starting transfers between devices, halos(): hi = lax.ppermute(head, axis, [(i + 1, i) for i in range(ends)])  6.12 us
    ppermute x1, starting transfers between devices, halos(): lo = lax.ppermute(tail, axis, [(i, i + 1) for i in range(ends)])  3.53 us
    slice x1, local copies, waits for them, and re-layouts, halos(): head = lax.slice_in_dim(cells, 0, width, axis=dim)  2.84 us
    unnamed x16, local copies, waits for them, and re-layouts  2.05 us
  transfers between devices with their start and end apart: 2, of which 0 were waited for; matrix products, arithmetic and copies ran while one was open for 10% of the time, Pallas kernels for 52%

profile of v5, /device:TPU:7, one launch (start us, length us, event | category | flops | bytes accessed | tf_op | source)
XLA Modules:
  0.0 73.5 jit_solution(11262320248902600180)
XLA Ops:
  0.0 0.0 copy-start
  0.0 0.0 copy-start.6
  0.0 0.0 copy-start.7
  0.0 0.0 copy-start.4
  0.0 0.0 copy-start.5
  0.0 2.8 %fusion.5 = (bf16[34,1,128,128]{3,2,1,0:T(8,128)(2,1)S(1)}, bf16[34,1,128,128]{3,2,1,0:T(8,128)(2,1)}) fusion(bf16[34,8,128,128]{3,2,1,0:T(8,128)(2,1)} %refs_10_.3), kind=kLoop, calls=%fused_computation.22 | loop fusion | bytes 4456448 | tf_op jit(solution)/shard_map/slice | solution.py:154
  2.9 3.5 %collective-permute-start = (bf16[34,1,128,128]{3,2,1,0:T(8,128)(2,1)}, bf16[34,1,128,128]{3,2,1,0:T(8,128)(2,1)S(1)}, u32[]{:S(2)}, u32[]{:S(2)}) collective-permute-start(bf16[34,1,128,128]{3,2,1,0:T(8,128)(2,1)} %get-tuple-element.8), channel_id=1, source_target_pairs={{0,1},{1,2},{2,3},{3,4},{4,5},{5,6},{6,7},{7,8},{8,9},{9,10},{10,1... | collective-permute-start | bytes 3342344 | tf_op jit(solution)/shard_map/ppermute | solution.py:156
  6.4 6.1 %collective-permute-start.1 = (bf16[34,1,128,128]{3,2,1,0:T(8,128)(2,1)S(1)}, bf16[34,1,128,128]{3,2,1,0:T(8,128)(2,1)S(1)}, u32[]{:S(2)}, u32[]{:S(2)}) collective-permute-start(bf16[34,1,128,128]{3,2,1,0:T(8,128)(2,1)S(1)} %get-tuple-element.7), channel_id=1, source_target_pairs={{1,0},{2,1},{3,2},{4,3},{5,4},{6,5},{7,6},{8,7},{9,8},{10,9},{11,1... | collective-permute-start | bytes 3342344 | tf_op jit(solution)/shard_map/ppermute | solution.py:157
  12.6 0.0 copy-done.6
  12.6 0.1 copy.38
  12.7 0.0 copy-done.7
  12.7 0.1 copy.37
  12.8 0.0 copy-done.4
  12.8 0.1 reshape.104
  12.9 0.7 maximum_convert_fusion.x_ref
  13.6 8.6 %shard_map.82 = f32[8,8,258]{2,1,0:T(8,128)} custom-call(f32[8,258]{1,0:T(8,128)} %maximum_convert_fusion.x_ref), custom_call_target="tpu_custom_call" | custom-call | tf_op jit(solution)/shard_map/pallas_call | solution.py:141
  22.2 0.0 copy-done.5
  22.2 0.1 compare_select_fusion
  22.3 0.1 reshape.119
  22.4 0.0 copy-done
  22.4 0.0 copy-start.3
  22.4 1.3 %gather_fusion.1 = s32[128]{0:T(128)S(1)} fusion(s32[256]{0:T(256)S(1)} %copy-done, s32[1024]{0:T(1024)S(1)} %pad_clamp_fusion), kind=kCustom, calls=%fused_computation.1 | custom fusion | bytes 1536 | tf_op jit(solution)/shard_map/gather | solution.py:24
  23.7 0.1 reshape.118
  23.7 0.1 fusion.3
  23.8 1.2 %gather_fusion = s32[8]{0:T(128)} fusion(s32[256]{0:T(256)S(1)} %copy-done, s32[1024]{0:T(1024)S(1)} %pad_clamp_fusion.1), kind=kCustom, calls=%fused_computation | custom fusion | bytes 96 | tf_op jit(solution)/shard_map/gather | solution.py:23
  25.0 0.7 select_n.36.refs_3_
  25.6 0.6 dynamic_slice.10.refs_5_
  26.3 0.1 constant_dynamic-slice_fusion.1
  26.4 0.6 reshape.106.refs_4_
  26.9 0.0 copy-done.3
  27.0 0.1 copy.39
  27.1 0.1 copy.40
  27.2 0.1 copy.41
  27.3 0.7 %copy.43.refs_8_ = bf16[128,256]{1,0:T(8,128)(2,1)} copy(bf16[128,256]{0,1:T(8,128)(2,1)S(1)} %bitcast.14) | data formatting | bytes 131072 | tf_op jit(solution)/shard_map/reshape | solution.py:186
  28.0 0.8 %fusion = (s32[64]{0:T(128)}, s32[64]{0:T(128)}) fusion(f32[64,258]{1,0:T(8,128)S(1)} %bitcast.13), kind=kLoop, calls=%fused_computation.4 | loop fusion | flops 128 | bytes 1024 | tf_op jit(solution)/shard_map/convert_element_type | solution.py:179
  28.8 29.3 %shard_map.83.refs_13_ = bf16[8,2,128,128]{3,2,1,0:T(8,128)(2,1)} custom-call(s32[64]{0:T(128)} %get-tuple-element.6.refs_0_, s32[64]{0:T(128)} %get-tuple-element.5.refs_1_, s32[8]{0:T(128)} %gather_fusion, s32[128]{0:T(128)} %select_n.36.refs_3_, s32[16]{0:T(128)} %reshape.106.refs_4_, s32[2]{0:T(128)} %dynamic_slice.10.refs_5_, ...), custom_call_target="tpu_custom_call" | custom-call | flops 7247757312 | bytes 29884416 | tf_op jit(solution)/shard_map/pallas_call | solution.py:242
  58.1 0.0 collective-permute-done.refs_11_
  58.1 0.0 copy-start.1
  58.1 0.0 collective-permute-done.1.refs_12_
  58.1 1.0 %copy-done.1 = bf16[34,1,128,128]{3,2,1,0:T(8,128)(2,1)} copy-done((bf16[34,1,128,128]{3,2,1,0:T(8,128)(2,1)}, bf16[34,1,128,128]{3,2,1,0:T(8,128)(2,1)S(1)}, u32[]{:S(2)}) %copy-start.1) | copy-done | bytes 1114136
  59.1 0.0 copy-start.2
  59.1 1.0 %copy-done.2 = bf16[34,1,128,128]{3,2,1,0:T(8,128)(2,1)} copy-done((bf16[34,1,128,128]{3,2,1,0:T(8,128)(2,1)}, bf16[34,1,128,128]{3,2,1,0:T(8,128)(2,1)S(1)}, u32[]{:S(2)}) %copy-start.2) | copy-done | bytes 1114136
  60.1 13.4 %shard_map.84 = bf16[8,2,128,128]{3,2,1,0:T(8,128)(2,1)} custom-call(s32[64]{0:T(128)} %get-tuple-element.6.refs_0_, s32[64]{0:T(128)} %get-tuple-element.5.refs_1_, s32[8]{0:T(128)} %gather_fusion, s32[128]{0:T(128)} %select_n.36.refs_3_, s32[16]{0:T(128)} %reshape.106.refs_4_, s32[2]{0:T(128)} %dynamic_slice.10.refs_5_, ...), custom_call_target="tpu_custom_call", output_to_operand_aliasing={{}: (13, {})} | custom-call | flops 2415919104 | bytes 9961472 | tf_op jit(solution)/shard_map/pallas_call | solution.py:242
  (9 shorter events, 0.1 us)
Async XLA Ops:
  0.0 22.4 %copy-start = (s32[256]{0:T(256)S(1)}, s32[256]{0:T(256)}, u32[]{:S(2)}) copy-start(s32[256]{0:T(256)} %param.15) | copy-start | bytes 3076
  0.0 12.6 %copy-start.6 = (s32[8]{0:T(128)S(1)}, s32[8]{0:T(128)}, u32[]{:S(2)}) copy-start(s32[8]{0:T(128)} %param.13) | copy-start | bytes 100
  0.0 12.7 %copy-start.7 = (s32[8]{0:T(128)S(1)}, s32[8]{0:T(128)}, u32[]{:S(2)}) copy-start(s32[8]{0:T(128)} %param.12) | copy-start | bytes 100
  0.0 12.8 %copy-start.4 = (bf16[8,16,16]{2,1,0:T(8,128)(2,1)S(1)}, bf16[8,16,16]{2,1,0:T(8,128)(2,1)}, u32[]{:S(2)}) copy-start(bf16[8,16,16]{2,1,0:T(8,128)(2,1)} %param.11) | copy-start | bytes 12292
  0.0 22.2 %copy-start.5 = (s32[16]{0:T(128)S(1)}, s32[16]{0:T(128)}, u32[]{:S(2)}) copy-start(s32[16]{0:T(128)} %param.14) | copy-start | bytes 196
  2.9 55.2 %collective-permute-start = (bf16[34,1,128,128]{3,2,1,0:T(8,128)(2,1)}, bf16[34,1,128,128]{3,2,1,0:T(8,128)(2,1)S(1)}, u32[]{:S(2)}, u32[]{:S(2)}) collective-permute-start(bf16[34,1,128,128]{3,2,1,0:T(8,128)(2,1)} %get-tuple-element.8), channel_id=1, source_target_pairs={{0,1},{1,2},{2,3},{3,4},{4,5},{5,6},{6,7},{7,8},{8,9},{9,10},{10,1... | collective-permute-start | bytes 3342344 | tf_op jit(solution)/shard_map/ppermute | solution.py:156
  6.4 51.6 %collective-permute-start.1 = (bf16[34,1,128,128]{3,2,1,0:T(8,128)(2,1)S(1)}, bf16[34,1,128,128]{3,2,1,0:T(8,128)(2,1)S(1)}, u32[]{:S(2)}, u32[]{:S(2)}) collective-permute-start(bf16[34,1,128,128]{3,2,1,0:T(8,128)(2,1)S(1)} %get-tuple-element.7), channel_id=1, source_target_pairs={{1,0},{2,1},{3,2},{4,3},{5,4},{6,5},{7,6},{8,7},{9,8},{10,9},{11,1... | collective-permute-start | bytes 3342344 | tf_op jit(solution)/shard_map/ppermute | solution.py:157
  22.4 4.6 %copy-start.3 = (f32[8,8,258]{2,1,0:T(8,128)S(1)}, f32[8,8,258]{2,1,0:T(8,128)}, u32[]{:S(2)}) copy-start(f32[8,8,258]{2,1,0:T(8,128)} %shard_map.82) | copy-start | bytes 198148
  58.1 1.0 %copy-start.1 = (bf16[34,1,128,128]{3,2,1,0:T(8,128)(2,1)}, bf16[34,1,128,128]{3,2,1,0:T(8,128)(2,1)S(1)}, u32[]{:S(2)}) copy-start(bf16[34,1,128,128]{3,2,1,0:T(8,128)(2,1)S(1)} %collective-permute-done.refs_11_) | copy-start | bytes 3342340
  59.1 1.0 %copy-start.2 = (bf16[34,1,128,128]{3,2,1,0:T(8,128)(2,1)}, bf16[34,1,128,128]{3,2,1,0:T(8,128)(2,1)S(1)}, u32[]{:S(2)}) copy-start(bf16[34,1,128,128]{3,2,1,0:T(8,128)(2,1)S(1)} %collective-permute-done.1.refs_12_) | copy-start | bytes 3342340

commit v6 on v5

--- a/solution.py
+++ b/solution.py
@@ -16,33 +16,32 @@
 RCHUNK = 64
 
 
-def sector_limits(block_sizes, shifts, first, blocks, total):
-    rows_left = first + jnp.arange(blocks, dtype=jnp.int32)
-    right_index = rows_left[:, None] + shifts[None, :]
-    inside = (right_index >= 0) & (right_index < total)
-    size_left = block_sizes[rows_left]
-    size_right = jnp.where(inside, block_sizes[jnp.clip(right_index, 0, total - 1)], 0)
-    return size_left.astype(jnp.int32), size_right.astype(jnp.int32)
-
-
-def kernel(npl, nt, base, stride, nb, halo, *refs):
-    (tl_ref, tr_ref, rowlim_ref, collim_ref, outlim_ref, sloc_ref,
-     ts_ref, left_ref, mq_ref, rloc0_ref, rloc1_ref) = refs[:11]
+def kernel(npl, nt, base, stride, nb, total, halo, *refs):
+    (tl_ref, tr_ref, bs_ref, sh_ref, ids_ref,
+     ts_ref, left_ref, mq_ref, rloc0_ref, rloc1_ref) = refs[:10]
     if halo:
-        lo_ref, hi_ref = refs[11:13]
-        refs = refs[14:]
+        lo_ref, hi_ref = refs[10:12]
+        refs = refs[13:]
     else:
-        refs = refs[11:]
+        refs = refs[10:]
     out_ref, c_scr, x_scr, y_scr, kron_scr = refs
     first_step = pl.program_id(0) == 0
     i = base + pl.program_id(0) * stride
+    gi = ids_ref[0] + i
+
+    def size_at(shift):
+        j = gi + shift
+        inside = (j >= 0) & (j < total)
+        return jnp.where(inside, bs_ref[jnp.clip(j, 0, total - 1)], 0)
+
+    sloc = [sh_ref[ids_ref[1] + p] for p in range(npl)]
     depth = ts_ref.shape[-1]
     nq = ts_ref.shape[1]
     rows = lax.broadcasted_iota(jnp.int32, (depth, depth), 0)
     cols = lax.broadcasted_iota(jnp.int32, (depth, depth), 1)
-    row_ok = rows < rowlim_ref[i]
+    row_ok = rows < bs_ref[gi]
     for q in range(nq):
-        keep = row_ok & (cols < collim_ref[i * nq + q])
+        keep = row_ok & (cols < size_at(sh_ref[q]))
         c_scr[q] = jnp.where(keep, ts_ref[0, q], jnp.zeros_like(ts_ref[0, q]))
 
     nr = npl * nt
@@ -90,14 +89,14 @@
             return acc + jnp.dot(lhs, rhs, preferred_element_type=jnp.float32)
         acc = lax.fori_loop(0, nt // RG, step, jnp.zeros((depth, depth), jnp.float32),
                             unroll=RUNROLL)
-        keep = row_ok & (cols < outlim_ref[i * npl + p])
+        keep = row_ok & (cols < size_at(sloc[p]))
         out_ref[0, p] = jnp.where(keep, acc, 0.0).astype(out_ref.dtype)
 
     for p, rloc in enumerate(() if "noright" in VARIANT else (rloc0_ref, rloc1_ref)):
         if not halo:
             right_sum(p, rloc)
             continue
-        j = i + sloc_ref[p]
+        j = i + sloc[p]
 
         @pl.when(j < 0)
         def _():
@@ -178,36 +177,34 @@
     tl = packed[:, nq * nq].astype(jnp.int32)
     tr = packed[:, nq * nq + 1].astype(jnp.int32)
 
-    rowlim, collim = sector_limits(block_sizes, shifts, first, blocks, total)
-    outlim = lax.dynamic_slice_in_dim(collim, p_first, npl, axis=1)
-    sloc = lax.dynamic_slice_in_dim(shifts, p_first, npl)
+    ids = jnp.stack([first, p_first]).astype(jnp.int32)
 
     mine = lax.dynamic_slice_in_dim(terms, p_first, npl, axis=1).reshape(nt * npl, nq)
     mq = jnp.repeat(mine, YT, axis=1)
 
     lo, hi = halos(right_env, "blk", 1, SH)
 
-    scalars = (tl, tr, rowlim, collim.reshape(-1), outlim.reshape(-1), sloc)
-    inner = block_call(*scalars, two_site, left_env, mq, right_env, None, None, None)
-    return block_call(*scalars, two_site, left_env, mq, right_env, lo, hi, inner)
-
-
-def block_call(tl, tr, rowlim, collim, outlim, sloc, two_site, left_env, mq, right_env,
-               lo, hi, prev):
+    scalars = (tl, tr, block_sizes, shifts, ids)
+    inner = block_call(*scalars, two_site, left_env, mq, right_env, None, None, None, npl=npl)
+    return block_call(*scalars, two_site, left_env, mq, right_env, lo, hi, inner, npl=npl)
+
+
+def block_call(tl, tr, block_sizes, shifts, ids, two_site, left_env, mq, right_env,
+               lo, hi, prev, npl):
     blocks, nq, depth, _ = two_site.shape
+    total = block_sizes.shape[0]
     halo = prev is not None
     if halo:
         base, stride, steps = 0, blocks - 1, 2
     else:
         base, stride, steps = 1, 1, blocks - 2
     width = left_env.shape[0]
-    npl = sloc.shape[0]
     nt = tl.shape[0]
     rblock = (width, 1, depth, depth)
 
     def rloc_map(p):
-        def index(b, tl_r, tr_r, rl, cl, ol, sl):
-            return (0, jnp.clip(base + b * stride + sl[p], 0, blocks - 1), 0, 0)
+        def index(b, tl_r, tr_r, bs_r, sh_r, ids_r):
+            return (0, jnp.clip(base + b * stride + sh_r[ids_r[1] + p], 0, blocks - 1), 0, 0)
         return index
 
     const4 = lambda b, *refs: (0, 0, 0, 0)
@@ -224,9 +221,9 @@
         in_specs += [pl.BlockSpec(rblock, const4), pl.BlockSpec(rblock, const4),
                      pl.BlockSpec(memory_space=pl.ANY)]
         operands += [lo, hi, prev]
-        aliases = {6 + len(operands) - 1: 0}
+        aliases = {5 + len(operands) - 1: 0}
     grid_spec = pltpu.PrefetchScalarGridSpec(
-        num_scalar_prefetch=6,
+        num_scalar_prefetch=5,
         grid=(steps,),
         in_specs=in_specs,
         out_specs=pl.BlockSpec((1, npl, depth, depth),
@@ -240,7 +237,7 @@
     )
     flops = 2 * steps * (nt * npl * YT * nq * YT * depth + 2 * nt * npl * depth ** 3)
     return pl.pallas_call(
-        functools.partial(kernel, npl, nt, base, stride, blocks, halo),
+        functools.partial(kernel, npl, nt, base, stride, blocks, total, halo),
         out_shape=jax.ShapeDtypeStruct((blocks, npl, depth, depth), jnp.bfloat16),
         grid_spec=grid_spec,
         compiler_params=pltpu.CompilerParams(
@@ -250,7 +247,7 @@
             bytes_accessed=2 * steps * (two_site.size + left_env.size + 3 * right_env.size)
             // blocks),
         input_output_aliases=aliases,
-    )(tl, tr, rowlim, collim, outlim, sloc, *operands)
+    )(tl, tr, block_sizes, shifts, ids, *operands)
 
 
 def solution(mesh):

time: 73.7 us -> 71.4 us (0.969)
  local copies, waits for them, and re-layouts: 10.8 us -> 7.03 us
  other arithmetic: 1.61 us -> 2.88 us
    gather x3 -> x0, local copies, waits for them, and re-layouts: 2.5 us -> none  [the longest x2 1.34 us: sector_limits(): block_sizes[jnp.clip(right_index, 0, total - 1)]]
    convert_element_type x1, other arithmetic: 0.75 us -> 1.61 us  [body(): tr = packed[:, nq * nq + 1].astype(jnp.int32)]
    slice x2, local copies, waits for them, and re-layouts: 0.12 us -> 0.96 us  [body(): terms = packed[:, :nq * nq].reshape(nt, nq, nq).astype(mpo_terms.dtype)]
    select_n x2 -> x0, local copies, waits for them, and re-layouts: 0.74 us -> none  [the longest x1 0.66 us: sector_limits(): jnp.where(inside, block_sizes[jnp.clip(right_index, 0, total - 1)], 0)]
    unnamed x16 -> x10, local copies, waits for them, and re-layouts: 2.05 us -> 2.01 us
  transfers between devices with their start and end apart: 2 -> 2, of which waited for: 0 -> 0; matrix products, arithmetic and copies ran while one was open for 10% -> 7% of each run, Pallas kernels for 52% -> 53%
where the time goes in v6:
time: 71.4 us; the launch traced here: 71 us
  Pallas kernels  51.4 us (72%)
  starting transfers between devices  9.66 us (14%)
  local copies, waits for them, and re-layouts  7.03 us (10%)
  other arithmetic  2.88 us (4%)
    pallas_call x2, Pallas kernels, block_call(): pl.pallas_call(functools.partial(kernel, npl, nt, base, stride, blocks, t...  42.8 us
    pallas_call x1, Pallas kernels, gather_terms(): pl.pallas_call(functools.partial(gather_kernel, nm), out_shape=jax.ShapeD...  8.59 us
    ppermute x1, starting transfers between devices, halos(): hi = lax.ppermute(head, axis, [(i + 1, i) for i in range(ends)])  6.12 us
    ppermute x1, starting transfers between devices, halos(): lo = lax.ppermute(tail, axis, [(i, i + 1) for i in range(ends)])  3.53 us
    slice x1, local copies, waits for them, and re-layouts, halos(): head = lax.slice_in_dim(cells, 0, width, axis=dim)  2.82 us
    unnamed x10, local copies, waits for them, and re-layouts  2.01 us
    convert_element_type x1, other arithmetic, body(): tr = packed[:, nq * nq + 1].astype(jnp.int32)  1.61 us
  transfers between devices with their start and end apart: 2, of which 0 were waited for; matrix products, arithmetic and copies ran while one was open for 7% of the time, Pallas kernels for 53%

profile of v6, /device:TPU:7, one launch (start us, length us, event | category | flops | bytes accessed | tf_op | source)
XLA Modules:
  0.0 71.0 jit_solution(17563224669961146367)
XLA Ops:
  0.0 0.0 copy-start.3
  0.0 0.0 copy-start.4
  0.0 0.0 copy-start.2
  0.0 2.8 %fusion.2 = (bf16[34,1,128,128]{3,2,1,0:T(8,128)(2,1)S(1)}, bf16[34,1,128,128]{3,2,1,0:T(8,128)(2,1)}) fusion(bf16[34,8,128,128]{3,2,1,0:T(8,128)(2,1)} %refs_9_.3), kind=kLoop, calls=%fused_computation.10 | loop fusion | bytes 4456448 | tf_op jit(solution)/shard_map/slice | solution.py:153
  2.8 3.5 %collective-permute-start = (bf16[34,1,128,128]{3,2,1,0:T(8,128)(2,1)}, bf16[34,1,128,128]{3,2,1,0:T(8,128)(2,1)S(1)}, u32[]{:S(2)}, u32[]{:S(2)}) collective-permute-start(bf16[34,1,128,128]{3,2,1,0:T(8,128)(2,1)} %get-tuple-element.8), channel_id=1, source_target_pairs={{0,1},{1,2},{2,3},{3,4},{4,5},{5,6},{6,7},{7,8},{8,9},{9,10},{10,1... | collective-permute-start | bytes 3342344 | tf_op jit(solution)/shard_map/ppermute | solution.py:155
  6.4 6.1 %collective-permute-start.1 = (bf16[34,1,128,128]{3,2,1,0:T(8,128)(2,1)S(1)}, bf16[34,1,128,128]{3,2,1,0:T(8,128)(2,1)S(1)}, u32[]{:S(2)}, u32[]{:S(2)}) collective-permute-start(bf16[34,1,128,128]{3,2,1,0:T(8,128)(2,1)S(1)} %get-tuple-element.7), channel_id=1, source_target_pairs={{1,0},{2,1},{3,2},{4,3},{5,4},{6,5},{7,6},{8,7},{9,8},{10,9},{11,1... | collective-permute-start | bytes 3342344 | tf_op jit(solution)/shard_map/ppermute | solution.py:156
  12.5 0.0 copy-done.3
  12.5 0.1 copy.38
  12.6 0.0 copy-done.4
  12.6 0.1 copy.37
  12.7 0.0 copy-done.2
  12.7 0.1 reshape.18
  12.8 0.7 maximum_convert_fusion.x_ref
  13.5 8.6 %shard_map.82 = f32[8,8,258]{2,1,0:T(8,128)} custom-call(f32[8,258]{1,0:T(8,128)} %maximum_convert_fusion.x_ref), custom_call_target="tpu_custom_call" | custom-call | tf_op jit(solution)/shard_map/pallas_call | solution.py:140
  22.1 0.8 %slice.31 = bf16[64,256]{1,0:T(8,128)(2,1)S(1)} slice(f32[64,258]{1,0:T(8,128)} %bitcast.10), slice={[0:64], [0:256]} | slice | bytes 65536 | tf_op jit(solution)/shard_map/slice | solution.py:176
  23.0 0.1 copy.39
  23.1 0.1 copy.40
  23.2 0.1 copy.41
  23.3 0.7 %copy.43.refs_7_ = bf16[128,256]{1,0:T(8,128)(2,1)} copy(bf16[128,256]{0,1:T(8,128)(2,1)S(1)} %bitcast.12) | data formatting | bytes 131072 | tf_op jit(solution)/shard_map/reshape | solution.py:183
  24.0 0.6 pad_add_fusion.refs_4_
  24.6 1.6 %fusion = (s32[64]{0:T(128)}, s32[64]{0:T(128)}) fusion(f32[64,258]{1,0:T(8,128)} %bitcast.11), kind=kLoop, calls=%fused_computation.2 | loop fusion | flops 128 | bytes 1024 | tf_op jit(solution)/shard_map/convert_element_type | solution.py:178
  26.2 29.4 %shard_map.83.refs_12_ = bf16[8,2,128,128]{3,2,1,0:T(8,128)(2,1)} custom-call(s32[64]{0:T(128)} %get-tuple-element.6.refs_0_, s32[64]{0:T(128)} %get-tuple-element.5.refs_1_, s32[256]{0:T(256)} %refs_2_.3, s32[16]{0:T(128)} %refs_3_.3, s32[2]{0:T(128)} %pad_add_fusion.refs_4_, bf16[8,16,128,128]{3,2,1,0:T(8,128)(2,1)} %refs_5_.3, ...), custom_call_target="tpu_custom_call" | custom-call | flops 7247757312 | bytes 29884416 | tf_op jit(solution)/shard_map/pallas_call | solution.py:239
  55.6 0.0 collective-permute-done.refs_10_
  55.6 0.0 copy-start
  55.6 0.0 collective-permute-done.1.refs_11_
  55.6 1.0 %copy-done = bf16[34,1,128,128]{3,2,1,0:T(8,128)(2,1)} copy-done((bf16[34,1,128,128]{3,2,1,0:T(8,128)(2,1)}, bf16[34,1,128,128]{3,2,1,0:T(8,128)(2,1)S(1)}, u32[]{:S(2)}) %copy-start) | copy-done | bytes 1114136
  56.6 0.0 copy-start.1
  56.6 1.0 %copy-done.1 = bf16[34,1,128,128]{3,2,1,0:T(8,128)(2,1)} copy-done((bf16[34,1,128,128]{3,2,1,0:T(8,128)(2,1)}, bf16[34,1,128,128]{3,2,1,0:T(8,128)(2,1)S(1)}, u32[]{:S(2)}) %copy-start.1) | copy-done | bytes 1114136
  57.6 13.4 %shard_map.84 = bf16[8,2,128,128]{3,2,1,0:T(8,128)(2,1)} custom-call(s32[64]{0:T(128)} %get-tuple-element.6.refs_0_, s32[64]{0:T(128)} %get-tuple-element.5.refs_1_, s32[256]{0:T(256)} %refs_2_.3, s32[16]{0:T(128)} %refs_3_.3, s32[2]{0:T(128)} %pad_add_fusion.refs_4_, bf16[8,16,128,128]{3,2,1,0:T(8,128)(2,1)} %refs_5_.3, ...), custom_call_target="tpu_custom_call", output_to_operand_aliasing={{}: (12, {})} | custom-call | flops 2415919104 | bytes 9961472 | tf_op jit(solution)/shard_map/pallas_call | solution.py:239
  (4 shorter events, 0.1 us)
Async XLA Ops:
  0.0 12.5 %copy-start.3 = (s32[8]{0:T(128)S(1)}, s32[8]{0:T(128)}, u32[]{:S(2)}) copy-start(s32[8]{0:T(128)} %param.13) | copy-start | bytes 100
  0.0 12.6 %copy-start.4 = (s32[8]{0:T(128)S(1)}, s32[8]{0:T(128)}, u32[]{:S(2)}) copy-start(s32[8]{0:T(128)} %param.12) | copy-start | bytes 100
  0.0 12.7 %copy-start.2 = (bf16[8,16,16]{2,1,0:T(8,128)(2,1)S(1)}, bf16[8,16,16]{2,1,0:T(8,128)(2,1)}, u32[]{:S(2)}) copy-start(bf16[8,16,16]{2,1,0:T(8,128)(2,1)} %param.11) | copy-start | bytes 12292
  2.8 52.8 %collective-permute-start = (bf16[34,1,128,128]{3,2,1,0:T(8,128)(2,1)}, bf16[34,1,128,128]{3,2,1,0:T(8,128)(2,1)S(1)}, u32[]{:S(2)}, u32[]{:S(2)}) collective-permute-start(bf16[34,1,128,128]{3,2,1,0:T(8,128)(2,1)} %get-tuple-element.8), channel_id=1, source_target_pairs={{0,1},{1,2},{2,3},{3,4},{4,5},{5,6},{6,7},{7,8},{8,9},{9,10},{10,1... | collective-permute-start | bytes 3342344 | tf_op jit(solution)/shard_map/ppermute | solution.py:155
  6.4 49.2 %collective-permute-start.1 = (bf16[34,1,128,128]{3,2,1,0:T(8,128)(2,1)S(1)}, bf16[34,1,128,128]{3,2,1,0:T(8,128)(2,1)S(1)}, u32[]{:S(2)}, u32[]{:S(2)}) collective-permute-start(bf16[34,1,128,128]{3,2,1,0:T(8,128)(2,1)S(1)} %get-tuple-element.7), channel_id=1, source_target_pairs={{1,0},{2,1},{3,2},{4,3},{5,4},{6,5},{7,6},{8,7},{9,8},{10,9},{11,1... | collective-permute-start | bytes 3342344 | tf_op jit(solution)/shard_map/ppermute | solution.py:156
  55.6 1.0 %copy-start = (bf16[34,1,128,128]{3,2,1,0:T(8,128)(2,1)}, bf16[34,1,128,128]{3,2,1,0:T(8,128)(2,1)S(1)}, u32[]{:S(2)}) copy-start(bf16[34,1,128,128]{3,2,1,0:T(8,128)(2,1)S(1)} %collective-permute-done.refs_10_) | copy-start | bytes 3342340
  56.6 1.0 %copy-start.1 = (bf16[34,1,128,128]{3,2,1,0:T(8,128)(2,1)}, bf16[34,1,128,128]{3,2,1,0:T(8,128)(2,1)S(1)}, u32[]{:S(2)}) copy-start(bf16[34,1,128,128]{3,2,1,0:T(8,128)(2,1)S(1)} %collective-permute-done.1.refs_11_) | copy-start | bytes 3342340

commit v7 on v6

--- a/solution.py
+++ b/solution.py
@@ -17,13 +17,16 @@
 
 
 def kernel(npl, nt, base, stride, nb, total, halo, *refs):
-    (tl_ref, tr_ref, bs_ref, sh_ref, ids_ref,
-     ts_ref, left_ref, mq_ref, rloc0_ref, rloc1_ref) = refs[:10]
+    (idx_ref, bs_ref, sh_ref, ids_ref,
+     ts_ref, left_ref, mq_ref, rloc0_ref, rloc1_ref) = refs[:9]
     if halo:
-        lo_ref, hi_ref = refs[10:12]
-        refs = refs[13:]
+        lo_ref, hi_ref = refs[9:11]
+        refs = refs[12:]
     else:
-        refs = refs[10:]
+        refs = refs[9:]
+    per = idx_ref.shape[2]
+    tl_of = lambda t: idx_ref[t // per, 0, t % per]
+    tr_of = lambda t: idx_ref[t // per, 1, t % per]
     out_ref, c_scr, x_scr, y_scr, kron_scr = refs
     first_step = pl.program_id(0) == 0
     i = base + pl.program_id(0) * stride
@@ -71,7 +74,7 @@
                     .reshape(rchunk, YT, depth).astype(x_scr.dtype))
 
     def left_step(t, carry):
-        lt = left_ref[tl_ref[t], 0]
+        lt = left_ref[tl_of(t), 0]
         xs = jnp.concatenate([x_scr[t * npl + p] for p in range(npl)], axis=1)
         yt = jnp.dot(lt, xs, preferred_element_type=jnp.float32).astype(y_scr.dtype)
         for p in range(npl):
@@ -85,7 +88,7 @@
         def step(u, acc):
             ts_ = [RG * u + g for g in range(RG)]
             lhs = jnp.concatenate([y_scr[p, t] for t in ts_], axis=1)
-            rhs = jnp.concatenate([src[tr_ref[t], 0] for t in ts_], axis=0)
+            rhs = jnp.concatenate([src[tr_of(t), 0] for t in ts_], axis=0)
             return acc + jnp.dot(lhs, rhs, preferred_element_type=jnp.float32)
         acc = lax.fori_loop(0, nt // RG, step, jnp.zeros((depth, depth), jnp.float32),
                             unroll=RUNROLL)
@@ -111,7 +114,8 @@
             right_sum(p, hi_ref)
 
 
-def gather_kernel(nm, x_ref, out_ref, send_sem, recv_sem):
+def gather_kernel(nm, x_ref, idx_ref, out_ref, idx_out_ref, send_sem, recv_sem,
+                  isend_sem, irecv_sem):
     me = lax.axis_index("mpo")
     barrier = pltpu.get_barrier_semaphore()
     for d in range(1, nm):
@@ -120,31 +124,37 @@
     pl.semaphore_wait(barrier, nm - 1)
     copies = []
     for d in range(1, nm):
-        copy = pltpu.make_async_remote_copy(
-            src_ref=x_ref,
-            dst_ref=out_ref.at[me],
-            send_sem=send_sem.at[d],
-            recv_sem=recv_sem.at[d],
-            device_id={"mpo": lax.rem(me + d, nm)},
-            device_id_type=pl.DeviceIdType.MESH,
-        )
-        copy.start()
-        copies.append(copy)
-    out_ref[me] = x_ref[...]
+        peer = lax.rem(me + d, nm)
+        for src, dst, ssem, rsem in ((x_ref.at[peer], out_ref.at[me], send_sem, recv_sem),
+                                     (idx_ref, idx_out_ref.at[me], isend_sem, irecv_sem)):
+            copy = pltpu.make_async_remote_copy(
+                src_ref=src,
+                dst_ref=dst,
+                send_sem=ssem.at[d],
+                recv_sem=rsem.at[d],
+                device_id={"mpo": peer},
+                device_id_type=pl.DeviceIdType.MESH,
+            )
+            copy.start()
+            copies.append(copy)
+    out_ref[me] = x_ref[me]
+    idx_out_ref[me] = idx_ref[...]
     for copy in copies:
         copy.wait()
 
 
-def gather_terms(packed):
+def gather_terms(rows, idx):
     nm = lax.axis_size("mpo")
+    sems = [pltpu.SemaphoreType.DMA((nm,)) for _ in range(4)]
     return pl.pallas_call(
         functools.partial(gather_kernel, nm),
-        out_shape=jax.ShapeDtypeStruct((nm,) + packed.shape, packed.dtype),
-        in_specs=[pl.BlockSpec(memory_space=pltpu.VMEM)],
-        out_specs=pl.BlockSpec(memory_space=pltpu.VMEM),
-        scratch_shapes=[pltpu.SemaphoreType.DMA((nm,)), pltpu.SemaphoreType.DMA((nm,))],
+        out_shape=(jax.ShapeDtypeStruct(rows.shape, rows.dtype),
+                   jax.ShapeDtypeStruct((nm,) + idx.shape, idx.dtype)),
+        in_specs=[pl.BlockSpec(memory_space=pltpu.VMEM)] * 2,
+        out_specs=(pl.BlockSpec(memory_space=pltpu.VMEM),) * 2,
+        scratch_shapes=sems,
         compiler_params=pltpu.CompilerParams(collective_id=0, has_side_effects=True),
-    )(packed).reshape(nm * packed.shape[0], packed.shape[1])
+    )(rows, idx)
 
 
 def halos(cells, axis, dim, width):
@@ -167,29 +177,22 @@
     p_first = lax.axis_index("mpo") * npl
 
     local_terms = mpo_terms.shape[0]
-    packed = jnp.concatenate(
-        [mpo_terms.reshape(local_terms, nq * nq),
-         term_left[:, None].astype(mpo_terms.dtype),
-         term_right[:, None].astype(mpo_terms.dtype)], axis=1).astype(jnp.float32)
-    packed = gather_terms(packed)
-    nt = packed.shape[0]
-    terms = packed[:, :nq * nq].reshape(nt, nq, nq).astype(mpo_terms.dtype)
-    tl = packed[:, nq * nq].astype(jnp.int32)
-    tr = packed[:, nq * nq + 1].astype(jnp.int32)
-
+    rows = mpo_terms.reshape(local_terms, nmpo, npl, nq).transpose(1, 0, 2, 3)
+    rows = jnp.repeat(rows.reshape(nmpo, local_terms * npl, nq), YT, axis=2)
+    idx = jnp.stack([term_left, term_right]).astype(jnp.int32)
+    mq, idx = gather_terms(rows, idx)
+    nt = nmpo * local_terms
+    mq = mq.reshape(nt * npl, nq * YT)
     ids = jnp.stack([first, p_first]).astype(jnp.int32)
 
-    mine = lax.dynamic_slice_in_dim(terms, p_first, npl, axis=1).reshape(nt * npl, nq)
-    mq = jnp.repeat(mine, YT, axis=1)
-
     lo, hi = halos(right_env, "blk", 1, SH)
 
-    scalars = (tl, tr, block_sizes, shifts, ids)
+    scalars = (idx, block_sizes, shifts, ids)
     inner = block_call(*scalars, two_site, left_env, mq, right_env, None, None, None, npl=npl)
     return block_call(*scalars, two_site, left_env, mq, right_env, lo, hi, inner, npl=npl)
 
 
-def block_call(tl, tr, block_sizes, shifts, ids, two_site, left_env, mq, right_env,
+def block_call(idx, block_sizes, shifts, ids, two_site, left_env, mq, right_env,
                lo, hi, prev, npl):
     blocks, nq, depth, _ = two_site.shape
     total = block_sizes.shape[0]
@@ -199,11 +202,11 @@
     else:
         base, stride, steps = 1, 1, blocks - 2
     width = left_env.shape[0]
-    nt = tl.shape[0]
+    nt = idx.shape[0] * idx.shape[2]
     rblock = (width, 1, depth, depth)
 
     def rloc_map(p):
-        def index(b, tl_r, tr_r, bs_r, sh_r, ids_r):
+        def index(b, idx_r, bs_r, sh_r, ids_r):
             return (0, jnp.clip(base + b * stride + sh_r[ids_r[1] + p], 0, blocks - 1), 0, 0)
         return index
 
@@ -221,9 +224,9 @@
         in_specs += [pl.BlockSpec(rblock, const4), pl.BlockSpec(rblock, const4),
                      pl.BlockSpec(memory_space=pl.ANY)]
         operands += [lo, hi, prev]
-        aliases = {5 + len(operands) - 1: 0}
+        aliases = {4 + len(operands) - 1: 0}
     grid_spec = pltpu.PrefetchScalarGridSpec(
-        num_scalar_prefetch=5,
+        num_scalar_prefetch=4,
         grid=(steps,),
         in_specs=in_specs,
         out_specs=pl.BlockSpec((1, npl, depth, depth),
@@ -247,7 +250,7 @@
             bytes_accessed=2 * steps * (two_site.size + left_env.size + 3 * right_env.size)
             // blocks),
         input_output_aliases=aliases,
-    )(tl, tr, block_sizes, shifts, ids, *operands)
+    )(idx, block_sizes, shifts, ids, *operands)
 
 
 def solution(mesh):

time: 71.4 us -> 70 us (0.980)
  other arithmetic: 2.88 us -> 1.23 us
    convert_element_type x4 -> x0, other arithmetic: 2.3 us -> none  [the longest x1 1.61 us: body(): tr = packed[:, nq * nq + 1].astype(jnp.int32)]
    slice x2 -> x0, local copies, waits for them, and re-layouts: 0.96 us -> none  [body(): terms = packed[:, :nq * nq].reshape(nt, nq, nq).astype(mpo_terms.dtype)]
    unnamed x10 -> x11, local copies, waits for them, and re-layouts: 2.01 us -> 2.02 us
  transfers between devices with their start and end apart: 2 -> 2, of which waited for: 0 -> 0; matrix products, arithmetic and copies ran while one was open for 7% -> 4% of each run, Pallas kernels for 53% -> 55%
where the time goes in v7:
time: 70 us; the launch traced here: 69.7 us
  Pallas kernels  51.9 us (74%)
  starting transfers between devices  9.79 us (14%)
  local copies, waits for them, and re-layouts  6.7 us (10%)
  other arithmetic  1.23 us (2%)
    pallas_call x2, Pallas kernels, block_call(): pl.pallas_call(functools.partial(kernel, npl, nt, base, stride, blocks, t...  43.2 us
    pallas_call x1, Pallas kernels, gather_terms(): pl.pallas_call(functools.partial(gather_kernel, nm), out_shape=(jax.Shape...  8.74 us
    ppermute x1, starting transfers between devices, halos(): hi = lax.ppermute(head, axis, [(i + 1, i) for i in range(ends)])  6.12 us
    ppermute x1, starting transfers between devices, halos(): lo = lax.ppermute(tail, axis, [(i, i + 1) for i in range(ends)])  3.66 us
    slice x1, local copies, waits for them, and re-layouts, halos(): head = lax.slice_in_dim(cells, 0, width, axis=dim)  3.23 us
    unnamed x11, local copies, waits for them, and re-layouts  2.02 us
  transfers between devices with their start and end apart: 2, of which 0 were waited for; matrix products, arithmetic and copies ran while one was open for 4% of the time, Pallas kernels for 55%

profile of v7, /device:TPU:7, one launch (start us, length us, event | category | flops | bytes accessed | tf_op | source)
XLA Modules:
  0.0 69.7 jit_solution(13267811962157761127)
XLA Ops:
  0.0 0.0 copy-start.2
  0.0 3.2 %fusion = (bf16[34,1,128,128]{3,2,1,0:T(8,128)(2,1)}, bf16[34,1,128,128]{3,2,1,0:T(8,128)(2,1)}) fusion(bf16[34,8,128,128]{3,2,1,0:T(8,128)(2,1)} %refs_8_.3), kind=kLoop, calls=%fused_computation.2 | loop fusion | bytes 4456448 | tf_op jit(solution)/shard_map/slice | solution.py:163
  3.2 0.0 copy-start.3
  3.2 0.0 copy-start.4
  3.2 3.7 %collective-permute-start = (bf16[34,1,128,128]{3,2,1,0:T(8,128)(2,1)}, bf16[34,1,128,128]{3,2,1,0:T(8,128)(2,1)S(1)}, u32[]{:S(2)}, u32[]{:S(2)}) collective-permute-start(bf16[34,1,128,128]{3,2,1,0:T(8,128)(2,1)} %get-tuple-element.10), channel_id=1, source_target_pairs={{0,1},{1,2},{2,3},{3,4},{4,5},{5,6},{6,7},{7,8},{8,9},{9,10},{10,1... | collective-permute-start | bytes 3342344 | tf_op jit(solution)/shard_map/ppermute | solution.py:165
  6.9 6.1 %collective-permute-start.1 = (bf16[34,1,128,128]{3,2,1,0:T(8,128)(2,1)}, bf16[34,1,128,128]{3,2,1,0:T(8,128)(2,1)S(1)}, u32[]{:S(2)}, u32[]{:S(2)}) collective-permute-start(bf16[34,1,128,128]{3,2,1,0:T(8,128)(2,1)} %get-tuple-element.9), channel_id=1, source_target_pairs={{1,0},{2,1},{3,2},{4,3},{5,4},{6,5},{7,6},{8,7},{9,8},{10,9},{11,1... | collective-permute-start | bytes 3342344 | tf_op jit(solution)/shard_map/ppermute | solution.py:166
  13.0 0.0 copy-done.2
  13.1 0.3 broadcast_in_dim.3
  13.4 1.1 %reshape.14.x_ref = bf16[8,16,256]{2,1,0:T(8,128)(2,1)} reshape(bf16[8,16,16,16]{3,2,1,0:T(8,128)(2,1)S(1)} %broadcast_in_dim.3) | data formatting | bytes 131072 | tf_op jit(solution)/shard_map/reshape | solution.py:181
  14.5 0.0 copy-done.3
  14.5 0.0 copy-done.4
  14.5 0.6 pad_add_fusion.idx_ref
  15.1 8.7 %shard_map.82 = (bf16[8,16,256]{2,1,0:T(8,128)(2,1)}, s32[8,2,8]{2,1,0:T(2,128)}) custom-call(bf16[8,16,256]{2,1,0:T(8,128)(2,1)} %reshape.14.x_ref, s32[2,8]{1,0:T(2,128)} %pad_add_fusion.idx_ref), custom_call_target="tpu_custom_call" | custom-call | tf_op jit(solution)/shard_map/pallas_call | solution.py:149
  23.9 0.6 pad_add_fusion.1.refs_3_
  24.5 29.6 %shard_map.83.refs_11_ = bf16[8,2,128,128]{3,2,1,0:T(8,128)(2,1)} custom-call(s32[8,2,8]{2,1,0:T(2,128)} %get-tuple-element.7.refs_0_, s32[256]{0:T(256)} %refs_1_.3, s32[16]{0:T(128)} %refs_2_.3, s32[2]{0:T(128)} %pad_add_fusion.1.refs_3_, bf16[8,16,128,128]{3,2,1,0:T(8,128)(2,1)} %refs_4_.3, bf16[34,8,128,128]{3,2,1,0:T(8,128)(2,1)} %refs_5_.3, ...), custom_call_target="tpu_custom_call" | custom-call | flops 7247757312 | bytes 29884416 | tf_op jit(solution)/shard_map/pallas_call | solution.py:242
  54.2 0.0 collective-permute-done.refs_9_
  54.2 0.0 copy-start
  54.2 0.0 collective-permute-done.1.refs_10_
  54.2 1.0 %copy-done = bf16[34,1,128,128]{3,2,1,0:T(8,128)(2,1)} copy-done((bf16[34,1,128,128]{3,2,1,0:T(8,128)(2,1)}, bf16[34,1,128,128]{3,2,1,0:T(8,128)(2,1)S(1)}, u32[]{:S(2)}) %copy-start) | copy-done | bytes 1114136
  55.2 0.0 copy-start.1
  55.2 1.0 %copy-done.1 = bf16[34,1,128,128]{3,2,1,0:T(8,128)(2,1)} copy-done((bf16[34,1,128,128]{3,2,1,0:T(8,128)(2,1)}, bf16[34,1,128,128]{3,2,1,0:T(8,128)(2,1)S(1)}, u32[]{:S(2)}) %copy-start.1) | copy-done | bytes 1114136
  56.2 13.5 %shard_map.84 = bf16[8,2,128,128]{3,2,1,0:T(8,128)(2,1)} custom-call(s32[8,2,8]{2,1,0:T(2,128)} %get-tuple-element.7.refs_0_, s32[256]{0:T(256)} %refs_1_.3, s32[16]{0:T(128)} %refs_2_.3, s32[2]{0:T(128)} %pad_add_fusion.1.refs_3_, bf16[8,16,128,128]{3,2,1,0:T(8,128)(2,1)} %refs_4_.3, ...), custom_call_target="tpu_custom_call", output_to_operand_aliasing={{}: (11, {})} | custom-call | flops 2415919104 | bytes 9961472 | tf_op jit(solution)/shard_map/pallas_call | solution.py:242
  (3 shorter events, 0.0 us)
Async XLA Ops:
  0.0 13.0 %copy-start.2 = (bf16[8,16,16]{2,1,0:T(8,128)(2,1)S(1)}, bf16[8,16,16]{2,1,0:T(8,128)(2,1)}, u32[]{:S(2)}) copy-start(bf16[8,16,16]{2,1,0:T(8,128)(2,1)} %param.11) | copy-start | bytes 12292
  3.2 11.3 %copy-start.3 = (s32[8]{0:T(128)S(1)}, s32[8]{0:T(128)}, u32[]{:S(2)}) copy-start(s32[8]{0:T(128)} %param.13) | copy-start | bytes 100
  3.2 11.3 %copy-start.4 = (s32[8]{0:T(128)S(1)}, s32[8]{0:T(128)}, u32[]{:S(2)}) copy-start(s32[8]{0:T(128)} %param.12) | copy-start | bytes 100
  3.2 50.9 %collective-permute-start = (bf16[34,1,128,128]{3,2,1,0:T(8,128)(2,1)}, bf16[34,1,128,128]{3,2,1,0:T(8,128)(2,1)S(1)}, u32[]{:S(2)}, u32[]{:S(2)}) collective-permute-start(bf16[34,1,128,128]{3,2,1,0:T(8,128)(2,1)} %get-tuple-element.10), channel_id=1, source_target_pairs={{0,1},{1,2},{2,3},{3,4},{4,5},{5,6},{6,7},{7,8},{8,9},{9,10},{10,1... | collective-permute-start | bytes 3342344 | tf_op jit(solution)/shard_map/ppermute | solution.py:165
  6.9 47.3 %collective-permute-start.1 = (bf16[34,1,128,128]{3,2,1,0:T(8,128)(2,1)}, bf16[34,1,128,128]{3,2,1,0:T(8,128)(2,1)S(1)}, u32[]{:S(2)}, u32[]{:S(2)}) collective-permute-start(bf16[34,1,128,128]{3,2,1,0:T(8,128)(2,1)} %get-tuple-element.9), channel_id=1, source_target_pairs={{1,0},{2,1},{3,2},{4,3},{5,4},{6,5},{7,6},{8,7},{9,8},{10,9},{11,1... | collective-permute-start | bytes 3342344 | tf_op jit(solution)/shard_map/ppermute | solution.py:166
  54.2 1.0 %copy-start = (bf16[34,1,128,128]{3,2,1,0:T(8,128)(2,1)}, bf16[34,1,128,128]{3,2,1,0:T(8,128)(2,1)S(1)}, u32[]{:S(2)}) copy-start(bf16[34,1,128,128]{3,2,1,0:T(8,128)(2,1)S(1)} %collective-permute-done.refs_9_) | copy-start | bytes 3342340
  55.2 1.0 %copy-start.1 = (bf16[34,1,128,128]{3,2,1,0:T(8,128)(2,1)}, bf16[34,1,128,128]{3,2,1,0:T(8,128)(2,1)S(1)}, u32[]{:S(2)}) copy-start(bf16[34,1,128,128]{3,2,1,0:T(8,128)(2,1)S(1)} %collective-permute-done.1.refs_10_) | copy-start | bytes 3342340

commit v8 on v7

--- a/solution.py
+++ b/solution.py
@@ -221,7 +221,7 @@
     operands = [two_site, left_env, mq, right_env, right_env]
     aliases = {}
     if halo:
-        in_specs += [pl.BlockSpec(rblock, const4), pl.BlockSpec(rblock, const4),
+        in_specs += [pl.BlockSpec(memory_space=pltpu.VMEM), pl.BlockSpec(memory_space=pltpu.VMEM),
                      pl.BlockSpec(memory_space=pl.ANY)]
         operands += [lo, hi, prev]
         aliases = {4 + len(operands) - 1: 0}
@@ -244,7 +244,7 @@
         out_shape=jax.ShapeDtypeStruct((blocks, npl, depth, depth), jnp.bfloat16),
         grid_spec=grid_spec,
         compiler_params=pltpu.CompilerParams(
-            dimension_semantics=("arbitrary",), vmem_limit_bytes=60 * 1024 * 1024),
+            dimension_semantics=("arbitrary",), vmem_limit_bytes=(48 if halo else 60) * 1024 * 1024),
         cost_estimate=pl.CostEstimate(
             flops=flops, transcendentals=0,
             bytes_accessed=2 * steps * (two_site.size + left_env.size + 3 * right_env.size)

time: 70 us -> 67.3 us (0.961)
  local copies, waits for them, and re-layouts: 6.7 us -> 4.73 us
  Pallas kernels: 51.9 us -> 51.1 us
    unnamed x11 -> x17, local copies, waits for them, and re-layouts: 2.02 us -> 0.04 us
    pallas_call x2, Pallas kernels: 43.2 us -> 42.4 us  [block_call(): pl.pallas_call(functools.partial(kernel, npl, nt, base, stride, blocks, t...]
  transfers between devices with their start and end apart: 2 -> 2, of which waited for: 0 -> 0; matrix products, arithmetic and copies ran while one was open for 4% -> 4% of each run, Pallas kernels for 55% -> 57%
where the time goes in v8:
time: 67.3 us; the launch traced here: 67 us
  Pallas kernels  51.1 us (76%)
  starting transfers between devices  9.79 us (15%)
  local copies, waits for them, and re-layouts  4.73 us (7%)
  other arithmetic  1.27 us (2%)
    pallas_call x2, Pallas kernels, block_call(): pl.pallas_call(functools.partial(kernel, npl, nt, base, stride, blocks, t...  42.4 us
    pallas_call x1, Pallas kernels, gather_terms(): pl.pallas_call(functools.partial(gather_kernel, nm), out_shape=(jax.Shape...  8.74 us
    ppermute x1, starting transfers between devices, halos(): hi = lax.ppermute(head, axis, [(i + 1, i) for i in range(ends)])  6.12 us
    ppermute x1, starting transfers between devices, halos(): lo = lax.ppermute(tail, axis, [(i, i + 1) for i in range(ends)])  3.66 us
    slice x1, local copies, waits for them, and re-layouts, halos(): head = lax.slice_in_dim(cells, 0, width, axis=dim)  3.24 us
  transfers between devices with their start and end apart: 2, of which 0 were waited for; matrix products, arithmetic and copies ran while one was open for 4% of the time, Pallas kernels for 57%

profile of v8, /device:TPU:7, one launch (start us, length us, event | category | flops | bytes accessed | tf_op | source)
XLA Modules:
  0.0 67.0 jit_solution(12126250816877705551)
XLA Ops:
  0.0 0.0 copy-start.5
  0.0 3.2 %fusion = (bf16[34,1,128,128]{3,2,1,0:T(8,128)(2,1)}, bf16[34,1,128,128]{3,2,1,0:T(8,128)(2,1)}) fusion(bf16[34,8,128,128]{3,2,1,0:T(8,128)(2,1)} %refs_8_.3), kind=kLoop, calls=%fused_computation.2 | loop fusion | bytes 4456448 | tf_op jit(solution)/shard_map/slice | solution.py:163
  3.2 0.0 copy-start.6
  3.2 0.0 copy-start.7
  3.2 3.7 %collective-permute-start = (bf16[34,1,128,128]{3,2,1,0:T(8,128)(2,1)}, bf16[34,1,128,128]{3,2,1,0:T(8,128)(2,1)S(1)}, u32[]{:S(2)}, u32[]{:S(2)}) collective-permute-start(bf16[34,1,128,128]{3,2,1,0:T(8,128)(2,1)} %get-tuple-element.10), channel_id=1, source_target_pairs={{0,1},{1,2},{2,3},{3,4},{4,5},{5,6},{6,7},{7,8},{8,9},{9,10},{10,1... | collective-permute-start | bytes 3342344 | tf_op jit(solution)/shard_map/ppermute | solution.py:165
  6.9 6.1 %collective-permute-start.1 = (bf16[34,1,128,128]{3,2,1,0:T(8,128)(2,1)}, bf16[34,1,128,128]{3,2,1,0:T(8,128)(2,1)S(1)}, u32[]{:S(2)}, u32[]{:S(2)}) collective-permute-start(bf16[34,1,128,128]{3,2,1,0:T(8,128)(2,1)} %get-tuple-element.9), channel_id=1, source_target_pairs={{1,0},{2,1},{3,2},{4,3},{5,4},{6,5},{7,6},{8,7},{9,8},{10,9},{11,1... | collective-permute-start | bytes 3342344 | tf_op jit(solution)/shard_map/ppermute | solution.py:166
  13.1 0.0 copy-done.5
  13.1 0.3 broadcast_in_dim.3
  13.5 1.1 %reshape.14.x_ref = bf16[8,16,256]{2,1,0:T(8,128)(2,1)} reshape(bf16[8,16,16,16]{3,2,1,0:T(8,128)(2,1)S(1)} %broadcast_in_dim.3) | data formatting | bytes 131072 | tf_op jit(solution)/shard_map/reshape | solution.py:181
  14.6 0.0 copy-done.6
  14.6 0.0 copy-done.7
  14.6 0.6 pad_add_fusion.idx_ref
  15.2 8.7 %shard_map.82 = (bf16[8,16,256]{2,1,0:T(8,128)(2,1)}, s32[8,2,8]{2,1,0:T(2,128)}) custom-call(bf16[8,16,256]{2,1,0:T(8,128)(2,1)} %reshape.14.x_ref, s32[2,8]{1,0:T(2,128)} %pad_add_fusion.idx_ref), custom_call_target="tpu_custom_call" | custom-call | tf_op jit(solution)/shard_map/pallas_call | solution.py:149
  23.9 0.7 pad_add_fusion.1.refs_3_
  24.6 0.0 copy-start
  24.6 0.0 copy-start.1
  24.6 0.0 copy-start.2
  24.6 0.0 copy-start.3
  24.6 0.0 copy-start.4
  24.6 29.7 %shard_map.83.refs_11_ = bf16[8,2,128,128]{3,2,1,0:T(8,128)(2,1)} custom-call(s32[8,2,8]{2,1,0:T(2,128)} %get-tuple-element.7.refs_0_, s32[256]{0:T(256)} %refs_1_.3, s32[16]{0:T(128)} %refs_2_.3, s32[2]{0:T(128)} %pad_add_fusion.1.refs_3_, bf16[8,16,128,128]{3,2,1,0:T(8,128)(2,1)} %refs_4_.3, bf16[34,8,128,128]{3,2,1,0:T(8,128)(2,1)} %refs_5_.3, ...), custom_call_target="tpu_custom_call" | custom-call | flops 7247757312 | bytes 29884416 | tf_op jit(solution)/shard_map/pallas_call | solution.py:242
  54.3 0.0 collective-permute-done.refs_9_
  54.3 0.0 collective-permute-done.1.refs_10_
  54.3 0.0 copy-done
  54.3 0.0 copy-done.1
  54.3 0.0 copy-done.2
  54.3 0.0 copy-done.3
  54.3 0.0 copy-done.4
  54.3 12.7 %shard_map.84 = bf16[8,2,128,128]{3,2,1,0:T(8,128)(2,1)} custom-call(s32[8,2,8]{2,1,0:T(2,128)S(1)} %copy-done.1, s32[256]{0:T(256)S(1)} %copy-done.2, s32[16]{0:T(128)S(1)} %copy-done.3, s32[2]{0:T(128)S(1)} %copy-done.4, bf16[8,16,128,128]{3,2,1,0:T(8,128)(2,1)} %refs_4_.3, bf16[34,8,128,128]{3,2,1,0:T(8,128)(2,1)} %refs_5_.3, ...), custom_call_target="tpu_custom_call", output_to_operand_aliasing={{}: (11, {})} | custom-call | flops 2415919104 | bytes 9961472 | tf_op jit(solution)/shard_map/pallas_call | solution.py:242
  (3 shorter events, 0.0 us)
Async XLA Ops:
  0.0 13.1 %copy-start.5 = (bf16[8,16,16]{2,1,0:T(8,128)(2,1)S(1)}, bf16[8,16,16]{2,1,0:T(8,128)(2,1)}, u32[]{:S(2)}) copy-start(bf16[8,16,16]{2,1,0:T(8,128)(2,1)} %param.11) | copy-start | bytes 12292
  3.2 11.3 %copy-start.6 = (s32[8]{0:T(128)S(1)}, s32[8]{0:T(128)}, u32[]{:S(2)}) copy-start(s32[8]{0:T(128)} %param.13) | copy-start | bytes 100
  3.2 11.3 %copy-start.7 = (s32[8]{0:T(128)S(1)}, s32[8]{0:T(128)}, u32[]{:S(2)}) copy-start(s32[8]{0:T(128)} %param.12) | copy-start | bytes 100
  3.2 51.0 %collective-permute-start = (bf16[34,1,128,128]{3,2,1,0:T(8,128)(2,1)}, bf16[34,1,128,128]{3,2,1,0:T(8,128)(2,1)S(1)}, u32[]{:S(2)}, u32[]{:S(2)}) collective-permute-start(bf16[34,1,128,128]{3,2,1,0:T(8,128)(2,1)} %get-tuple-element.10), channel_id=1, source_target_pairs={{0,1},{1,2},{2,3},{3,4},{4,5},{5,6},{6,7},{7,8},{8,9},{9,10},{10,1... | collective-permute-start | bytes 3342344 | tf_op jit(solution)/shard_map/ppermute | solution.py:165
  6.9 47.4 %collective-permute-start.1 = (bf16[34,1,128,128]{3,2,1,0:T(8,128)(2,1)}, bf16[34,1,128,128]{3,2,1,0:T(8,128)(2,1)S(1)}, u32[]{:S(2)}, u32[]{:S(2)}) collective-permute-start(bf16[34,1,128,128]{3,2,1,0:T(8,128)(2,1)} %get-tuple-element.9), channel_id=1, source_target_pairs={{1,0},{2,1},{3,2},{4,3},{5,4},{6,5},{7,6},{8,7},{9,8},{10,9},{11,1... | collective-permute-start | bytes 3342344 | tf_op jit(solution)/shard_map/ppermute | solution.py:166
  24.6 29.7 %copy-start = (bf16[8,16,256]{2,1,0:T(8,128)(2,1)S(1)}, bf16[8,16,256]{2,1,0:T(8,128)(2,1)}, u32[]{:S(2)}) copy-start(bf16[8,16,256]{2,1,0:T(8,128)(2,1)} %get-tuple-element.8) | copy-start | bytes 196612
  24.6 29.7 %copy-start.1 = (s32[8,2,8]{2,1,0:T(2,128)S(1)}, s32[8,2,8]{2,1,0:T(2,128)}, u32[]{:S(2)}) copy-start(s32[8,2,8]{2,1,0:T(2,128)} %get-tuple-element.7.refs_0_) | copy-start | bytes 1540
  24.6 29.7 %copy-start.2 = (s32[256]{0:T(256)S(1)}, s32[256]{0:T(256)}, u32[]{:S(2)}) copy-start(s32[256]{0:T(256)} %refs_1_.3) | copy-start | bytes 3076
  24.6 29.7 %copy-start.3 = (s32[16]{0:T(128)S(1)}, s32[16]{0:T(128)}, u32[]{:S(2)}) copy-start(s32[16]{0:T(128)} %refs_2_.3) | copy-start | bytes 196
  24.6 29.7 %copy-start.4 = (s32[2]{0:T(128)S(1)}, s32[2]{0:T(128)}, u32[]{:S(2)}) copy-start(s32[2]{0:T(128)} %pad_add_fusion.1.refs_3_) | copy-start | bytes 28

commit v9 on v8

--- a/solution.py
+++ b/solution.py
@@ -20,14 +20,13 @@
     (idx_ref, bs_ref, sh_ref, ids_ref,
      ts_ref, left_ref, mq_ref, rloc0_ref, rloc1_ref) = refs[:9]
     if halo:
-        lo_ref, hi_ref = refs[9:11]
-        refs = refs[12:]
+        lo_ref, hi_ref, kron_scr = refs[9:12]
+        out_ref, c_scr, x_scr, y_scr = refs[13:]
     else:
-        refs = refs[9:]
+        out_ref, kron_scr, c_scr, x_scr, y_scr = refs[9:]
     per = idx_ref.shape[2]
     tl_of = lambda t: idx_ref[t // per, 0, t % per]
     tr_of = lambda t: idx_ref[t // per, 1, t % per]
-    out_ref, c_scr, x_scr, y_scr, kron_scr = refs
     first_step = pl.program_id(0) == 0
     i = base + pl.program_id(0) * stride
     gi = ids_ref[0] + i
@@ -50,15 +49,16 @@
     nr = npl * nt
     rchunk = RCHUNK
 
-    @pl.when(first_step)
-    def _():
-        a = lax.broadcasted_iota(jnp.int32, (nr * YT, nr), 0)
-        r = lax.broadcasted_iota(jnp.int32, (nr * YT, nr), 1)
-        pick = jnp.where(a // YT == r, 1.0, 0.0).astype(mq_ref.dtype)
-        rep = jnp.dot(pick, mq_ref[...], preferred_element_type=jnp.float32)
-        ra = lax.broadcasted_iota(jnp.int32, rep.shape, 0)
-        cb = lax.broadcasted_iota(jnp.int32, rep.shape, 1)
-        kron_scr[...] = jnp.where(ra % YT == cb % YT, rep, 0.0).astype(kron_scr.dtype)
+    if not halo:
+        @pl.when(first_step)
+        def _():
+            a = lax.broadcasted_iota(jnp.int32, (nr * YT, nr), 0)
+            r = lax.broadcasted_iota(jnp.int32, (nr * YT, nr), 1)
+            pick = jnp.where(a // YT == r, 1.0, 0.0).astype(mq_ref.dtype)
+            rep = jnp.dot(pick, mq_ref[...], preferred_element_type=jnp.float32)
+            ra = lax.broadcasted_iota(jnp.int32, rep.shape, 0)
+            cb = lax.broadcasted_iota(jnp.int32, rep.shape, 1)
+            kron_scr[...] = jnp.where(ra % YT == cb % YT, rep, 0.0).astype(kron_scr.dtype)
 
     for yb in range(0 if "nomix" in VARIANT else depth // (2 * YT)):
         ya, yc = 2 * yb * YT, (2 * yb + 1) * YT
@@ -189,7 +189,8 @@
 
     scalars = (idx, block_sizes, shifts, ids)
     inner = block_call(*scalars, two_site, left_env, mq, right_env, None, None, None, npl=npl)
-    return block_call(*scalars, two_site, left_env, mq, right_env, lo, hi, inner, npl=npl)
+    inner, kron = inner
+    return block_call(*scalars, two_site, left_env, kron, right_env, lo, hi, inner, npl=npl)
 
 
 def block_call(idx, block_sizes, shifts, ids, two_site, left_env, mq, right_env,
@@ -220,28 +221,35 @@
     ]
     operands = [two_site, left_env, mq, right_env, right_env]
     aliases = {}
+    kron_shape = (nt * npl * YT, nq * YT)
     if halo:
         in_specs += [pl.BlockSpec(memory_space=pltpu.VMEM), pl.BlockSpec(memory_space=pltpu.VMEM),
+                     pl.BlockSpec(kron_shape, lambda b, *refs: (0, 0)),
                      pl.BlockSpec(memory_space=pl.ANY)]
-        operands += [lo, hi, prev]
+        operands += [lo, hi, mq, prev]
         aliases = {4 + len(operands) - 1: 0}
+    out_block = pl.BlockSpec((1, npl, depth, depth), lambda b, *refs: (base + b * stride, 0, 0, 0))
+    out_shape = jax.ShapeDtypeStruct((blocks, npl, depth, depth), jnp.bfloat16)
+    if halo:
+        out_specs = out_block
+    else:
+        out_specs = (out_block, pl.BlockSpec(kron_shape, lambda b, *refs: (0, 0)))
+        out_shape = (out_shape, jax.ShapeDtypeStruct(kron_shape, jnp.bfloat16))
     grid_spec = pltpu.PrefetchScalarGridSpec(
         num_scalar_prefetch=4,
         grid=(steps,),
         in_specs=in_specs,
-        out_specs=pl.BlockSpec((1, npl, depth, depth),
-                               lambda b, *refs: (base + b * stride, 0, 0, 0)),
+        out_specs=out_specs,
         scratch_shapes=[
             pltpu.VMEM((nq, depth, depth), jnp.bfloat16),
             pltpu.VMEM((nt * npl, depth, depth), jnp.bfloat16),
             pltpu.VMEM((npl, nt, depth, depth), jnp.bfloat16),
-            pltpu.VMEM((nt * npl * YT, nq * YT), jnp.bfloat16),
         ],
     )
     flops = 2 * steps * (nt * npl * YT * nq * YT * depth + 2 * nt * npl * depth ** 3)
     return pl.pallas_call(
         functools.partial(kernel, npl, nt, base, stride, blocks, total, halo),
-        out_shape=jax.ShapeDtypeStruct((blocks, npl, depth, depth), jnp.bfloat16),
+        out_shape=out_shape,
         grid_spec=grid_spec,
         compiler_params=pltpu.CompilerParams(
             dimension_semantics=("arbitrary",), vmem_limit_bytes=(48 if halo else 60) * 1024 * 1024),

time: 67.3 us -> 67.8 us (level)
  local copies, waits for them, and re-layouts: 4.73 us -> 5.94 us
    ppermute x1, starting transfers between devices: 6.12 us -> 7.87 us  [halos(): hi = lax.ppermute(head, axis, [(i + 1, i) for i in range(ends)])]
    ppermute x1, starting transfers between devices: 3.66 us -> 1.92 us  [halos(): lo = lax.ppermute(tail, axis, [(i, i + 1) for i in range(ends)])]
    unnamed x17, local copies, waits for them, and re-layouts: 0.04 us -> 1.25 us
where the time goes in v9:
time: 67.8 us; the launch traced here: 67.5 us
  Pallas kernels  50.5 us (74%)
  starting transfers between devices  9.79 us (14%)
  local copies, waits for them, and re-layouts  5.94 us (9%)
  other arithmetic  1.14 us (2%)
    pallas_call x2, Pallas kernels, block_call(): pl.pallas_call(functools.partial(kernel, npl, nt, base, stride, blocks, t...  41.8 us
    pallas_call x1, Pallas kernels, gather_terms(): pl.pallas_call(functools.partial(gather_kernel, nm), out_shape=(jax.Shape...  8.74 us
    ppermute x1, starting transfers between devices, halos(): hi = lax.ppermute(head, axis, [(i + 1, i) for i in range(ends)])  7.87 us
    slice x1, local copies, waits for them, and re-layouts, halos(): head = lax.slice_in_dim(cells, 0, width, axis=dim)  3.24 us
    ppermute x1, starting transfers between devices, halos(): lo = lax.ppermute(tail, axis, [(i, i + 1) for i in range(ends)])  1.92 us
  transfers between devices with their start and end apart: 2, of which 0 were waited for; matrix products, arithmetic and copies ran while one was open for 4% of the time, Pallas kernels for 57%

profile of v9, /device:TPU:7, one launch (start us, length us, event | category | flops | bytes accessed | tf_op | source)
XLA Modules:
  0.0 67.5 jit_solution(14700977049679234212)
XLA Ops:
  0.0 0.0 copy-start.5
  0.0 3.2 %fusion = (bf16[34,1,128,128]{3,2,1,0:T(8,128)(2,1)}, bf16[34,1,128,128]{3,2,1,0:T(8,128)(2,1)}) fusion(bf16[34,8,128,128]{3,2,1,0:T(8,128)(2,1)} %refs_8_.3), kind=kLoop, calls=%fused_computation.2 | loop fusion | bytes 4456448 | tf_op jit(solution)/shard_map/slice | solution.py:163
  3.2 0.0 copy-start.6
  3.2 0.0 copy-start.7
  3.2 7.9 %collective-permute-start.1 = (bf16[34,1,128,128]{3,2,1,0:T(8,128)(2,1)}, bf16[34,1,128,128]{3,2,1,0:T(8,128)(2,1)S(1)}, u32[]{:S(2)}, u32[]{:S(2)}) collective-permute-start(bf16[34,1,128,128]{3,2,1,0:T(8,128)(2,1)} %get-tuple-element.13), channel_id=1, source_target_pairs={{1,0},{2,1},{3,2},{4,3},{5,4},{6,5},{7,6},{8,7},{9,8},{10,9},{11,1... | collective-permute-start | bytes 3342344 | tf_op jit(solution)/shard_map/ppermute | solution.py:166
  11.1 1.9 %collective-permute-start = (bf16[34,1,128,128]{3,2,1,0:T(8,128)(2,1)}, bf16[34,1,128,128]{3,2,1,0:T(8,128)(2,1)S(1)}, u32[]{:S(2)}, u32[]{:S(2)}) collective-permute-start(bf16[34,1,128,128]{3,2,1,0:T(8,128)(2,1)} %get-tuple-element.14), channel_id=1, source_target_pairs={{0,1},{1,2},{2,3},{3,4},{4,5},{5,6},{6,7},{7,8},{8,9},{9,10},{10,1... | collective-permute-start | bytes 3342344 | tf_op jit(solution)/shard_map/ppermute | solution.py:165
  13.1 0.0 copy-done.5
  13.1 0.3 broadcast_in_dim.3
  13.5 1.1 %reshape.14.x_ref = bf16[8,16,256]{2,1,0:T(8,128)(2,1)} reshape(bf16[8,16,16,16]{3,2,1,0:T(8,128)(2,1)S(1)} %broadcast_in_dim.3) | data formatting | bytes 131072 | tf_op jit(solution)/shard_map/reshape | solution.py:181
  14.6 0.0 copy-done.6
  14.6 0.0 copy-done.7
  14.6 0.6 pad_add_fusion.idx_ref
  15.1 8.7 %shard_map.82 = (bf16[8,16,256]{2,1,0:T(8,128)(2,1)}, s32[8,2,8]{2,1,0:T(2,128)}) custom-call(bf16[8,16,256]{2,1,0:T(8,128)(2,1)} %reshape.14.x_ref, s32[2,8]{1,0:T(2,128)} %pad_add_fusion.idx_ref), custom_call_target="tpu_custom_call" | custom-call | tf_op jit(solution)/shard_map/pallas_call | solution.py:149
  23.9 0.6 pad_add_fusion.1.refs_3_
  24.4 0.0 copy-start.1
  24.4 0.0 copy-start.2
  24.4 0.0 copy-start.3
  24.5 0.0 copy-start.4
  24.5 29.8 %shard_map.83 = (bf16[8,2,128,128]{3,2,1,0:T(8,128)(2,1)}, bf16[2048,256]{1,0:T(8,128)(2,1)}) custom-call(s32[8,2,8]{2,1,0:T(2,128)} %get-tuple-element.9.refs_0_, s32[256]{0:T(256)} %refs_1_.3, s32[16]{0:T(128)} %refs_2_.3, s32[2]{0:T(128)} %pad_add_fusion.1.refs_3_, bf16[8,16,128,128]{3,2,1,0:T(8,128)(2,1)} %refs_4_.3, bf16[34,8,128,128]{3,2,1,0:T(8,128)(2,1)} %refs_5_.3, ...), custom_call_target="tpu_custom_call" | custom-call | flops 7247757312 | bytes 29884416 | tf_op jit(solution)/shard_map/pallas_call | solution.py:250
  54.2 0.0 collective-permute-done.1.refs_10_
  54.2 0.0 collective-permute-done.refs_9_
  54.3 0.0 copy-done.1
  54.3 0.0 copy-done.2
  54.3 0.0 copy-done.3
  54.3 0.0 copy-done.4
  54.3 0.0 copy-start
  54.3 1.2 %copy-done = bf16[2048,256]{1,0:T(8,128)(2,1)S(1)} copy-done((bf16[2048,256]{1,0:T(8,128)(2,1)S(1)}, bf16[2048,256]{1,0:T(8,128)(2,1)}, u32[]{:S(2)}) %copy-start) | copy-done | bytes 1048600
  55.5 12.0 %shard_map.84 = bf16[8,2,128,128]{3,2,1,0:T(8,128)(2,1)} custom-call(s32[8,2,8]{2,1,0:T(2,128)S(1)} %copy-done.1, s32[256]{0:T(256)S(1)} %copy-done.2, s32[16]{0:T(128)S(1)} %copy-done.3, s32[2]{0:T(128)S(1)} %copy-done.4, bf16[8,16,128,128]{3,2,1,0:T(8,128)(2,1)} %refs_4_.3, bf16[34,8,128,128]{3,2,1,0:T(8,128)(2,1)} %refs_5_.3, ...), custom_call_target="tpu_custom_call", output_to_operand_aliasing={{}: (12, {})} | custom-call | flops 2415919104 | bytes 9961472 | tf_op jit(solution)/shard_map/pallas_call | solution.py:250
  (3 shorter events, 0.0 us)
Async XLA Ops:
  0.0 13.1 %copy-start.5 = (bf16[8,16,16]{2,1,0:T(8,128)(2,1)S(1)}, bf16[8,16,16]{2,1,0:T(8,128)(2,1)}, u32[]{:S(2)}) copy-start(bf16[8,16,16]{2,1,0:T(8,128)(2,1)} %param.11) | copy-start | bytes 12292
  3.2 11.3 %copy-start.6 = (s32[8]{0:T(128)S(1)}, s32[8]{0:T(128)}, u32[]{:S(2)}) copy-start(s32[8]{0:T(128)} %param.13) | copy-start | bytes 100
  3.2 11.3 %copy-start.7 = (s32[8]{0:T(128)S(1)}, s32[8]{0:T(128)}, u32[]{:S(2)}) copy-start(s32[8]{0:T(128)} %param.12) | copy-start | bytes 100
  3.2 51.0 %collective-permute-start.1 = (bf16[34,1,128,128]{3,2,1,0:T(8,128)(2,1)}, bf16[34,1,128,128]{3,2,1,0:T(8,128)(2,1)S(1)}, u32[]{:S(2)}, u32[]{:S(2)}) collective-permute-start(bf16[34,1,128,128]{3,2,1,0:T(8,128)(2,1)} %get-tuple-element.13), channel_id=1, source_target_pairs={{1,0},{2,1},{3,2},{4,3},{5,4},{6,5},{7,6},{8,7},{9,8},{10,9},{11,1... | collective-permute-start | bytes 3342344 | tf_op jit(solution)/shard_map/ppermute | solution.py:166
  11.1 43.1 %collective-permute-start = (bf16[34,1,128,128]{3,2,1,0:T(8,128)(2,1)}, bf16[34,1,128,128]{3,2,1,0:T(8,128)(2,1)S(1)}, u32[]{:S(2)}, u32[]{:S(2)}) collective-permute-start(bf16[34,1,128,128]{3,2,1,0:T(8,128)(2,1)} %get-tuple-element.14), channel_id=1, source_target_pairs={{0,1},{1,2},{2,3},{3,4},{4,5},{5,6},{6,7},{7,8},{8,9},{9,10},{10,1... | collective-permute-start | bytes 3342344 | tf_op jit(solution)/shard_map/ppermute | solution.py:165
  24.4 29.8 %copy-start.1 = (s32[8,2,8]{2,1,0:T(2,128)S(1)}, s32[8,2,8]{2,1,0:T(2,128)}, u32[]{:S(2)}) copy-start(s32[8,2,8]{2,1,0:T(2,128)} %get-tuple-element.9.refs_0_) | copy-start | bytes 1540
  24.4 29.8 %copy-start.2 = (s32[256]{0:T(256)S(1)}, s32[256]{0:T(256)}, u32[]{:S(2)}) copy-start(s32[256]{0:T(256)} %refs_1_.3) | copy-start | bytes 3076
  24.4 29.8 %copy-start.3 = (s32[16]{0:T(128)S(1)}, s32[16]{0:T(128)}, u32[]{:S(2)}) copy-start(s32[16]{0:T(128)} %refs_2_.3) | copy-start | bytes 196
  24.5 29.8 %copy-start.4 = (s32[2]{0:T(128)S(1)}, s32[2]{0:T(128)}, u32[]{:S(2)}) copy-start(s32[2]{0:T(128)} %pad_add_fusion.1.refs_3_) | copy-start | bytes 28
  54.3 1.2 %copy-start = (bf16[2048,256]{1,0:T(8,128)(2,1)S(1)}, bf16[2048,256]{1,0:T(8,128)(2,1)}, u32[]{:S(2)}) copy-start(bf16[2048,256]{1,0:T(8,128)(2,1)} %get-tuple-element.11.refs_6_.refs_11_) | copy-start | bytes 3145732

commit v10 on v8

--- a/solution.py
+++ b/solution.py
@@ -157,11 +157,32 @@
     )(rows, idx)
 
 
+def edge_kernel(width, src_ref, head_ref, tail_ref, sem):
+    last = src_ref.shape[1] - width
+    copies = [pltpu.make_async_copy(src_ref.at[:, pl.ds(0, width)], head_ref, sem.at[0]),
+              pltpu.make_async_copy(src_ref.at[:, pl.ds(last, width)], tail_ref, sem.at[1])]
+    for copy in copies:
+        copy.start()
+    for copy in copies:
+        copy.wait()
+
+
+def edges(cells, width):
+    shape = (cells.shape[0], width) + cells.shape[2:]
+    part = jax.ShapeDtypeStruct(shape, cells.dtype)
+    return pl.pallas_call(
+        functools.partial(edge_kernel, width),
+        out_shape=(part, part),
+        in_specs=[pl.BlockSpec(memory_space=pl.ANY)],
+        out_specs=(pl.BlockSpec(memory_space=pltpu.VMEM),) * 2,
+        scratch_shapes=[pltpu.SemaphoreType.DMA((2,))],
+    )(cells)
+
+
 def halos(cells, axis, dim, width):
     count = lax.axis_size(axis)
     ends = count - 1
-    head = lax.slice_in_dim(cells, 0, width, axis=dim)
-    tail = lax.slice_in_dim(cells, cells.shape[dim] - width, cells.shape[dim], axis=dim)
+    head, tail = edges(cells, width)
     lo = lax.ppermute(tail, axis, [(i, i + 1) for i in range(ends)])
     hi = lax.ppermute(head, axis, [(i + 1, i) for i in range(ends)])
     return lo, hi

time: 67.3 us -> 66.9 us (level)
  local copies, waits for them, and re-layouts: 4.73 us -> 1.49 us
  Pallas kernels: 51.1 us -> 54.1 us
    slice x1 -> x0, local copies, waits for them, and re-layouts: 3.24 us -> none  [halos(): head = lax.slice_in_dim(cells, 0, width, axis=dim)]
    pallas_call x0 -> x1, Pallas kernels: none -> 2.99 us  [edges(): pl.pallas_call(functools.partial(edge_kernel, width), out_shape=(part, pa...]
  transfers between devices with their start and end apart: 2 -> 2, of which waited for: 0 -> 0; matrix products, arithmetic and copies ran while one was open for 4% -> 4% of each run, Pallas kernels for 57% -> 58%
where the time goes in v10:
time: 66.9 us; the launch traced here: 66.7 us
  Pallas kernels  54.1 us (81%)
  starting transfers between devices  9.67 us (14%)
  local copies, waits for them, and re-layouts  1.49 us (2%)
  other arithmetic  1.27 us (2%)
    pallas_call x2, Pallas kernels, block_call(): pl.pallas_call(functools.partial(kernel, npl, nt, base, stride, blocks, t...  42.3 us
    pallas_call x1, Pallas kernels, gather_terms(): pl.pallas_call(functools.partial(gather_kernel, nm), out_shape=(jax.Shape...  8.74 us
    ppermute x1, starting transfers between devices, halos(): hi = lax.ppermute(head, axis, [(i + 1, i) for i in range(ends)])  6.12 us
    ppermute x1, starting transfers between devices, halos(): lo = lax.ppermute(tail, axis, [(i, i + 1) for i in range(ends)])  3.55 us
    pallas_call x1, Pallas kernels, edges(): pl.pallas_call(functools.partial(edge_kernel, width), out_shape=(part, pa...  2.99 us
  transfers between devices with their start and end apart: 2, of which 0 were waited for; matrix products, arithmetic and copies ran while one was open for 4% of the time, Pallas kernels for 58%

profile of v10, /device:TPU:7, one launch (start us, length us, event | category | flops | bytes accessed | tf_op | source)
XLA Modules:
  0.0 66.7 jit_solution(7948736230243332226)
XLA Ops:
  0.0 0.0 copy-start.5
  0.0 3.0 %shard_map.83 = (bf16[34,1,128,128]{3,2,1,0:T(8,128)(2,1)}, bf16[34,1,128,128]{3,2,1,0:T(8,128)(2,1)}) custom-call(bf16[34,8,128,128]{3,2,1,0:T(8,128)(2,1)} %refs_8_.3), custom_call_target="tpu_custom_call" | custom-call | tf_op jit(solution)/shard_map/pallas_call | solution.py:173
  3.0 0.0 copy-start.6
  3.0 0.0 copy-start.7
  3.0 3.5 %collective-permute-start = (bf16[34,1,128,128]{3,2,1,0:T(8,128)(2,1)}, bf16[34,1,128,128]{3,2,1,0:T(8,128)(2,1)S(1)}, u32[]{:S(2)}, u32[]{:S(2)}) collective-permute-start(bf16[34,1,128,128]{3,2,1,0:T(8,128)(2,1)} %get-tuple-element.11), channel_id=1, source_target_pairs={{0,1},{1,2},{2,3},{3,4},{4,5},{5,6},{6,7},{7,8},{8,9},{9,10},{10,1... | collective-permute-start | bytes 3342344 | tf_op jit(solution)/shard_map/ppermute | solution.py:186
  6.6 6.1 %collective-permute-start.1 = (bf16[34,1,128,128]{3,2,1,0:T(8,128)(2,1)}, bf16[34,1,128,128]{3,2,1,0:T(8,128)(2,1)S(1)}, u32[]{:S(2)}, u32[]{:S(2)}) collective-permute-start(bf16[34,1,128,128]{3,2,1,0:T(8,128)(2,1)} %get-tuple-element.12), channel_id=1, source_target_pairs={{1,0},{2,1},{3,2},{4,3},{5,4},{6,5},{7,6},{8,7},{9,8},{10,9},{11,1... | collective-permute-start | bytes 3342344 | tf_op jit(solution)/shard_map/ppermute | solution.py:187
  12.7 0.0 copy-done.5
  12.8 0.3 broadcast_in_dim.3
  13.1 1.1 %reshape.14.x_ref = bf16[8,16,256]{2,1,0:T(8,128)(2,1)} reshape(bf16[8,16,16,16]{3,2,1,0:T(8,128)(2,1)S(1)} %broadcast_in_dim.3) | data formatting | bytes 131072 | tf_op jit(solution)/shard_map/reshape | solution.py:202
  14.2 0.0 copy-done.6
  14.2 0.0 copy-done.7
  14.2 0.6 pad_add_fusion.idx_ref
  14.8 8.7 %shard_map.82 = (bf16[8,16,256]{2,1,0:T(8,128)(2,1)}, s32[8,2,8]{2,1,0:T(2,128)}) custom-call(bf16[8,16,256]{2,1,0:T(8,128)(2,1)} %reshape.14.x_ref, s32[2,8]{1,0:T(2,128)} %pad_add_fusion.idx_ref), custom_call_target="tpu_custom_call" | custom-call | tf_op jit(solution)/shard_map/pallas_call | solution.py:149
  23.6 0.7 %pad_add_fusion.1.refs_3_ = s32[2]{0:T(128)} fusion(s32[1]{0:T(128)} %bitcast.6, s32[1]{0:T(128)} %bitcast.5), kind=kLoop, calls=%fused_computation.1 | loop fusion | flops 2 | bytes 16 | tf_op jit(solution)/shard_map/stack | solution.py:207
  24.2 0.0 copy-start
  24.2 0.0 copy-start.1
  24.2 0.0 copy-start.2
  24.2 0.0 copy-start.3
  24.2 0.0 copy-start.4
  24.3 29.7 %shard_map.84.refs_11_ = bf16[8,2,128,128]{3,2,1,0:T(8,128)(2,1)} custom-call(s32[8,2,8]{2,1,0:T(2,128)} %get-tuple-element.9.refs_0_, s32[256]{0:T(256)} %refs_1_.3, s32[16]{0:T(128)} %refs_2_.3, s32[2]{0:T(128)} %pad_add_fusion.1.refs_3_, bf16[8,16,128,128]{3,2,1,0:T(8,128)(2,1)} %refs_4_.3, bf16[34,8,128,128]{3,2,1,0:T(8,128)(2,1)} %refs_5_.3, ...), custom_call_target="tpu_custom_call" | custom-call | flops 7247757312 | bytes 29884416 | tf_op jit(solution)/shard_map/pallas_call | solution.py:263
  53.9 0.0 collective-permute-done.refs_9_
  53.9 0.0 collective-permute-done.1.refs_10_
  53.9 0.0 copy-done
  53.9 0.0 copy-done.1
  54.0 0.0 copy-done.2
  54.0 0.0 copy-done.3
  54.0 0.0 copy-done.4
  54.0 12.7 %shard_map.85 = bf16[8,2,128,128]{3,2,1,0:T(8,128)(2,1)} custom-call(s32[8,2,8]{2,1,0:T(2,128)S(1)} %copy-done.1, s32[256]{0:T(256)S(1)} %copy-done.2, s32[16]{0:T(128)S(1)} %copy-done.3, s32[2]{0:T(128)S(1)} %copy-done.4, bf16[8,16,128,128]{3,2,1,0:T(8,128)(2,1)} %refs_4_.3, bf16[34,8,128,128]{3,2,1,0:T(8,128)(2,1)} %refs_5_.3, ...), custom_call_target="tpu_custom_call", output_to_operand_aliasing={{}: (11, {})} | custom-call | flops 2415919104 | bytes 9961472 | tf_op jit(solution)/shard_map/pallas_call | solution.py:263
  (3 shorter events, 0.0 us)
Async XLA Ops:
  0.0 12.7 %copy-start.5 = (bf16[8,16,16]{2,1,0:T(8,128)(2,1)S(1)}, bf16[8,16,16]{2,1,0:T(8,128)(2,1)}, u32[]{:S(2)}) copy-start(bf16[8,16,16]{2,1,0:T(8,128)(2,1)} %param.11) | copy-start | bytes 12292
  3.0 11.2 %copy-start.6 = (s32[8]{0:T(128)S(1)}, s32[8]{0:T(128)}, u32[]{:S(2)}) copy-start(s32[8]{0:T(128)} %param.13) | copy-start | bytes 100
  3.0 11.2 %copy-start.7 = (s32[8]{0:T(128)S(1)}, s32[8]{0:T(128)}, u32[]{:S(2)}) copy-start(s32[8]{0:T(128)} %param.12) | copy-start | bytes 100
  3.0 50.9 %collective-permute-start = (bf16[34,1,128,128]{3,2,1,0:T(8,128)(2,1)}, bf16[34,1,128,128]{3,2,1,0:T(8,128)(2,1)S(1)}, u32[]{:S(2)}, u32[]{:S(2)}) collective-permute-start(bf16[34,1,128,128]{3,2,1,0:T(8,128)(2,1)} %get-tuple-element.11), channel_id=1, source_target_pairs={{0,1},{1,2},{2,3},{3,4},{4,5},{5,6},{6,7},{7,8},{8,9},{9,10},{10,1... | collective-permute-start | bytes 3342344 | tf_op jit(solution)/shard_map/ppermute | solution.py:186
  6.6 47.4 %collective-permute-start.1 = (bf16[34,1,128,128]{3,2,1,0:T(8,128)(2,1)}, bf16[34,1,128,128]{3,2,1,0:T(8,128)(2,1)S(1)}, u32[]{:S(2)}, u32[]{:S(2)}) collective-permute-start(bf16[34,1,128,128]{3,2,1,0:T(8,128)(2,1)} %get-tuple-element.12), channel_id=1, source_target_pairs={{1,0},{2,1},{3,2},{4,3},{5,4},{6,5},{7,6},{8,7},{9,8},{10,9},{11,1... | collective-permute-start | bytes 3342344 | tf_op jit(solution)/shard_map/ppermute | solution.py:187
  24.2 29.7 %copy-start = (bf16[8,16,256]{2,1,0:T(8,128)(2,1)S(1)}, bf16[8,16,256]{2,1,0:T(8,128)(2,1)}, u32[]{:S(2)}) copy-start(bf16[8,16,256]{2,1,0:T(8,128)(2,1)} %get-tuple-element.10) | copy-start | bytes 196612
  24.2 29.7 %copy-start.1 = (s32[8,2,8]{2,1,0:T(2,128)S(1)}, s32[8,2,8]{2,1,0:T(2,128)}, u32[]{:S(2)}) copy-start(s32[8,2,8]{2,1,0:T(2,128)} %get-tuple-element.9.refs_0_) | copy-start | bytes 1540
  24.2 29.7 %copy-start.2 = (s32[256]{0:T(256)S(1)}, s32[256]{0:T(256)}, u32[]{:S(2)}) copy-start(s32[256]{0:T(256)} %refs_1_.3) | copy-start | bytes 3076
  24.2 29.7 %copy-start.3 = (s32[16]{0:T(128)S(1)}, s32[16]{0:T(128)}, u32[]{:S(2)}) copy-start(s32[16]{0:T(128)} %refs_2_.3) | copy-start | bytes 196
  24.2 29.7 %copy-start.4 = (s32[2]{0:T(128)S(1)}, s32[2]{0:T(128)}, u32[]{:S(2)}) copy-start(s32[2]{0:T(128)} %pad_add_fusion.1.refs_3_) | copy-start | bytes 28

commit v11 on v10

--- a/solution.py
+++ b/solution.py
@@ -30,14 +30,14 @@
     out_ref, c_scr, x_scr, y_scr, kron_scr = refs
     first_step = pl.program_id(0) == 0
     i = base + pl.program_id(0) * stride
-    gi = ids_ref[0] + i
+    gi = ids_ref[0, 0] + i
 
     def size_at(shift):
         j = gi + shift
         inside = (j >= 0) & (j < total)
         return jnp.where(inside, bs_ref[jnp.clip(j, 0, total - 1)], 0)
 
-    sloc = [sh_ref[ids_ref[1] + p] for p in range(npl)]
+    sloc = [sh_ref[ids_ref[0, 1] + p] for p in range(npl)]
     depth = ts_ref.shape[-1]
     nq = ts_ref.shape[1]
     rows = lax.broadcasted_iota(jnp.int32, (depth, depth), 0)
@@ -157,7 +157,10 @@
     )(rows, idx)
 
 
-def edge_kernel(width, src_ref, head_ref, tail_ref, sem):
+def edge_kernel(width, npl, src_ref, head_ref, tail_ref, ids_ref, sem):
+    lane = lax.broadcasted_iota(jnp.int32, ids_ref.shape, 1)
+    first = lax.axis_index("blk") * src_ref.shape[1]
+    ids_ref[...] = jnp.where(lane == 0, first, lax.axis_index("mpo") * npl).astype(jnp.int32)
     last = src_ref.shape[1] - width
     copies = [pltpu.make_async_copy(src_ref.at[:, pl.ds(0, width)], head_ref, sem.at[0]),
               pltpu.make_async_copy(src_ref.at[:, pl.ds(last, width)], tail_ref, sem.at[1])]
@@ -167,25 +170,25 @@
         copy.wait()
 
 
-def edges(cells, width):
+def edges(cells, width, npl):
     shape = (cells.shape[0], width) + cells.shape[2:]
     part = jax.ShapeDtypeStruct(shape, cells.dtype)
     return pl.pallas_call(
-        functools.partial(edge_kernel, width),
-        out_shape=(part, part),
+        functools.partial(edge_kernel, width, npl),
+        out_shape=(part, part, jax.ShapeDtypeStruct((1, 128), jnp.int32)),
         in_specs=[pl.BlockSpec(memory_space=pl.ANY)],
-        out_specs=(pl.BlockSpec(memory_space=pltpu.VMEM),) * 2,
+        out_specs=(pl.BlockSpec(memory_space=pltpu.VMEM),) * 3,
         scratch_shapes=[pltpu.SemaphoreType.DMA((2,))],
     )(cells)
 
 
-def halos(cells, axis, dim, width):
+def halos(cells, axis, dim, width, npl):
     count = lax.axis_size(axis)
     ends = count - 1
-    head, tail = edges(cells, width)
+    head, tail, ids = edges(cells, width, npl)
     lo = lax.ppermute(tail, axis, [(i, i + 1) for i in range(ends)])
     hi = lax.ppermute(head, axis, [(i + 1, i) for i in range(ends)])
-    return lo, hi
+    return lo, hi, ids
 
 
 def body(two_site, left_env, right_env, mpo_terms, term_left, term_right, shifts, block_sizes):
@@ -204,9 +207,8 @@
     mq, idx = gather_terms(rows, idx)
     nt = nmpo * local_terms
     mq = mq.reshape(nt * npl, nq * YT)
-    ids = jnp.stack([first, p_first]).astype(jnp.int32)
-
-    lo, hi = halos(right_env, "blk", 1, SH)
+
+    lo, hi, ids = halos(right_env, "blk", 1, SH, npl)
 
     scalars = (idx, block_sizes, shifts, ids)
     inner = block_call(*scalars, two_site, left_env, mq, right_env, None, None, None, npl=npl)
@@ -228,7 +230,7 @@
 
     def rloc_map(p):
         def index(b, idx_r, bs_r, sh_r, ids_r):
-            return (0, jnp.clip(base + b * stride + sh_r[ids_r[1] + p], 0, blocks - 1), 0, 0)
+            return (0, jnp.clip(base + b * stride + sh_r[ids_r[0, 1] + p], 0, blocks - 1), 0, 0)
         return index
 
     const4 = lambda b, *refs: (0, 0, 0, 0)

time: 66.9 us -> 66.3 us (level)
  other arithmetic: 1.27 us -> 0.6 us
  transfers between devices with their start and end apart: 2 -> 2, of which waited for: 0 -> 0; matrix products, arithmetic and copies ran while one was open for 4% -> 3% of each run, Pallas kernels for 58% -> 58%
where the time goes in v11:
time: 66.3 us; the launch traced here: 66.1 us
  Pallas kernels  54.2 us (82%)
  starting transfers between devices  9.67 us (15%)
  local copies, waits for them, and re-layouts  1.5 us (2%)
    pallas_call x2, Pallas kernels, block_call(): pl.pallas_call(functools.partial(kernel, npl, nt, base, stride, blocks, t...  42.5 us
    pallas_call x1, Pallas kernels, gather_terms(): pl.pallas_call(functools.partial(gather_kernel, nm), out_shape=(jax.Shape...  8.74 us
    ppermute x1, starting transfers between devices, halos(): hi = lax.ppermute(head, axis, [(i + 1, i) for i in range(ends)])  6.12 us
    ppermute x1, starting transfers between devices, halos(): lo = lax.ppermute(tail, axis, [(i, i + 1) for i in range(ends)])  3.55 us
    pallas_call x1, Pallas kernels, edges(): pl.pallas_call(functools.partial(edge_kernel, width, npl), out_shape=(par...  2.98 us
  transfers between devices with their start and end apart: 2, of which 0 were waited for; matrix products, arithmetic and copies ran while one was open for 3% of the time, Pallas kernels for 58%

profile of v11, /device:TPU:7, one launch (start us, length us, event | category | flops | bytes accessed | tf_op | source)
XLA Modules:
  0.0 66.1 jit_solution(11396240992878569100)
XLA Ops:
  0.0 0.0 copy-start.5
  0.0 3.0 %shard_map.83 = (bf16[34,1,128,128]{3,2,1,0:T(8,128)(2,1)}, bf16[34,1,128,128]{3,2,1,0:T(8,128)(2,1)}, s32[1,128]{1,0:T(1,128)}) custom-call(bf16[34,8,128,128]{3,2,1,0:T(8,128)(2,1)} %refs_8_.3), custom_call_target="tpu_custom_call" | custom-call | tf_op jit(solution)/shard_map/pallas_call | solution.py:176
  3.0 0.0 copy-start.6
  3.0 0.0 copy-start.7
  3.0 3.5 %collective-permute-start = (bf16[34,1,128,128]{3,2,1,0:T(8,128)(2,1)}, bf16[34,1,128,128]{3,2,1,0:T(8,128)(2,1)S(1)}, u32[]{:S(2)}, u32[]{:S(2)}) collective-permute-start(bf16[34,1,128,128]{3,2,1,0:T(8,128)(2,1)} %get-tuple-element.13), channel_id=1, source_target_pairs={{0,1},{1,2},{2,3},{3,4},{4,5},{5,6},{6,7},{7,8},{8,9},{9,10},{10,1... | collective-permute-start | bytes 3342344 | tf_op jit(solution)/shard_map/ppermute | solution.py:189
  6.6 6.1 %collective-permute-start.1 = (bf16[34,1,128,128]{3,2,1,0:T(8,128)(2,1)}, bf16[34,1,128,128]{3,2,1,0:T(8,128)(2,1)S(1)}, u32[]{:S(2)}, u32[]{:S(2)}) collective-permute-start(bf16[34,1,128,128]{3,2,1,0:T(8,128)(2,1)} %get-tuple-element.14), channel_id=1, source_target_pairs={{1,0},{2,1},{3,2},{4,3},{5,4},{6,5},{7,6},{8,7},{9,8},{10,9},{11,1... | collective-permute-start | bytes 3342344 | tf_op jit(solution)/shard_map/ppermute | solution.py:190
  12.7 0.0 copy-done.5
  12.8 0.3 broadcast_in_dim.3
  13.1 1.1 %reshape.14.x_ref = bf16[8,16,256]{2,1,0:T(8,128)(2,1)} reshape(bf16[8,16,16,16]{3,2,1,0:T(8,128)(2,1)S(1)} %broadcast_in_dim.3) | data formatting | bytes 131072 | tf_op jit(solution)/shard_map/reshape | solution.py:205
  14.2 0.0 copy-done.6
  14.2 0.0 copy-done.7
  14.2 0.6 pad_add_fusion.idx_ref
  14.8 8.7 %shard_map.82 = (bf16[8,16,256]{2,1,0:T(8,128)(2,1)}, s32[8,2,8]{2,1,0:T(2,128)}) custom-call(bf16[8,16,256]{2,1,0:T(8,128)(2,1)} %reshape.14.x_ref, s32[2,8]{1,0:T(2,128)} %pad_add_fusion.idx_ref), custom_call_target="tpu_custom_call" | custom-call | tf_op jit(solution)/shard_map/pallas_call | solution.py:149
  23.6 0.0 copy-start
  23.6 0.0 copy-start.1
  23.6 0.0 copy-start.2
  23.6 0.0 copy-start.3
  23.6 0.0 copy-start.4
  23.6 29.8 %shard_map.84.refs_11_ = bf16[8,2,128,128]{3,2,1,0:T(8,128)(2,1)} custom-call(s32[8,2,8]{2,1,0:T(2,128)} %get-tuple-element.10.refs_0_, s32[256]{0:T(256)} %refs_1_.3, s32[16]{0:T(128)} %refs_2_.3, s32[1,128]{1,0:T(1,128)} %get-tuple-element.11.refs_3_, bf16[8,16,128,128]{3,2,1,0:T(8,128)(2,1)} %refs_4_.3, bf16[34,8,128,128]{3,2,1,0:T(8,128)(2,1)} %refs_5_.3, ...), custom_call_target="tpu_custom_call" | custom-call | flops 7247757312 | bytes 29884416 | tf_op jit(solution)/shard_map/pallas_call | solution.py:265
  53.4 0.0 collective-permute-done.refs_9_
  53.4 0.0 collective-permute-done.1.refs_10_
  53.4 0.0 copy-done
  53.4 0.0 copy-done.1
  53.4 0.0 copy-done.2
  53.4 0.0 copy-done.3
  53.4 0.0 copy-done.4
  53.4 12.7 %shard_map.85 = bf16[8,2,128,128]{3,2,1,0:T(8,128)(2,1)} custom-call(s32[8,2,8]{2,1,0:T(2,128)S(1)} %copy-done.1, s32[256]{0:T(256)S(1)} %copy-done.2, s32[16]{0:T(128)S(1)} %copy-done.3, s32[1,128]{1,0:T(1,128)S(1)} %copy-done.4, bf16[8,16,128,128]{3,2,1,0:T(8,128)(2,1)} %refs_4_.3, ...), custom_call_target="tpu_custom_call", output_to_operand_aliasing={{}: (11, {})} | custom-call | flops 2415919104 | bytes 9961472 | tf_op jit(solution)/shard_map/pallas_call | solution.py:265
  (3 shorter events, 0.0 us)
Async XLA Ops:
  0.0 12.7 %copy-start.5 = (bf16[8,16,16]{2,1,0:T(8,128)(2,1)S(1)}, bf16[8,16,16]{2,1,0:T(8,128)(2,1)}, u32[]{:S(2)}) copy-start(bf16[8,16,16]{2,1,0:T(8,128)(2,1)} %param.11) | copy-start | bytes 12292
  3.0 11.2 %copy-start.6 = (s32[8]{0:T(128)S(1)}, s32[8]{0:T(128)}, u32[]{:S(2)}) copy-start(s32[8]{0:T(128)} %param.13) | copy-start | bytes 100
  3.0 11.2 %copy-start.7 = (s32[8]{0:T(128)S(1)}, s32[8]{0:T(128)}, u32[]{:S(2)}) copy-start(s32[8]{0:T(128)} %param.12) | copy-start | bytes 100
  3.0 50.4 %collective-permute-start = (bf16[34,1,128,128]{3,2,1,0:T(8,128)(2,1)}, bf16[34,1,128,128]{3,2,1,0:T(8,128)(2,1)S(1)}, u32[]{:S(2)}, u32[]{:S(2)}) collective-permute-start(bf16[34,1,128,128]{3,2,1,0:T(8,128)(2,1)} %get-tuple-element.13), channel_id=1, source_target_pairs={{0,1},{1,2},{2,3},{3,4},{4,5},{5,6},{6,7},{7,8},{8,9},{9,10},{10,1... | collective-permute-start | bytes 3342344 | tf_op jit(solution)/shard_map/ppermute | solution.py:189
  6.6 46.8 %collective-permute-start.1 = (bf16[34,1,128,128]{3,2,1,0:T(8,128)(2,1)}, bf16[34,1,128,128]{3,2,1,0:T(8,128)(2,1)S(1)}, u32[]{:S(2)}, u32[]{:S(2)}) collective-permute-start(bf16[34,1,128,128]{3,2,1,0:T(8,128)(2,1)} %get-tuple-element.14), channel_id=1, source_target_pairs={{1,0},{2,1},{3,2},{4,3},{5,4},{6,5},{7,6},{8,7},{9,8},{10,9},{11,1... | collective-permute-start | bytes 3342344 | tf_op jit(solution)/shard_map/ppermute | solution.py:190
  23.6 29.8 %copy-start = (bf16[8,16,256]{2,1,0:T(8,128)(2,1)S(1)}, bf16[8,16,256]{2,1,0:T(8,128)(2,1)}, u32[]{:S(2)}) copy-start(bf16[8,16,256]{2,1,0:T(8,128)(2,1)} %get-tuple-element.12) | copy-start | bytes 196612
  23.6 29.8 %copy-start.1 = (s32[8,2,8]{2,1,0:T(2,128)S(1)}, s32[8,2,8]{2,1,0:T(2,128)}, u32[]{:S(2)}) copy-start(s32[8,2,8]{2,1,0:T(2,128)} %get-tuple-element.10.refs_0_) | copy-start | bytes 1540
  23.6 29.8 %copy-start.2 = (s32[256]{0:T(256)S(1)}, s32[256]{0:T(256)}, u32[]{:S(2)}) copy-start(s32[256]{0:T(256)} %refs_1_.3) | copy-start | bytes 3076
  23.6 29.8 %copy-start.3 = (s32[16]{0:T(128)S(1)}, s32[16]{0:T(128)}, u32[]{:S(2)}) copy-start(s32[16]{0:T(128)} %refs_2_.3) | copy-start | bytes 196
  23.6 29.8 %copy-start.4 = (s32[1,128]{1,0:T(1,128)S(1)}, s32[1,128]{1,0:T(1,128)}, u32[]{:S(2)}) copy-start(s32[1,128]{1,0:T(1,128)} %get-tuple-element.11.refs_3_) | copy-start | bytes 1540
